TPU v7x, 32 devices: a whole 2x2x4 slice. The times are simulated.
32 devices in a mesh: box: 4 (over y, core), gz: 8 (over z, x).
Axes of the slice: x: 2, y: 2, z: 4, core: 2. Of those that a mesh axis runs over, the one named last changes fastest.
Arguments:
- coarse_mismatch: float32 [64, 512, 512], P('gz', 'box'), may hold values from -4 to 4, as said below
- fine_div: float32 [64, 128, 256], P('box', 'gz'), may hold values from -12 to 12
- reflux: float32 [64, 128, 128], P('box', 'gz'), may hold values from -12 to 12
- box_list: int32 [64, 3], replicated, may hold values from 0 to 500, as said below
- cf_mask: int32 [64, 4], replicated, may hold values 0 or 1
Outputs:
- sync_phi: float32 [64, 512, 512], P('gz', 'box')
Inputs may be any that keep to these rules, and one draw needn't show every extreme that they name: `coarse_mismatch`: the base level's divergence mismatch. `box_list`: column 0 is the owning box group; columns 1 and 2 are 4 more than multiples of 16, with column 1 below 128 and column 2 below 512; patches of one owner never share a position. The 16 patches of one box group (rows of one aligned block) have at most 4 with one owner, and some owner has exactly 4 in every block.
All inputs are finite; a program needn't handle non-finite values.
Results may differ from a plain program's by a relative error of at most 0.0003.
Values sent between devices are 32-bit elements; how exact they have to be, the bound alone decides.
No kernel may reach another device: no remote copies, remote signals or barrier semaphores. Data moves between devices by JAX's collectives and lax.ppermute only.
A program may use at most 320 MiB of HBM per device.

v0:
```python
import functools

import jax
import jax.numpy as jnp
from jax import lax
from jax.experimental import pallas as pl
from jax.experimental.pallas import tpu as pltpu
from jax.sharding import PartitionSpec as P


CSWEEPS = 16
OMEGA = 0.8
C = OMEGA / 6.0
HX = 32
HU = 8
LANES = 128
F32 = jnp.float32
BF16 = jnp.bfloat16
I32 = jnp.int32

VM = pl.BlockSpec(memory_space=pltpu.VMEM)
SM = pl.BlockSpec(memory_space=pltpu.SMEM)
ANY = pl.BlockSpec(memory_space=pl.ANY)
PARAMS = pltpu.CompilerParams(vmem_limit_bytes=56 << 20)


def iota(shape, dim):
    return lax.broadcasted_iota(I32, shape, dim)


def as_matrix(condition):
    return condition.astype(F32).astype(BF16)


def pair_matrix(length):
    shape = (length, length // 2)
    return as_matrix((iota(shape, 0) >> 1) == iota(shape, 1))


def copy_matrix(length):
    shape = (length, 2 * length)
    return as_matrix(iota(shape, 0) == (iota(shape, 1) >> 1))


def select_dot(values, matrix):
    high = values.astype(BF16)
    low = (values - high.astype(F32)).astype(BF16)
    return jnp.dot(high, matrix, preferred_element_type=F32) + jnp.dot(
        low, matrix, preferred_element_type=F32
    )


def each(count, body, unroll=1):
    def step(index, carry):
        body(index)
        return carry

    lax.fori_loop(0, count, step, 0, unroll=unroll)


def beside_lanes(blocks):
    lane = iota(blocks[0].shape, 1)
    right = [pltpu.roll(block, 1, 1) for block in blocks]
    left = [pltpu.roll(block, LANES - 1, 1) for block in blocks]
    sums = []
    for b in range(len(blocks)):
        before = right[b - 1] if b > 0 else 0.0
        after = left[b + 1] if b + 1 < len(blocks) else 0.0
        sums.append(
            jnp.where(lane == 0, before, right[b]) + jnp.where(lane == LANES - 1, after, left[b])
        )
    return sums


def around(field, plane, row, rows):
    count = field.shape[1]

    def at(p, first):
        return [field[p, b, first : first + rows, :] for b in range(count)]

    middle = at(plane, row + 8)
    parts = zip(
        at(plane, row + 7), at(plane, row + 9), beside_lanes(middle), at(plane - 1, row + 8), at(plane + 1, row + 8)
    )
    return middle, [(a + b) + (c + (d + e)) for a, b, c, d, e in parts]


class Edges:
    def __init__(self, boxes, slabs):
        self.box, self.slab = lax.axis_index("box"), lax.axis_index("gz")
        self.boxes, self.slabs = boxes, slabs

    def planes(self, plane, count):
        outside = ((plane < 0) & (self.slab == 0)) | ((plane >= count) & (self.slab == self.slabs - 1))
        return jnp.where(outside, 0.0, 1.0).astype(F32)

    def low(self):
        return jnp.where(self.box == 0, 0.0, 1.0).astype(F32)

    def high(self):
        return jnp.where(self.box == self.boxes - 1, 0.0, 1.0).astype(F32)


def chunks_of(rows, halo, chunk, cut=0):
    out = [] if cut else [(0, halo, -1)]
    inner = (halo, rows - halo)
    for first in range(inner[0], inner[1], chunk):
        out.append((first, min(chunk, inner[1] - first), 0))
    return out if cut else out + [(rows - halo, halo, 1)]


def scale_of(side, edges, plane_scale):
    if side == 0:
        return plane_scale
    row_scale = edges.low() if side < 0 else edges.high()
    return row_scale if plane_scale is None else row_scale * plane_scale


def relax(new, noff, planes, source, soff, rows, halo, edges, count, old=None, ooff=0, extra=None, chunk=16, shift=8, cut=0):
    def body(index):
        plane_scale = None if count is None else edges.planes(index + planes[0], count)
        for first, size, side in chunks_of(rows, halo, chunk, cut):
            scale = scale_of(side, edges, plane_scale)
            if old is None:
                middle, near = around(source, index + (planes[0] + soff), first, size)
                values = [(1.2 * C) * m + (C * C) * n for m, n in zip(middle, near)]
                if extra is not None:
                    values = [v + extra(index, b, first, size) for b, v in enumerate(values)]
            else:
                middle, near = around(old, index + (planes[0] + ooff), first, size)
                at = index + (planes[0] + soff)
                values = [
                    (1.0 - OMEGA) * m + C * (source[at, b, first + 8 : first + 8 + size, :] + n)
                    for b, (m, n) in enumerate(zip(middle, near))
                ]
            for b, value in enumerate(values):
                if scale is not None:
                    value = value * scale
                new[index + (planes[0] + noff), b, first + shift : first + shift + size, :] = value

    each(planes[1] - planes[0], body)


def restrict(source, soff, v, voff, pairs, rows, store, chunk=16):
    count = v.shape[1]
    width = min(2, count)
    half = rows // 2

    def body(index):
        low_v, low_s = 2 * index + (2 * pairs[0] + voff), 2 * index + (2 * pairs[0] + soff)
        matrix = pair_matrix(width * LANES)
        for first in range(0, half, chunk):
            size = min(chunk, half - first)

            def at(field, plane, b, offset):
                return field[plane, b, pl.ds(8 + 2 * first + offset, size, stride=2), :]

            whole = [
                (at(v, low_v, b, 0) + at(v, low_v, b, 1)) + (at(v, low_v + 1, b, 0) + at(v, low_v + 1, b, 1))
                for b in range(count)
            ]
            near = beside_lanes(whole)
            sums = []
            for b in range(count):
                total = near[b] - 4.0 * whole[b]
                total = total + (at(source, low_s, b, 0) + at(source, low_s, b, 1))
                total = total + (at(source, low_s + 1, b, 0) + at(source, low_s + 1, b, 1))
                total = total + (at(v, low_v - 1, b, 0) + at(v, low_v - 1, b, 1))
                total = total + (at(v, low_v + 2, b, 0) + at(v, low_v + 2, b, 1))
                total = total + (at(v, low_v, b, -1) + at(v, low_v + 1, b, -1))
                total = total + (at(v, low_v, b, 2) + at(v, low_v + 1, b, 2))
                sums.append(total)
            for group in range(count // width):
                piece = sums[width * group]
                if width == 2:
                    piece = jnp.concatenate([piece, sums[2 * group + 1]], axis=1)
                store(index, group, first, size, 0.5 * select_dot(piece, matrix))

    each(pairs[1] - pairs[0], body)


def zero(ref, planes):
    for plane in planes:
        ref[plane] = jnp.zeros(ref.shape[1:], F32)


def zero_rims(ref, planes=None):
    rows = ref.shape[2]
    for plane in range(ref.shape[0]) if planes is None else planes:
        for b in range(ref.shape[1]):
            ref[plane, b, 0:8, :] = jnp.zeros((8, LANES), F32)
            ref[plane, b, rows - 8 : rows, :] = jnp.zeros((8, LANES), F32)


def block_copies(wide, tiled, planes, first, rows, sem, back=False):
    copies = []
    for b in range(tiled.shape[1]):
        pair = (
            wide.at[:, :, pl.ds(LANES * b, LANES)],
            tiled.at[pl.ds(planes[0], planes[1]), b, pl.ds(first, rows), :],
        )
        copies.append(pltpu.make_async_copy(*(pair[::-1] if back else pair), sem))
    return copies


def pack_kernel(mask, fine, flux, out, fine_s, flux_s, sem):
    patches, fine_z = fine.shape[0], fine.shape[1]
    n0 = fine_z // 2
    blocks = fine_s.shape[0]
    copies = [
        pltpu.make_async_copy(fine.at[:, :, pl.ds(LANES * b, LANES)], fine_s.at[b], sem.at[b])
        for b in range(blocks)
    ]
    copies.append(pltpu.make_async_copy(flux, flux_s, sem.at[blocks]))
    for copy in copies:
        copy.start()
    base = lax.axis_index("box") * patches
    side = (iota((n0, LANES), 1) >> 4) & 3
    source, target = iota((LANES, LANES), 0), iota((LANES, LANES), 1)
    s, i = (source >> 4) & 3, (source & 15) >> 1
    goal = jnp.where(
        s == 0, i + 91, jnp.where(s == 1, i + 1, jnp.where(s == 2, 80 - 10 * i, 89 - 10 * i))
    )
    matrices = [as_matrix(goal == target)]
    for b in range(blocks):
        place = source + LANES * b
        goal = 10 * (8 - (place >> 5)) + ((place & 15) >> 1) + 1
        matrices.append(as_matrix(goal == target))
    for copy in copies:
        copy.wait()
    masked, fine_rows = [], [[] for _ in range(blocks)]
    for patch in range(patches):
        m = [mask[s, base + patch].astype(F32) for s in range(4)]
        factor = jnp.where(side == 0, m[0], jnp.where(side == 1, m[1], jnp.where(side == 2, m[2], m[3])))
        masked.append(
            (flux_s[patch, pl.ds(0, n0, stride=2), :] + flux_s[patch, pl.ds(1, n0, stride=2), :]) * factor
        )
        for b in range(blocks):
            fine_rows[b].append(
                fine_s[b, patch, pl.ds(0, n0, stride=2), :] + fine_s[b, patch, pl.ds(1, n0, stride=2), :]
            )
    total = select_dot(jnp.concatenate(masked, axis=0), matrices[0])
    for b in range(blocks):
        total = total + select_dot(jnp.concatenate(fine_rows[b], axis=0), matrices[b + 1])
    out[...] = 0.125 * total


class Tiles:
    def __init__(self):
        self.lane = iota((16, LANES), 1)
        row = iota((16, LANES), 0)
        self.ring_row = (row >= 3) & (row < 13)
        self.core_row = (row >= 4) & (row < 12)

    def put(self, field, row, column, pairs):
        row = pl.multiple_of(row, 8)
        block, offset = column >> 7, column & (LANES - 1)
        across = self.lane - offset
        ring = self.ring_row & (across >= 3) & (across < 13)
        core = self.core_row & (across >= 4) & (across < 12)
        for plane, line in pairs:
            values = jnp.broadcast_to(line, (8, LANES))
            values = pltpu.roll(values, 0, 1, stride=10, stride_axis=0)
            tile = jnp.concatenate(
                [
                    pltpu.roll(values, (offset + 11) & (LANES - 1), 1),
                    pltpu.roll(values, (offset + 91) & (LANES - 1), 1),
                ],
                axis=0,
            )
            now = field[plane, block, pl.ds(row, 16), :]
            field[plane, block, pl.ds(row, 16), :] = jnp.where(core, 0.0, now) + jnp.where(ring, tile, 0.0)


def each_owned(box_list, box, body):
    def step(patch, slot):
        mine = box_list[0, patch] == box

        @pl.when(mine)
        def _():
            body(patch, slot)

        return slot + jnp.where(mine, 1, 0)

    lax.fori_loop(0, box_list.shape[1], step, jnp.zeros((), I32))


def down_kernel(
    boxes, slabs, n0, x0,
    box_list, coarse, x_low, x_high, packed,
    f_own, rim_top, rim_bot, c1, c2, up, down,
    fb, vb, g1, v1, sem, out_sem,
):
    edges = Edges(boxes, slabs)
    rows0, rows1, rows2 = x0 + 2 * HX, x0 // 2 + HX, x0 // 4 + HX // 2
    n1, n2 = n0 // 2, n0 // 4
    copies = (
        block_copies(x_low, fb, (2, n0), 8, HX, sem.at[0])
        + block_copies(coarse, fb, (2, n0), 8 + HX, x0, sem.at[1])
        + block_copies(x_high, fb, (2, n0), 8 + HX + x0, HX, sem.at[2])
    )
    for copy in copies:
        copy.start()
    zero(fb, (0, 1, n0 + 2, n0 + 3))
    zero_rims(fb, range(2, n0 + 2))
    zero(vb, (0, 1, n0 + 4, n0 + 5))
    zero_rims(vb, range(2, n0 + 4))
    zero(g1, (0, 1, 2, n1 + 5, n1 + 6, n1 + 7))
    zero_rims(g1, range(3, n1 + 5))
    zero(v1, (0, 1, 2, n1 + 7, n1 + 8, n1 + 9))
    zero_rims(v1, range(3, n1 + 7))
    for copy in copies:
        copy.wait()

    tiles = Tiles()

    def place(patch):
        start = (box_list[0, patch] - edges.box) * x0 + box_list[1, patch] - 4 + HX

        @pl.when((start >= 0) & (start < rows0))
        def _():
            tiles.put(
                fb,
                start + 8,
                box_list[2, patch] - 4,
                [(2 + z, packed[pl.ds(patch * n0 + z, 1), :]) for z in range(n0)],
            )

    each(box_list.shape[1], place)

    inner = pl.ds(8 + HX - HU, x0 + 2 * HU)
    out_copy = pltpu.make_async_copy(fb.at[pl.ds(2, n0), :, inner, :], f_own, out_sem)
    out_copy.start()

    relax(vb, 3, (-1, n0 + 1), fb, 2, rows0, HX, edges, n0)

    h1 = HX // 2

    def store1(index, group, first, size, value):
        scale = edges.planes(index - 1, n1)
        if first < h1:
            scale = scale * edges.low()
        if first >= rows1 - h1:
            scale = scale * edges.high()
        g1[index + 3, group, 8 + first : 8 + first + size, :] = value * scale

    restrict(fb, 2, vb, 3, (-1, n1 + 1), rows0, store1)
    for plane in range(n1 + 2):
        for b in range(g1.shape[1]):
            c1[plane, b] = g1[plane + 3, b, 8 + h1 - HU : 8 + rows1 - h1 + HU, :]

    relax(v1, 5, (-2, n1 + 2), g1, 4, rows1, h1, edges, n1)

    h2 = HX // 4

    def store2(index, group, first, size, value):
        if first < h2:
            value = value * edges.low()
        if first >= rows2 - h2:
            value = value * edges.high()
        c2[index, group, first : first + size, :] = value

    restrict(g1, 4, v1, 5, (-2, n2 + 2), rows1, store2, chunk=8)

    r1 = c1.shape[2]
    for target, fine_plane, coarse_first in ((up, n1 + 1, n2 + 2), (down, 0, 0)):
        target[0:rows2] = c2[coarse_first, 0]
        target[rows2 : 2 * rows2] = c2[coarse_first + 1, 0]
        for b in range(c1.shape[1]):
            first = 2 * rows2 + b * r1
            target[first : first + r1] = c1[fine_plane, b]

    slots = rim_top.shape[0] - 24 * fb.shape[1]
    base = 24 * fb.shape[1]

    def keep(patch, slot):
        for z in range(3):
            rim_top[pl.ds(base + z * (slots // 3) + slot, 1), :] = packed[pl.ds(patch * n0 + n0 - 3 + z, 1), :]
            rim_bot[pl.ds(base + z * (slots // 3) + slot, 1), :] = packed[pl.ds(patch * n0 + z, 1), :]

    rim_top[base:, :] = jnp.zeros((slots, LANES), F32)
    rim_bot[base:, :] = jnp.zeros((slots, LANES), F32)
    each_owned(box_list, edges.box, keep)
    for z in range(3):
        for b in range(fb.shape[1]):
            first = 8 * (fb.shape[1] * z + b)
            for rim, plane in ((rim_top, n0 - 1 + z), (rim_bot, 2 + z)):
                rim[first : first + 3, :] = fb[plane, b, 8 + HX - 3 : 8 + HX, :]
                rim[first + 3 : first + 6, :] = fb[plane, b, 8 + HX + x0 : 8 + HX + x0 + 3, :]
                rim[first + 6 : first + 8, :] = jnp.zeros((2, LANES), F32)
    out_copy.wait()


def total_kernel(c2, below, above, copies):
    n2, rows2 = c2.shape[0] - 4, c2.shape[2]
    for plane in range(n2):
        value = c2[2 + plane, 0]
        if plane < 2:
            value = value + below[plane * rows2 : (plane + 1) * rows2]
        if plane >= n2 - 2:
            first = (plane - (n2 - 2)) * rows2
            value = value + above[first : first + rows2]
        for slab in range(copies.shape[0]):
            copies[slab, plane * rows2 : (plane + 1) * rows2] = value


def join_kernel(rows2, c1, below, above, rim_top, rim_bot, s1, up, down):
    n1, r1 = s1.shape[0], c1.shape[2]
    for plane in range(n1):
        s1[plane] = c1[1 + plane]
    for b in range(s1.shape[1]):
        first = 2 * rows2 + b * r1
        s1[0, b] = s1[0, b] + below[first : first + r1]
        s1[n1 - 1, b] = s1[n1 - 1, b] + above[first : first + r1]
    near = r1 - HU
    for p in range(4):
        for b in range(s1.shape[1]):
            first = near * (p * s1.shape[1] + b)
            up[first : first + near] = s1[n1 - 4 + p, b, HU // 2 : HU // 2 + near, :]
            down[first : first + near] = s1[p, b, HU // 2 : HU // 2 + near, :]
    first = near * 4 * s1.shape[1]
    up[first:] = rim_top[...]
    down[first:] = rim_bot[...]


def third_kernel(boxes, slabs, s2, s3, fb, vb):
    edges = Edges(boxes, slabs)
    planes, rows = s2.shape[0], s2.shape[1]
    zero(fb, (0, planes + 1))
    zero(vb, (0, planes + 1))
    zero_rims(fb, range(1, planes + 1))
    zero_rims(vb, range(1, planes + 1))
    for plane in range(planes):
        fb[plane + 1, 0, 8 : 8 + rows, :] = s2[plane]
    relax(vb, 1, (0, planes), fb, 1, rows, HX // 4, edges, None, chunk=32)
    quarter = planes // 4
    h3 = HX // 8
    own = rows // 2 - 2 * h3
    lanes = LANES // 2

    for part in range(2):

        def store(index, group, first, size, value, part=part):
            s3[index, :, lanes * part : lanes * (part + 1)] = value[h3 : h3 + own]

        restrict(
            fb, 1, vb, 1, (quarter * part, quarter * (part + 1)), rows, store, chunk=rows // 2
        )


def coarse_kernel(
    boxes, slabs,
    s3, s2, s1, below, above,
    e1,
    sc, va3, vb3, e3p, f2, v2a, v2b, e2p, f1, v1a, v1b,
):
    edges = Edges(boxes, slabs)
    slab = edges.slab
    half, rows3 = sc.shape[0], sc.shape[2] - 16
    own3 = s3.shape[2]
    zero_rims(va3)
    zero_rims(vb3)
    for box in range(boxes):
        for plane in range(half):
            value = s3[box, plane]
            sc[plane, 0, 8 + box * own3 : 8 + (box + 1) * own3, :] = value
            va3[plane, 0, 8 + box * own3 : 8 + (box + 1) * own3, :] = C * value

    def coarsest(old, new):
        chunk = 16
        lane = iota((chunk, LANES), 1)
        for row in range(0, rows3, chunk):
            inner = slice(row + 8, row + 8 + chunk)
            for plane in range(half):
                middle = old[plane, 0, inner, :]
                before = jnp.where((lane & 63) == 0, 0.0, pltpu.roll(middle, 1, 1))
                after = jnp.where((lane & 63) == 63, 0.0, pltpu.roll(middle, LANES - 1, 1))
                if plane > 0:
                    lower = old[plane - 1, 0, inner, :]
                else:
                    lower = jnp.where(lane < 64, 0.0, pltpu.roll(old[half - 1, 0, inner, :], 64, 1))
                if plane < half - 1:
                    upper = old[plane + 1, 0, inner, :]
                else:
                    upper = jnp.where(lane < 64, pltpu.roll(old[0, 0, inner, :], 64, 1), 0.0)
                beside = old[plane, 0, row + 7 : row + 7 + chunk, :] + old[plane, 0, row + 9 : row + 9 + chunk, :]
                near = beside + ((before + after) + (lower + upper))
                new[plane, 0, inner, :] = (1.0 - OMEGA) * middle + C * (sc[plane, 0, inner, :] + near)

    def double(index):
        coarsest(va3, vb3)
        coarsest(vb3, va3)

    each((CSWEEPS - 1) // 2, double)
    coarsest(va3, vb3)

    n2, rows2 = s2.shape[0] // slabs, s2.shape[1]
    n3 = n2 // 2
    shape = (LANES, LANES)
    copy_low = (iota(shape, 0) == (iota(shape, 1) >> 1)).astype(F32)
    copy_high = (iota(shape, 0) == (iota(shape, 1) >> 1) + 64).astype(F32)
    total3 = 2 * half
    h3 = HX // 8
    window = pl.multiple_of(edges.box * own3, 8)
    for k in range(-2, n3 + 2):
        plane = slab * n3 + k
        inside = (plane >= 0) & (plane < total3)
        safe = jnp.clip(plane, 0, total3 - 1)
        upper = safe >= half
        matrix = jnp.where(upper, copy_high, copy_low) * jnp.where(inside, 1.0, 0.0)
        value = vb3[jnp.where(upper, safe - half, safe), 0, pl.ds(window, own3 + 16), :]
        value = select_dot(value, matrix.astype(BF16))[8 - h3 : 8 + own3 + h3]
        e3p[k + 2, pl.ds(0, own3 + 2 * h3, stride=2), :] = value
        e3p[k + 2, pl.ds(1, own3 + 2 * h3, stride=2), :] = value

    zero_rims(f2)
    zero_rims(v2a)
    zero_rims(v2b)
    planes2 = s2.shape[0]
    for p in range(-5, n2 + 5):
        plane = slab * n2 + p
        inside = jnp.where((plane >= 0) & (plane < planes2), 1.0, 0.0)
        f2[p + 5, 0, 8 : 8 + rows2, :] = s2[jnp.clip(plane, 0, planes2 - 1)] * inside

    def extra2(index, b, first, size):
        return e3p[index >> 1, first : first + size, :]

    h2 = HX // 4
    relax(v2a, 5, (-4, n2 + 4), f2, 5, rows2, h2, edges, n2, extra=extra2, chunk=32)
    relax(v2b, 5, (-3, n2 + 3), f2, 5, rows2, h2, edges, n2, old=v2a, ooff=5, chunk=32)
    relax(v2a, 5, (-2, n2 + 2), f2, 5, rows2, h2, edges, n2, old=v2b, ooff=5, chunk=32)

    n1, rows1 = s1.shape[0], s1.shape[2]
    cut = h2 - HU // 2
    matrix2 = copy_matrix(LANES)
    for k in range(-2, n2 + 2):
        value = select_dot(v2a[k + 5, 0, 8 + cut : 8 + rows2 - cut, :], matrix2)
        for b in range(2):
            part = value[:, LANES * b : LANES * (b + 1)]
            e2p[k + 2, b, pl.ds(0, rows2 - 2 * cut, stride=2), :] = part
            e2p[k + 2, b, pl.ds(1, rows2 - 2 * cut, stride=2), :] = part
    zero_rims(f1)
    zero_rims(v1a)
    zero_rims(v1b)
    near = rows1 - HU
    inner = slice(8 + HU // 2, 8 + HU // 2 + near)
    for b in range(f1.shape[1]):
        for p in range(4):
            first = near * (p * f1.shape[1] + b)
            for plane, message in ((p, below), (4 + n1 + p, above)):
                f1[plane, b, 8:16, :] = jnp.zeros((8, LANES), F32)
                f1[plane, b, rows1 : 8 + rows1, :] = jnp.zeros((8, LANES), F32)
                f1[plane, b, inner, :] = message[first : first + near]
        for p in range(n1):
            f1[4 + p, b, 8 : 8 + rows1, :] = s1[p, b]

    def extra1(index, b, first, size):
        return e2p[(index + 1) >> 1, b, first : first + size, :]

    relax(v1a, 4, (-3, n1 + 3), f1, 4, rows1, HU, edges, n1, extra=extra1)
    relax(v1b, 4, (-2, n1 + 2), f1, 4, rows1, HU, edges, n1, old=v1a, ooff=4)
    relax(e1, 1, (-1, n1 + 1), f1, 4, rows1, HU, edges, n1, old=v1b, ooff=4, shift=0)


def finish_kernel(
    boxes, slabs, n0, x0,
    box_list, e1, f_own, z_below, z_above, below, above,
    out,
    fb, va, vb, ep, ob, sem, out_sem,
):
    edges = Edges(boxes, slabs)
    rows = x0 + 2 * HU
    copies = (
        [pltpu.make_async_copy(f_own, fb.at[pl.ds(3, n0), :, pl.ds(8, rows), :], sem.at[0])]
        + block_copies(z_below, fb, (0, 3), 8 + HU, x0, sem.at[1])
        + block_copies(z_above, fb, (3 + n0, 3), 8 + HU, x0, sem.at[2])
    )
    for copy in copies:
        copy.start()
    zero_rims(fb)
    zero_rims(va)
    zero_rims(vb)
    rim = 8 * 3 * fb.shape[1]
    slots = boxes * max(2, box_list.shape[1] // boxes // 4)
    first = below.shape[0] - rim - 3 * slots
    for z in range(3):
        for b in range(fb.shape[1]):
            at = first + 8 * (fb.shape[1] * z + b)
            for plane, message in ((z, below), (3 + n0 + z, above)):
                fb[plane, b, 8 : 8 + HU, :] = jnp.zeros((HU, LANES), F32)
                fb[plane, b, 8 + HU + x0 : 8 + rows, :] = jnp.zeros((HU, LANES), F32)
                fb[plane, b, 5 + HU : 8 + HU, :] = message[at : at + 3]
                fb[plane, b, 8 + HU + x0 : 11 + HU + x0, :] = message[at + 3 : at + 6]
    matrix = copy_matrix(LANES)
    cut = HU // 2
    r1 = e1.shape[2]
    size1 = r1 - 2 * cut

    def prolong(k):
        for group in range(e1.shape[1]):
            value = select_dot(e1[k, group, cut : r1 - cut, :], matrix)
            for b in range(2):
                part = value[:, LANES * b : LANES * (b + 1)]
                ep[k, 2 * group + b, pl.ds(0, size1, stride=2), :] = part
                ep[k, 2 * group + b, pl.ds(1, size1, stride=2), :] = part

    each(e1.shape[0], prolong)
    for copy in copies:
        copy.wait()
    tiles = Tiles()

    def place(patch, slot):
        lines = [(z, below, z) for z in range(3)] + [(3 + n0 + z, above, z) for z in range(3)]
        tiles.put(
            fb,
            box_list[1, patch] - 4 + HU + 8,
            box_list[2, patch] - 4,
            [(plane, message[pl.ds(first + rim + z * slots + slot, 1), :]) for plane, message, z in lines],
        )

    each_owned(box_list, edges.box, place)

    def extra(index, b, first, size):
        return ep[index >> 1, b, first : first + size, :]

    relax(va, 3, (-2, n0 + 2), fb, 3, rows, HU, edges, n0, extra=extra)
    relax(vb, 3, (-1, n0 + 1), fb, 3, rows, HU, edges, n0, old=va, ooff=3)

    def last(z):
        view = ob.at[pl.ds(z, 1)]
        relax(view, 0, (0, 1), fb.at[pl.ds(z + 3, 1)], 0, rows, HU, edges, None, old=vb.at[pl.ds(z + 2, 3)], ooff=1, shift=-HU, cut=1)
        for copy in block_copies(out.at[pl.ds(z, 1)], ob, (z, 1), 0, x0, out_sem, back=True):
            copy.start()

    each(n0, last)
    for copy in block_copies(out, ob, (0, n0), 0, x0, out_sem, back=True):
        copy.wait()


def shape_of(*dims):
    return jax.ShapeDtypeStruct(dims, F32)


def scratch(*dims):
    return pltpu.VMEM(dims, F32)


def cost(flops, moved):
    return pl.CostEstimate(flops=flops, bytes_accessed=moved, transcendentals=0)


def shift_by(array, axis, step):
    size = lax.axis_size(axis)
    pairs = [(i, i + step) for i in range(size) if 0 <= i + step < size]
    return lax.ppermute(array, axis, pairs)


def per_device(coarse, fine_div, reflux, box_list, cf_mask):
    boxes, slabs = lax.axis_size("box"), lax.axis_size("gz")
    n0, x0, y0 = coarse.shape
    n1, n2 = n0 // 2, n0 // 4
    b0, b1 = y0 // LANES, y0 // LANES // 2
    patches, fine_z, fine_lanes = fine_div.shape
    rows0, rows1, rows2 = x0 + 2 * HX, x0 // 2 + HX, x0 // 4 + HX // 2
    up_rows0, up_rows1 = x0 + 2 * HU, x0 // 2 + 2 * HU
    dma = pltpu.SemaphoreType.DMA

    x_low = shift_by(coarse[:, x0 - HX :], "box", 1)
    x_high = shift_by(coarse[:, :HX], "box", -1)

    z_below = shift_by(coarse[n0 - 3 :], "gz", 1)
    z_above = shift_by(coarse[:3], "gz", -1)

    fine_blocks = fine_lanes // LANES
    packed = pl.pallas_call(
        pack_kernel,
        name="pack",
        out_shape=shape_of(patches * n0, LANES),
        in_specs=[SM, ANY, ANY],
        out_specs=VM,
        scratch_shapes=[
            scratch(fine_blocks, patches, fine_z, LANES),
            scratch(patches, fine_z, LANES),
            dma((fine_blocks + 1,)),
        ],
        compiler_params=PARAMS,
        cost_estimate=cost(10**7, 10**6),
    )(cf_mask.T, fine_div, reflux)
    packed = lax.all_gather(packed, "box", axis=0, tiled=True)

    message = 2 * rows2 + b1 * up_rows1
    slots = boxes * max(2, patches // 4)
    rim = 3 * (8 * b0 + slots)
    f_own, rim_top, rim_bot, c1, c2, up, down = pl.pallas_call(
        functools.partial(down_kernel, boxes, slabs, n0, x0),
        name="down",
        out_shape=(
            shape_of(n0, b0, up_rows0, LANES),
            shape_of(rim, LANES),
            shape_of(rim, LANES),
            shape_of(n1 + 2, b1, up_rows1, LANES),
            shape_of(n2 + 4, 1, rows2, LANES),
            shape_of(message, LANES),
            shape_of(message, LANES),
        ),
        in_specs=[SM, ANY, ANY, ANY, VM],
        out_specs=(ANY,) + (VM,) * 6,
        scratch_shapes=[
            scratch(n0 + 4, b0, rows0 + 16, LANES),
            scratch(n0 + 6, b0, rows0 + 16, LANES),
            scratch(n1 + 8, b1, rows1 + 16, LANES),
            scratch(n1 + 10, b1, rows1 + 16, LANES),
            dma((3,)),
            dma(()),
        ],
        compiler_params=PARAMS,
        cost_estimate=cost(3 * 10**7, 10**7),
    )(box_list.T, coarse, x_low, x_high, packed)

    from_below = shift_by(up, "gz", 1)
    from_above = shift_by(down, "gz", -1)
    copies = pl.pallas_call(
        total_kernel,
        name="total",
        out_shape=shape_of(slabs, n2 * rows2, LANES),
        in_specs=[VM] * 3,
        out_specs=VM,
        compiler_params=PARAMS,
        cost_estimate=cost(10**6, 10**6),
    )(c2, from_below, from_above)
    s2 = lax.all_to_all(copies, "gz", split_axis=0, concat_axis=0, tiled=True)
    s2 = s2.reshape(slabs * n2, rows2, LANES)
    last = 4 * b1 * (up_rows1 - HU) + rim
    s1, up, down = pl.pallas_call(
        functools.partial(join_kernel, rows2),
        name="join",
        out_shape=(shape_of(n1, b1, up_rows1, LANES), shape_of(last, LANES), shape_of(last, LANES)),
        in_specs=[VM] * 5,
        out_specs=(VM,) * 3,
        compiler_params=PARAMS,
        cost_estimate=cost(10**6, 10**6),
    )(c1, from_below, from_above, rim_top, rim_bot)
    below = shift_by(up, "gz", 1)
    above = shift_by(down, "gz", -1)

    planes2, half = slabs * n2, slabs * n2 // 4
    own3 = x0 // 8
    s3 = pl.pallas_call(
        functools.partial(third_kernel, boxes, slabs),
        name="third",
        out_shape=shape_of(half, own3, LANES),
        in_specs=[VM],
        out_specs=VM,
        scratch_shapes=[scratch(planes2 + 2, 1, rows2 + 16, LANES)] * 2,
        compiler_params=PARAMS,
        cost_estimate=cost(10**6, 10**6),
    )(s2)
    s3 = lax.all_gather(s3, "box", axis=0)
    rows3 = boxes * own3
    e1 = pl.pallas_call(
        functools.partial(coarse_kernel, boxes, slabs),
        name="coarse",
        out_shape=shape_of(n1 + 2, b1, up_rows1, LANES),
        in_specs=[VM] * 5,
        out_specs=VM,
        scratch_shapes=[scratch(half, 1, rows3 + 16, LANES)] * 3
        + [scratch(n2 // 2 + 4, rows2, LANES)]
        + [scratch(n2 + 10, 1, rows2 + 16, LANES)] * 3
        + [scratch(n2 + 4, 2, up_rows1, LANES)]
        + [scratch(n1 + 8, b1, up_rows1 + 16, LANES)] * 3,
        compiler_params=PARAMS,
        cost_estimate=cost(10**7, 4 * 10**6),
    )(s3, s2, s1, below, above)

    return pl.pallas_call(
        functools.partial(finish_kernel, boxes, slabs, n0, x0),
        name="finish",
        out_shape=shape_of(n0, x0, y0),
        in_specs=[SM, VM, ANY, ANY, ANY, VM, VM],
        out_specs=ANY,
        scratch_shapes=[scratch(n0 + 6, b0, up_rows0 + 16, LANES)] * 3
        + [
            scratch(n1 + 2, b0, up_rows0, LANES),
            scratch(n0, b0, x0, LANES),
            dma((3,)),
            dma(()),
        ],
        compiler_params=PARAMS,
        cost_estimate=cost(3 * 10**7, 10**7),
    )(box_list.T, e1, f_own, z_below, z_above, below, above)


def solution(mesh):
    return jax.shard_map(
        per_device,
        mesh=mesh,
        in_specs=(P("gz", "box", None), P("box", "gz", None), P("box", "gz", None), P(), P()),
        out_specs=P("gz", "box", None),
        check_vma=False,
    )
```

profile of v0, /device:TPU:19, one launch (start us, length us, event | category | flops | bytes accessed | tf_op | source)
XLA Modules:
  0.0 129.7 jit_solution(10541513821944084617)
XLA Ops:
  0.0 1.3 fusion.1
  1.3 2.6 %collective-permute-start.1 = (f32[8,32,512]{2,1,0:T(8,128)S(1)}, f32[8,32,512]{2,1,0:T(8,128)S(1)}, u32[]{:S(2)}, u32[]{:S(2)}) collective-permute-start(f32[8,32,512]{2,1,0:T(8,128)S(1)} %get-tuple-element.27), channel_id=1, source_target_pairs={{8,0},{16,8},{24,16},{9,1},{17,9},{25,17},{10,2},{18,10},{26,18},{... | collective-permute-start | bytes 1572872 | tf_op jit(solution)/shard_map/ppermute | solution.py:655
  3.9 3.0 %collective-permute-start = (f32[8,32,512]{2,1,0:T(8,128)S(1)}, f32[8,32,512]{2,1,0:T(8,128)S(1)}, u32[]{:S(2)}, u32[]{:S(2)}) collective-permute-start(f32[8,32,512]{2,1,0:T(8,128)S(1)} %get-tuple-element.28), channel_id=1, source_target_pairs={{0,8},{8,16},{16,24},{1,9},{9,17},{17,25},{2,10},{10,18},{18,26},{... | collective-permute-start | bytes 1572872 | tf_op jit(solution)/shard_map/ppermute | solution.py:655
  6.9 0.0 copy-start
  7.0 2.7 %pack.1 = f32[128,128]{1,0:T(8,128)} custom-call(s32[4,64]{1,0:T(4,128)} %bitcast.9, f32[16,16,256]{2,1,0:T(8,128)} %fine.1, f32[16,16,128]{2,1,0:T(8,128)} %flux.1), custom_call_target="tpu_custom_call" | custom-call | flops 10000000 | bytes 1000000 | tf_op jit(solution)/shard_map/pack/pallas_call | solution.py:675
  9.7 6.6 %all_gather.9.packed = f32[512,128]{1,0:T(8,128)} all-gather(f32[128,128]{1,0:T(8,128)} %pack.1), channel_id=1, replica_groups=mesh['box'=4,'gz'=8] {'box'}, dimensions={0}, use_global_device_ids=true | all-gather | bytes 327680 | tf_op jit(solution)/shard_map/all_gather | solution.py:689
  16.3 0.0 collective-permute-done.1.x_high
  16.3 0.0 copy-start.8
  16.4 0.8 copy-done.7
  17.1 0.2 copy-done.8
  17.3 17.9 %down.1 = (f32[8,4,144,128]{3,2,1,0:T(8,128)}, f32[144,128]{1,0:T(8,128)}, f32[144,128]{1,0:T(8,128)}, f32[6,2,80,128]{3,2,1,0:T(8,128)}, f32[6,1,48,128]{3,2,1,...) custom-call(s32[3,64]{1,0:T(4,128)} %bitcast.7, f32[8,128,512]{2,1,0:T(8,128)} %coarse.2, f32[8,32,512]{2,1,0:T(8,128)} %copy-done.8, ...), custom_call_target="tpu_custom_call" | custom-call | flops 30000000 | bytes 10000000 | tf_op jit(solution)/shard_map/down/pallas_call | solution.py:694
  35.2 3.2 %collective-permute-start.2 = (f32[256,128]{1,0:T(8,128)}, f32[256,128]{1,0:T(8,128)S(1)}, u32[]{:S(2)}, u32[]{:S(2)}) collective-permute-start(f32[256,128]{1,0:T(8,128)} %get-tuple-element.16), channel_id=1, source_target_pairs={{0,1},{1,2},{2,3},{3,4},{4,5},{5,6},{6,7},{8,9},{9,10},{10,11},{11... | collective-permute-start | bytes 393224 | tf_op jit(solution)/shard_map/ppermute | solution.py:655
  38.3 2.1 %collective-permute-start.3 = (f32[256,128]{1,0:T(8,128)}, f32[256,128]{1,0:T(8,128)S(1)}, u32[]{:S(2)}, u32[]{:S(2)}) collective-permute-start(f32[256,128]{1,0:T(8,128)} %get-tuple-element.17), channel_id=1, source_target_pairs={{1,0},{2,1},{3,2},{4,3},{5,4},{6,5},{7,6},{9,8},{10,9},{11,10},{12... | collective-permute-start | bytes 393224 | tf_op jit(solution)/shard_map/ppermute | solution.py:655
  40.5 0.2 fusion
  40.7 3.1 %collective-permute-start.7 = (f32[3,128,512]{2,1,0:T(8,128)S(1)}, f32[3,128,512]{2,1,0:T(8,128)S(1)}, u32[]{:S(2)}, u32[]{:S(2)}) collective-permute-start(f32[3,128,512]{2,1,0:T(8,128)S(1)} %get-tuple-element.25), channel_id=1, source_target_pairs={{1,0},{2,1},{3,2},{4,3},{5,4},{6,5},{7,6},{9,8},{10,9},{11,10},{12... | collective-permute-start | bytes 2359304 | tf_op jit(solution)/shard_map/ppermute | solution.py:655
  43.7 3.1 %collective-permute-start.6 = (f32[3,128,512]{2,1,0:T(8,128)S(1)}, f32[3,128,512]{2,1,0:T(8,128)}, u32[]{:S(2)}, u32[]{:S(2)}) collective-permute-start(f32[3,128,512]{2,1,0:T(8,128)S(1)} %get-tuple-element.26), channel_id=1, source_target_pairs={{0,1},{1,2},{2,3},{3,4},{4,5},{5,6},{6,7},{8,9},{9,10},{10,11},{11... | collective-permute-start | bytes 2359304 | tf_op jit(solution)/shard_map/ppermute | solution.py:655
  46.9 0.6 copy-done.5
  47.5 0.0 copy-done.6
  47.6 1.8 %total.1 = f32[8,96,128]{2,1,0:T(8,128)} custom-call(f32[6,1,48,128]{3,2,1,0:T(8,128)} %get-tuple-element.15.c2, f32[256,128]{1,0:T(8,128)} %copy-done.5, f32[256,128]{1,0:T(8,128)} %copy-done.6), custom_call_target="tpu_custom_call" | custom-call | flops 1000000 | bytes 1000000 | tf_op jit(solution)/shard_map/total/pallas_call | solution.py:722
  49.4 4.7 %all-to-all-start = ((f32[8,96,128]{2,1,0:T(8,128)}), f32[8,96,128]{2,1,0:T(8,128)S(1)}, u32[]{:S(2)}, u32[]{:S(2)}) async-start(f32[8,96,128]{2,1,0:T(8,128)} %total.1), calls=%async_computation | async-start | bytes 786432 | tf_op jit(solution)/shard_map/all_to_all | solution.py:731
  54.1 2.2 %join.1 = (f32[4,2,80,128]{3,2,1,0:T(8,128)}, f32[720,128]{1,0:T(8,128)}, f32[720,128]{1,0:T(8,128)}) custom-call(f32[6,2,80,128]{3,2,1,0:T(8,128)} %get-tuple-element.18.c1, f32[256,128]{1,0:T(8,128)} %copy-done.5, f32[256,128]{1,0:T(8,128)} %copy-done.6, f32[144,128]{1,0:T(8,128)} %get-tuple-element.19.rim_top, f32[144,128]{1,0:T(8,128)} %get-tuple-element.20.rim_bot), custom_call_target="tpu_custom_call" | custom-call | flops 1000000 | bytes 1000000 | tf_op jit(solution)/shard_map/join/pallas_call | solution.py:734
  56.2 3.1 %collective-permute-start.4 = (f32[720,128]{1,0:T(8,128)}, f32[720,128]{1,0:T(8,128)S(1)}, u32[]{:S(2)}, u32[]{:S(2)}) collective-permute-start(f32[720,128]{1,0:T(8,128)} %get-tuple-element.22), channel_id=1, source_target_pairs={{0,1},{1,2},{2,3},{3,4},{4,5},{5,6},{6,7},{8,9},{9,10},{10,11},{11... | collective-permute-start | bytes 1105928 | tf_op jit(solution)/shard_map/ppermute | solution.py:655
  59.3 2.2 %collective-permute-start.5 = (f32[720,128]{1,0:T(8,128)}, f32[720,128]{1,0:T(8,128)S(1)}, u32[]{:S(2)}, u32[]{:S(2)}) collective-permute-start(f32[720,128]{1,0:T(8,128)} %get-tuple-element.23), channel_id=1, source_target_pairs={{1,0},{2,1},{3,2},{4,3},{5,4},{6,5},{7,6},{9,8},{10,9},{11,10},{12... | collective-permute-start | bytes 1105928 | tf_op jit(solution)/shard_map/ppermute | solution.py:655
  61.5 30.9 %all-to-all-done = f32[8,96,128]{2,1,0:T(8,128)S(1)} async-done(((f32[8,96,128]{2,1,0:T(8,128)}), f32[8,96,128]{2,1,0:T(8,128)S(1)}, u32[]{:S(2)}, u32[]{:S(2)}) %all-to-all-start) | async-done | bytes 393248 | tf_op jit(solution)/shard_map/all_to_all | solution.py:731
  92.4 0.7 copy-done.1
  93.2 5.0 %third.1 = f32[4,16,128]{2,1,0:T(8,128)} custom-call(f32[16,48,128]{2,1,0:T(8,128)} %bitcast.4), custom_call_target="tpu_custom_call" | custom-call | flops 1000000 | bytes 1000000 | tf_op jit(solution)/shard_map/third/pallas_call | solution.py:748
  98.2 6.7 %all-gather = f32[16,16,128]{2,1,0:T(8,128)} all-gather(f32[4,16,128]{2,1,0:T(8,128)} %third.1), channel_id=2, replica_groups=mesh['box'=4,'gz'=8] {'box'}, dimensions={0}, use_global_device_ids=true | all-gather | bytes 163840 | tf_op jit(solution)/shard_map/all_gather | solution.py:758
  104.9 0.7 copy-done.2
  105.6 0.1 copy-done.3
  105.8 9.5 %coarse.3.e1 = f32[6,2,80,128]{3,2,1,0:T(8,128)} custom-call(f32[4,4,16,128]{3,2,1,0:T(8,128)} %bitcast.6, f32[16,48,128]{2,1,0:T(8,128)} %bitcast.5, f32[4,2,80,128]{3,2,1,0:T(8,128)} %get-tuple-element.21.s1, f32[720,128]{1,0:T(8,128)} %copy-done.2, f32[720,128]{1,0:T(8,128)} %copy-done.3), custom_call_target="tpu_custom_call" | custom-call | flops 10000000 | bytes 4000000 | tf_op jit(solution)/shard_map/coarse/pallas_call | solution.py:760
  115.3 0.9 copy-done.4
  116.2 13.5 %finish.1 = f32[8,128,512]{2,1,0:T(8,128)} custom-call(s32[3,64]{1,0:T(4,128)} %bitcast.8, f32[6,2,80,128]{3,2,1,0:T(8,128)} %coarse.3.e1, f32[8,4,144,128]{3,2,1,0:T(8,128)} %get-tuple-element.24.f_own, f32[3,128,512]{2,1,0:T(8,128)} %collective-permute-done.6.z_below, f32[3,128,512]{2,1,0:T(8,128)} %copy-done.4, f32[720,128]{1,0:T(8,128)} %copy-done.2, ...), custom_call_target="tpu_custom_call" | custom-call | flops 30000000 | bytes 10000000 | tf_op jit(solution)/shard_map/finish/pallas_call | solution.py:775
  (15 shorter events, 0.0 us)
Async XLA Ops:
  1.3 15.0 %collective-permute-start.1 = (f32[8,32,512]{2,1,0:T(8,128)S(1)}, f32[8,32,512]{2,1,0:T(8,128)S(1)}, u32[]{:S(2)}, u32[]{:S(2)}) collective-permute-start(f32[8,32,512]{2,1,0:T(8,128)S(1)} %get-tuple-element.27), channel_id=1, source_target_pairs={{8,0},{16,8},{24,16},{9,1},{17,9},{25,17},{10,2},{18,10},{26,18},{... | collective-permute-start | bytes 1572872 | tf_op jit(solution)/shard_map/ppermute | solution.py:655
  3.9 12.5 %collective-permute-start = (f32[8,32,512]{2,1,0:T(8,128)S(1)}, f32[8,32,512]{2,1,0:T(8,128)S(1)}, u32[]{:S(2)}, u32[]{:S(2)}) collective-permute-start(f32[8,32,512]{2,1,0:T(8,128)S(1)} %get-tuple-element.28), channel_id=1, source_target_pairs={{0,8},{8,16},{16,24},{1,9},{9,17},{17,25},{2,10},{10,18},{18,26},{... | collective-permute-start | bytes 1572872 | tf_op jit(solution)/shard_map/ppermute | solution.py:655
  6.9 33.5 %copy-start = (f32[8,128,512]{2,1,0:T(8,128)S(1)}, f32[8,128,512]{2,1,0:T(8,128)}, u32[]{:S(2)}) copy-start(f32[8,128,512]{2,1,0:T(8,128)} %coarse.2) | copy-start | bytes 6291460
  16.3 0.8 copy-start.7
  16.3 1.0 copy-start.8
  35.2 11.7 %collective-permute-start.2 = (f32[256,128]{1,0:T(8,128)}, f32[256,128]{1,0:T(8,128)S(1)}, u32[]{:S(2)}, u32[]{:S(2)}) collective-permute-start(f32[256,128]{1,0:T(8,128)} %get-tuple-element.16), channel_id=1, source_target_pairs={{0,1},{1,2},{2,3},{3,4},{4,5},{5,6},{6,7},{8,9},{9,10},{10,11},{11... | collective-permute-start | bytes 393224 | tf_op jit(solution)/shard_map/ppermute | solution.py:655
  38.3 8.6 %collective-permute-start.3 = (f32[256,128]{1,0:T(8,128)}, f32[256,128]{1,0:T(8,128)S(1)}, u32[]{:S(2)}, u32[]{:S(2)}) collective-permute-start(f32[256,128]{1,0:T(8,128)} %get-tuple-element.17), channel_id=1, source_target_pairs={{1,0},{2,1},{3,2},{4,3},{5,4},{6,5},{7,6},{9,8},{10,9},{11,10},{12... | collective-permute-start | bytes 393224 | tf_op jit(solution)/shard_map/ppermute | solution.py:655
  40.7 74.6 %collective-permute-start.7 = (f32[3,128,512]{2,1,0:T(8,128)S(1)}, f32[3,128,512]{2,1,0:T(8,128)S(1)}, u32[]{:S(2)}, u32[]{:S(2)}) collective-permute-start(f32[3,128,512]{2,1,0:T(8,128)S(1)} %get-tuple-element.25), channel_id=1, source_target_pairs={{1,0},{2,1},{3,2},{4,3},{5,4},{6,5},{7,6},{9,8},{10,9},{11,10},{12... | collective-permute-start | bytes 2359304 | tf_op jit(solution)/shard_map/ppermute | solution.py:655
  43.7 71.5 %collective-permute-start.6 = (f32[3,128,512]{2,1,0:T(8,128)S(1)}, f32[3,128,512]{2,1,0:T(8,128)}, u32[]{:S(2)}, u32[]{:S(2)}) collective-permute-start(f32[3,128,512]{2,1,0:T(8,128)S(1)} %get-tuple-element.26), channel_id=1, source_target_pairs={{0,1},{1,2},{2,3},{3,4},{4,5},{5,6},{6,7},{8,9},{9,10},{10,11},{11... | collective-permute-start | bytes 2359304 | tf_op jit(solution)/shard_map/ppermute | solution.py:655
  46.9 0.7 copy-start.5
  46.9 0.7 copy-start.6
  49.4 43.0 %all-to-all-start = ((f32[8,96,128]{2,1,0:T(8,128)}), f32[8,96,128]{2,1,0:T(8,128)S(1)}, u32[]{:S(2)}, u32[]{:S(2)}) async-start(f32[8,96,128]{2,1,0:T(8,128)} %total.1), calls=%async_computation | async-start | bytes 786432 | tf_op jit(solution)/shard_map/all_to_all | solution.py:731
  56.2 48.7 %collective-permute-start.4 = (f32[720,128]{1,0:T(8,128)}, f32[720,128]{1,0:T(8,128)S(1)}, u32[]{:S(2)}, u32[]{:S(2)}) collective-permute-start(f32[720,128]{1,0:T(8,128)} %get-tuple-element.22), channel_id=1, source_target_pairs={{0,1},{1,2},{2,3},{3,4},{4,5},{5,6},{6,7},{8,9},{9,10},{10,11},{11... | collective-permute-start | bytes 1105928 | tf_op jit(solution)/shard_map/ppermute | solution.py:655
  59.3 45.6 %collective-permute-start.5 = (f32[720,128]{1,0:T(8,128)}, f32[720,128]{1,0:T(8,128)S(1)}, u32[]{:S(2)}, u32[]{:S(2)}) collective-permute-start(f32[720,128]{1,0:T(8,128)} %get-tuple-element.23), channel_id=1, source_target_pairs={{1,0},{2,1},{3,2},{4,3},{5,4},{6,5},{7,6},{9,8},{10,9},{11,10},{12... | collective-permute-start | bytes 1105928 | tf_op jit(solution)/shard_map/ppermute | solution.py:655
  92.4 0.7 copy-start.1
  104.9 0.7 copy-start.2
  104.9 0.9 copy-start.3
  115.3 0.9 copy-start.4
where the time goes:
time: 131 us; the launch traced here: 130 us
  Pallas kernels  52.6 us (40%)
  waiting for transfers between devices  30.9 us (24%)
  starting transfers between devices  27 us (21%)
  blocking collectives  13.4 us (10%)
  local copies, waits for them, and re-layouts  5.61 us (4%)
    all_to_all x1, waiting for transfers between devices, per_device(): s2 = lax.all_to_all(copies, 'gz', split_axis=0, concat_axis=0, tiled=True)  30.9 us
    ppermute x8, starting transfers between devices, shift_by(): return lax.ppermute(array, axis, pairs)  22.4 us
    pallas_call x1, Pallas kernels, per_device(): pl.pallas_call(functools.partial(down_kernel, boxes, slabs, n0, x0), name...  17.9 us
    pallas_call x1, Pallas kernels, per_device(): pl.pallas_call(functools.partial(finish_kernel, boxes, slabs, n0, x0), na...  13.5 us
    pallas_call x1, Pallas kernels, per_device(): pl.pallas_call(functools.partial(coarse_kernel, boxes, slabs), name='coar...  9.51 us
    all_gather x1, blocking collectives, per_device(): s3 = lax.all_gather(s3, 'box', axis=0)  6.73 us
    all_gather x1, blocking collectives, per_device(): packed = lax.all_gather(packed, 'box', axis=0, tiled=True)  6.62 us
    pallas_call x1, Pallas kernels, per_device(): pl.pallas_call(functools.partial(third_kernel, boxes, slabs), name='third...  4.98 us
  transfers between devices with their start and end apart: 9, of which 1 were waited for; matrix products, arithmetic and copies ran while one was open for 0% of the time, Pallas kernels for 16%

commit v1 on v0

--- a/solution.py
+++ b/solution.py
@@ -20,8 +20,7 @@
 
 VM = pl.BlockSpec(memory_space=pltpu.VMEM)
 SM = pl.BlockSpec(memory_space=pltpu.SMEM)
-ANY = pl.BlockSpec(memory_space=pl.ANY)
-PARAMS = pltpu.CompilerParams(vmem_limit_bytes=56 << 20)
+HBM = pl.BlockSpec(memory_space=pltpu.MemorySpace.HBM)
 
 
 def iota(shape, dim):
@@ -72,17 +71,21 @@
     return sums
 
 
-def around(field, plane, row, rows):
+def around(field, plane, row, rows, has=(True, True, True)):
     count = field.shape[1]
 
     def at(p, first):
         return [field[p, b, first : first + rows, :] for b in range(count)]
 
+    sides = [at(plane + p, row + 8) for p in (-1, 1) if has[p + 1]]
+    if not has[1]:
+        return None, sides[0]
     middle = at(plane, row + 8)
-    parts = zip(
-        at(plane, row + 7), at(plane, row + 9), beside_lanes(middle), at(plane - 1, row + 8), at(plane + 1, row + 8)
-    )
-    return middle, [(a + b) + (c + (d + e)) for a, b, c, d, e in parts]
+    beside = zip(at(plane, row + 7), at(plane, row + 9), beside_lanes(middle))
+    near = [(a + b) + c for a, b, c in beside]
+    for side in sides:
+        near = [a + b for a, b in zip(near, side)]
+    return middle, near
 
 
 class Edges:
@@ -116,14 +119,16 @@
     return row_scale if plane_scale is None else row_scale * plane_scale
 
 
-def relax(new, noff, planes, source, soff, rows, halo, edges, count, old=None, ooff=0, extra=None, chunk=16, shift=8, cut=0):
-    def body(index):
+def relax(new, noff, planes, source, soff, rows, halo, edges, count, old=None, ooff=0, extra=None, chunk=16, shift=8, cut=0, s_planes=None, unroll=1):
+    def body(index, has=(True, True, True)):
         plane_scale = None if count is None else edges.planes(index + planes[0], count)
         for first, size, side in chunks_of(rows, halo, chunk, cut):
             scale = scale_of(side, edges, plane_scale)
             if old is None:
-                middle, near = around(source, index + (planes[0] + soff), first, size)
-                values = [(1.2 * C) * m + (C * C) * n for m, n in zip(middle, near)]
+                middle, near = around(source, index + (planes[0] + soff), first, size, has)
+                values = [(C * C) * n for n in near]
+                if middle is not None:
+                    values = [(1.2 * C) * m + v for m, v in zip(middle, values)]
                 if extra is not None:
                     values = [v + extra(index, b, first, size) for b, v in enumerate(values)]
             else:
@@ -138,15 +143,27 @@
                     value = value * scale
                 new[index + (planes[0] + noff), b, first + shift : first + shift + size, :] = value
 
-    each(planes[1] - planes[0], body)
-
-
-def restrict(source, soff, v, voff, pairs, rows, store, chunk=16):
+    if s_planes is None:
+        each(planes[1] - planes[0], body, unroll)
+        return
+    inner = []
+    for plane in range(*planes):
+        has = tuple(s_planes[0] <= plane + p < s_planes[1] for p in (-1, 0, 1))
+        if all(has):
+            inner.append(plane)
+        else:
+            body(plane - planes[0], has)
+    if inner:
+        first = inner[0] - planes[0]
+        each(len(inner), lambda index: body(index + first), unroll)
+
+
+def restrict(source, soff, v, voff, pairs, rows, summed, store, chunk=8, v_planes=None, s_planes=None):
     count = v.shape[1]
     width = min(2, count)
     half = rows // 2
 
-    def body(index):
+    def body(index, has_v=(True,) * 4, has_s=(True,) * 2):
         low_v, low_s = 2 * index + (2 * pairs[0] + voff), 2 * index + (2 * pairs[0] + soff)
         matrix = pair_matrix(width * LANES)
         for first in range(0, half, chunk):
@@ -155,28 +172,47 @@
             def at(field, plane, b, offset):
                 return field[plane, b, pl.ds(8 + 2 * first + offset, size, stride=2), :]
 
-            whole = [
-                (at(v, low_v, b, 0) + at(v, low_v, b, 1)) + (at(v, low_v + 1, b, 0) + at(v, low_v + 1, b, 1))
-                for b in range(count)
-            ]
-            near = beside_lanes(whole)
+            def both(field, plane, b):
+                return at(field, plane, b, 0) + at(field, plane, b, 1)
+
+            def total_of(terms):
+                total = terms[0]
+                for term in terms[1:]:
+                    total = total + term
+                return total
+
+            inside = [p for p in (1, 2) if has_v[p]]
             sums = []
+            if inside:
+                whole = [total_of([both(v, low_v + p - 1, b) for p in inside]) for b in range(count)]
+                near = beside_lanes(whole)
             for b in range(count):
-                total = near[b] - 4.0 * whole[b]
-                total = total + (at(source, low_s, b, 0) + at(source, low_s, b, 1))
-                total = total + (at(source, low_s + 1, b, 0) + at(source, low_s + 1, b, 1))
-                total = total + (at(v, low_v - 1, b, 0) + at(v, low_v - 1, b, 1))
-                total = total + (at(v, low_v + 2, b, 0) + at(v, low_v + 2, b, 1))
-                total = total + (at(v, low_v, b, -1) + at(v, low_v + 1, b, -1))
-                total = total + (at(v, low_v, b, 2) + at(v, low_v + 1, b, 2))
-                sums.append(total)
-            for group in range(count // width):
-                piece = sums[width * group]
-                if width == 2:
-                    piece = jnp.concatenate([piece, sums[2 * group + 1]], axis=1)
-                store(index, group, first, size, 0.5 * select_dot(piece, matrix))
-
-    each(pairs[1] - pairs[0], body)
+                terms = []
+                if inside:
+                    terms.append(near[b] - 4.0 * whole[b])
+                    terms += [at(v, low_v + p - 1, b, -1) + at(v, low_v + p - 1, b, 2) for p in inside]
+                terms += [both(source, low_s + p, b) for p in (0, 1) if has_s[p]]
+                terms += [both(v, low_v + p - 1, b) for p in (0, 3) if has_v[p]]
+                sums.append(total_of(terms))
+            for b in range(count):
+                summed[b // width, first : first + size, LANES * (b % width) : LANES * (b % width + 1)] = sums[b]
+        for group in range(count // width):
+            store(index, group, 0.5 * select_dot(summed[group], matrix))
+
+    if v_planes is None:
+        each(pairs[1] - pairs[0], body)
+        return
+    inner = []
+    for coarse in range(*pairs):
+        has_v = tuple(v_planes[0] <= 2 * coarse + p - 1 < v_planes[1] for p in range(4))
+        has_s = tuple(s_planes[0] <= 2 * coarse + p < s_planes[1] for p in range(2))
+        if all(has_v + has_s):
+            inner.append(coarse)
+        else:
+            body(coarse - pairs[0], has_v, has_s)
+    if inner:
+        first = inner[0] - pairs[0]
+        each(len(inner), lambda index: body(index + first))
 
 
 def zero(ref, planes):
@@ -203,7 +239,7 @@
     return copies
 
 
-def pack_kernel(mask, fine, flux, out, fine_s, flux_s, sem):
+def pack_kernel(mask, fine, flux, coarse, out, x_first, x_last, z_first, z_last, fine_s, flux_s, sem, edge_sem):
     patches, fine_z = fine.shape[0], fine.shape[1]
     n0 = fine_z // 2
     blocks = fine_s.shape[0]
@@ -212,7 +248,14 @@
         for b in range(blocks)
     ]
     copies.append(pltpu.make_async_copy(flux, flux_s, sem.at[blocks]))
-    for copy in copies:
+    n, x = coarse.shape[0], coarse.shape[1]
+    cuts = [
+        pltpu.make_async_copy(coarse.at[pl.ds(n - 2, 2)], z_last, edge_sem.at[0]),
+        pltpu.make_async_copy(coarse.at[pl.ds(0, 2)], z_first, edge_sem.at[1]),
+        pltpu.make_async_copy(coarse.at[:, pl.ds(x - HX, HX), :], x_last, edge_sem.at[2]),
+        pltpu.make_async_copy(coarse.at[:, pl.ds(0, HX), :], x_first, edge_sem.at[3]),
+    ]
+    for copy in copies + cuts:
         copy.start()
     base = lax.axis_index("box") * patches
     side = (iota((n0, LANES), 1) >> 4) & 3
@@ -243,6 +286,8 @@
     for b in range(blocks):
         total = total + select_dot(jnp.concatenate(fine_rows[b], axis=0), matrices[b + 1])
     out[...] = 0.125 * total
+    for cut in cuts:
+        cut.wait()
 
 
 class Tiles:
@@ -272,24 +317,22 @@
             field[plane, block, pl.ds(row, 16), :] = jnp.where(core, 0.0, now) + jnp.where(ring, tile, 0.0)
 
 
-def each_owned(box_list, box, body):
-    def step(patch, slot):
-        mine = box_list[0, patch] == box
-
-        @pl.when(mine)
-        def _():
-            body(patch, slot)
-
-        return slot + jnp.where(mine, 1, 0)
-
-    lax.fori_loop(0, box_list.shape[1], step, jnp.zeros((), I32))
+def listed(box_list, row_of, found):
+    def step(patch, count):
+        row, keep = row_of(box_list[0, patch], box_list[1, patch])
+        found[0, count] = row
+        found[1, count] = box_list[2, patch] - 4
+        found[2, count] = patch
+        return count + jnp.where(keep, 1, 0)
+
+    return lax.fori_loop(0, box_list.shape[1], step, jnp.zeros((), I32), unroll=8)
 
 
 def down_kernel(
     boxes, slabs, n0, x0,
     box_list, coarse, x_low, x_high, packed,
-    f_own, rim_top, rim_bot, c1, c2, up, down,
-    fb, vb, g1, v1, sem, out_sem,
+    f_own, c1, c2, up, down, third_up, third_down,
+    fb, vb, g1, v1, summed0, summed1, found, owned, sem, out_sem,
 ):
     edges = Edges(boxes, slabs)
     rows0, rows1, rows2 = x0 + 2 * HX, x0 // 2 + HX, x0 // 4 + HX // 2
@@ -301,66 +344,56 @@
     )
     for copy in copies:
         copy.start()
-    zero(fb, (0, 1, n0 + 2, n0 + 3))
-    zero_rims(fb, range(2, n0 + 2))
-    zero(vb, (0, 1, n0 + 4, n0 + 5))
-    zero_rims(vb, range(2, n0 + 4))
-    zero(g1, (0, 1, 2, n1 + 5, n1 + 6, n1 + 7))
-    zero_rims(g1, range(3, n1 + 5))
-    zero(v1, (0, 1, 2, n1 + 7, n1 + 8, n1 + 9))
-    zero_rims(v1, range(3, n1 + 7))
+
+    def near_row(owner, x):
+        row = (owner - edges.box) * x0 + x - 4 + HX
+        return row + 8, (row >= 0) & (row < rows0)
+
+    def own_row(owner, x):
+        return x, owner == edges.box
+
+    near_count = listed(box_list, near_row, found)
+    own_count = listed(box_list, own_row, owned)
     for copy in copies:
         copy.wait()
-
     tiles = Tiles()
 
-    def place(patch):
-        start = (box_list[0, patch] - edges.box) * x0 + box_list[1, patch] - 4 + HX
-
-        @pl.when((start >= 0) & (start < rows0))
-        def _():
-            tiles.put(
-                fb,
-                start + 8,
-                box_list[2, patch] - 4,
-                [(2 + z, packed[pl.ds(patch * n0 + z, 1), :]) for z in range(n0)],
-            )
-
-    each(box_list.shape[1], place)
+    def place(index):
+        patch = found[2, index]
+        lines = [(2 + z, packed[pl.ds(patch * n0 + z, 1), :]) for z in range(n0)]
+        tiles.put(fb, found[0, index], found[1, index], lines)
+
+    lax.fori_loop(0, near_count, lambda index, carry: place(index) or carry, 0)
 
     inner = pl.ds(8 + HX - HU, x0 + 2 * HU)
     out_copy = pltpu.make_async_copy(fb.at[pl.ds(2, n0), :, inner, :], f_own, out_sem)
     out_copy.start()
 
-    relax(vb, 3, (-1, n0 + 1), fb, 2, rows0, HX, edges, n0)
+    relax(vb, 3, (-1, n0 + 1), fb, 2, rows0, HX, edges, n0, s_planes=(0, n0), unroll=2)
 
     h1 = HX // 2
 
-    def store1(index, group, first, size, value):
-        scale = edges.planes(index - 1, n1)
-        if first < h1:
-            scale = scale * edges.low()
-        if first >= rows1 - h1:
-            scale = scale * edges.high()
-        g1[index + 3, group, 8 + first : 8 + first + size, :] = value * scale
-
-    restrict(fb, 2, vb, 3, (-1, n1 + 1), rows0, store1)
+    def store1(index, group, value):
+        value = value * edges.planes(index - 1, n1)
+        g1[index + 3, group, 8 : 8 + h1, :] = value[:h1] * edges.low()
+        g1[index + 3, group, 8 + h1 : 8 + rows1 - h1, :] = value[h1 : rows1 - h1]
+        g1[index + 3, group, 8 + rows1 - h1 : 8 + rows1, :] = value[rows1 - h1 :] * edges.high()
+
+    restrict(fb, 2, vb, 3, (-1, n1 + 1), rows0, summed0, store1, v_planes=(-1, n0 + 1), s_planes=(0, n0))
     for plane in range(n1 + 2):
         for b in range(g1.shape[1]):
             c1[plane, b] = g1[plane + 3, b, 8 + h1 - HU : 8 + rows1 - h1 + HU, :]
 
-    relax(v1, 5, (-2, n1 + 2), g1, 4, rows1, h1, edges, n1)
+    relax(v1, 5, (-2, n1 + 2), g1, 4, rows1, h1, edges, n1, s_planes=(-1, n1 + 1))
 
     h2 = HX // 4
 
-    def store2(index, group, first, size, value):
-        if first < h2:
-            value = value * edges.low()
-        if first >= rows2 - h2:
-            value = value * edges.high()
-        c2[index, group, first : first + size, :] = value
-
-    restrict(g1, 4, v1, 5, (-2, n2 + 2), rows1, store2, chunk=8)
+    def store2(index, group, value):
+        c2[index, group, 0:h2, :] = value[:h2] * edges.low()
+        c2[index, group, h2 : rows2 - h2, :] = value[h2 : rows2 - h2]
+        c2[index, group, rows2 - h2 : rows2, :] = value[rows2 - h2 :] * edges.high()
+
+    restrict(g1, 4, v1, 5, (-2, n2 + 2), rows1, summed1, store2, v_planes=(-2, n1 + 2), s_planes=(-1, n1 + 1))
 
     r1 = c1.shape[2]
     for target, fine_plane, coarse_first in ((up, n1 + 1, n2 + 2), (down, 0, 0)):
@@ -370,24 +403,30 @@
             first = 2 * rows2 + b * r1
             target[first : first + r1] = c1[fine_plane, b]
 
-    slots = rim_top.shape[0] - 24 * fb.shape[1]
-    base = 24 * fb.shape[1]
-
-    def keep(patch, slot):
-        for z in range(3):
-            rim_top[pl.ds(base + z * (slots // 3) + slot, 1), :] = packed[pl.ds(patch * n0 + n0 - 3 + z, 1), :]
-            rim_bot[pl.ds(base + z * (slots // 3) + slot, 1), :] = packed[pl.ds(patch * n0 + z, 1), :]
-
-    rim_top[base:, :] = jnp.zeros((slots, LANES), F32)
-    rim_bot[base:, :] = jnp.zeros((slots, LANES), F32)
-    each_owned(box_list, edges.box, keep)
-    for z in range(3):
-        for b in range(fb.shape[1]):
-            first = 8 * (fb.shape[1] * z + b)
-            for rim, plane in ((rim_top, n0 - 1 + z), (rim_bot, 2 + z)):
-                rim[first : first + 3, :] = fb[plane, b, 8 + HX - 3 : 8 + HX, :]
-                rim[first + 3 : first + 6, :] = fb[plane, b, 8 + HX + x0 : 8 + HX + x0 + 3, :]
-                rim[first + 6 : first + 8, :] = jnp.zeros((2, LANES), F32)
+    rim = 2 * rows2 + c1.shape[1] * r1
+    slots = (up.shape[0] - rim) // 2 - 8 * fb.shape[1]
+    wide = third_up.shape[0] // fb.shape[1]
+    for b in range(fb.shape[1]):
+        at = slice(4 + HX, 4 + HX + wide)
+        third_up[wide * b : wide * (b + 1)] = fb[n0 - 1, b, at, :]
+        third_down[wide * b : wide * (b + 1)] = fb[4, b, at, :]
+        for z in range(2):
+            first = rim + 8 * (fb.shape[1] * z + b)
+            for target, plane in ((up, n0 + z), (down, 2 + z)):
+                target[first : first + 3, :] = fb[plane, b, 8 + HX - 3 : 8 + HX, :]
+                target[first + 3 : first + 6, :] = fb[plane, b, 8 + HX + x0 : 8 + HX + x0 + 3, :]
+                target[first + 6 : first + 8, :] = jnp.zeros((2, LANES), F32)
+    rim = rim + 16 * fb.shape[1]
+    up[rim:, :] = jnp.zeros((2 * slots, LANES), F32)
+    down[rim:, :] = jnp.zeros((2 * slots, LANES), F32)
+
+    def keep(slot):
+        patch = owned[2, slot]
+        for z in range(2):
+            up[pl.ds(rim + z * slots + slot, 1), :] = packed[pl.ds(patch * n0 + n0 - 2 + z, 1), :]
+            down[pl.ds(rim + z * slots + slot, 1), :] = packed[pl.ds(patch * n0 + z, 1), :]
+
+    lax.fori_loop(0, own_count, lambda index, carry: keep(index) or carry, 0)
     out_copy.wait()
 
 
@@ -404,7 +443,7 @@
             copies[slab, plane * rows2 : (plane + 1) * rows2] = value
 
 
-def join_kernel(rows2, c1, below, above, rim_top, rim_bot, s1, up, down):
+def join_kernel(rows2, c1, below, above, third_up, third_down, s1, up, down):
     n1, r1 = s1.shape[0], c1.shape[2]
     for plane in range(n1):
         s1[plane] = c1[1 + plane]
@@ -419,17 +458,15 @@
             up[first : first + near] = s1[n1 - 4 + p, b, HU // 2 : HU // 2 + near, :]
             down[first : first + near] = s1[p, b, HU // 2 : HU // 2 + near, :]
     first = near * 4 * s1.shape[1]
-    up[first:] = rim_top[...]
-    down[first:] = rim_bot[...]
-
-
-def third_kernel(boxes, slabs, s2, s3, fb, vb):
+    up[first:] = third_up[...]
+    down[first:] = third_down[...]
+
+
+def third_kernel(boxes, slabs, s2, s3, fb, vb, summed):
     edges = Edges(boxes, slabs)
     planes, rows = s2.shape[0], s2.shape[1]
     zero(fb, (0, planes + 1))
     zero(vb, (0, planes + 1))
-    zero_rims(fb, range(1, planes + 1))
-    zero_rims(vb, range(1, planes + 1))
     for plane in range(planes):
         fb[plane + 1, 0, 8 : 8 + rows, :] = s2[plane]
     relax(vb, 1, (0, planes), fb, 1, rows, HX // 4, edges, None, chunk=32)
@@ -440,21 +477,16 @@
 
     for part in range(2):
 
-        def store(index, group, first, size, value, part=part):
+        def store(index, group, value, part=part):
             s3[index, :, lanes * part : lanes * (part + 1)] = value[h3 : h3 + own]
 
-        restrict(
-            fb, 1, vb, 1, (quarter * part, quarter * (part + 1)), rows, store, chunk=rows // 2
-        )
-
-
-def coarse_kernel(
-    boxes, slabs,
-    s3, s2, s1, below, above,
-    e1,
+        restrict(fb, 1, vb, 1, (quarter * part, quarter * (part + 1)), rows, summed, store)
+
+
+def coarse_levels(
+    edges, boxes, slabs, s3, s2, s1, below, above, e1,
     sc, va3, vb3, e3p, f2, v2a, v2b, e2p, f1, v1a, v1b,
 ):
-    edges = Edges(boxes, slabs)
     slab = edges.slab
     half, rows3 = sc.shape[0], sc.shape[2] - 16
     own3 = s3.shape[2]
@@ -513,9 +545,6 @@
         e3p[k + 2, pl.ds(0, own3 + 2 * h3, stride=2), :] = value
         e3p[k + 2, pl.ds(1, own3 + 2 * h3, stride=2), :] = value
 
-    zero_rims(f2)
-    zero_rims(v2a)
-    zero_rims(v2b)
     planes2 = s2.shape[0]
     for p in range(-5, n2 + 5):
         plane = slab * n2 + p
@@ -539,17 +568,12 @@
             part = value[:, LANES * b : LANES * (b + 1)]
             e2p[k + 2, b, pl.ds(0, rows2 - 2 * cut, stride=2), :] = part
             e2p[k + 2, b, pl.ds(1, rows2 - 2 * cut, stride=2), :] = part
-    zero_rims(f1)
-    zero_rims(v1a)
-    zero_rims(v1b)
     near = rows1 - HU
     inner = slice(8 + HU // 2, 8 + HU // 2 + near)
     for b in range(f1.shape[1]):
         for p in range(4):
             first = near * (p * f1.shape[1] + b)
             for plane, message in ((p, below), (4 + n1 + p, above)):
-                f1[plane, b, 8:16, :] = jnp.zeros((8, LANES), F32)
-                f1[plane, b, rows1 : 8 + rows1, :] = jnp.zeros((8, LANES), F32)
                 f1[plane, b, inner, :] = message[first : first + near]
         for p in range(n1):
             f1[4 + p, b, 8 : 8 + rows1, :] = s1[p, b]
@@ -562,77 +586,103 @@
     relax(e1, 1, (-1, n1 + 1), f1, 4, rows1, HU, edges, n1, old=v1b, ooff=4, shift=0)
 
 
-def finish_kernel(
-    boxes, slabs, n0, x0,
-    box_list, e1, f_own, z_below, z_above, below, above,
-    out,
-    fb, va, vb, ep, ob, sem, out_sem,
+def early_kernel(
+    boxes, slabs, n0, x0, rim,
+    box_list, f_own, z_below, z_above, below, above,
+    f_out, v_out,
+    fb, va, found, sem, out_sem,
 ):
     edges = Edges(boxes, slabs)
     rows = x0 + 2 * HU
     copies = (
-        [pltpu.make_async_copy(f_own, fb.at[pl.ds(3, n0), :, pl.ds(8, rows), :], sem.at[0])]
-        + block_copies(z_below, fb, (0, 3), 8 + HU, x0, sem.at[1])
-        + block_copies(z_above, fb, (3 + n0, 3), 8 + HU, x0, sem.at[2])
+        [pltpu.make_async_copy(f_own, fb.at[pl.ds(2, n0), :, pl.ds(8, rows), :], sem.at[0])]
+        + block_copies(z_below, fb, (0, 2), 8 + HU, x0, sem.at[1])
+        + block_copies(z_above, fb, (2 + n0, 2), 8 + HU, x0, sem.at[2])
     )
     for copy in copies:
         copy.start()
-    zero_rims(fb)
-    zero_rims(va)
-    zero_rims(vb)
-    rim = 8 * 3 * fb.shape[1]
-    slots = boxes * max(2, box_list.shape[1] // boxes // 4)
-    first = below.shape[0] - rim - 3 * slots
-    for z in range(3):
+
+    def own_row(owner, x):
+        return x - 4 + HU + 8, owner == edges.box
+
+    count = listed(box_list, own_row, found)
+    packed = rim + 16 * fb.shape[1]
+    slots = (below.shape[0] - packed) // 2
+    for copy in copies:
+        copy.wait()
+    for z in range(2):
         for b in range(fb.shape[1]):
-            at = first + 8 * (fb.shape[1] * z + b)
-            for plane, message in ((z, below), (3 + n0 + z, above)):
-                fb[plane, b, 8 : 8 + HU, :] = jnp.zeros((HU, LANES), F32)
-                fb[plane, b, 8 + HU + x0 : 8 + rows, :] = jnp.zeros((HU, LANES), F32)
+            at = rim + 8 * (fb.shape[1] * z + b)
+            for plane, message in ((z, below), (2 + n0 + z, above)):
                 fb[plane, b, 5 + HU : 8 + HU, :] = message[at : at + 3]
                 fb[plane, b, 8 + HU + x0 : 11 + HU + x0, :] = message[at + 3 : at + 6]
+    tiles = Tiles()
+
+    def place(slot):
+        lines = [(z, below, z) for z in range(2)] + [(2 + n0 + z, above, z) for z in range(2)]
+        lines = [(plane, message[pl.ds(packed + z * slots + slot, 1), :]) for plane, message, z in lines]
+        tiles.put(fb, found[0, slot], found[1, slot], lines)
+
+    lax.fori_loop(0, count, lambda index, carry: place(index) or carry, 0)
+    f_copy = pltpu.make_async_copy(fb.at[pl.ds(1, n0 + 2)], f_out, out_sem.at[0])
+    f_copy.start()
+    relax(va, 2, (-2, n0 + 2), fb, 2, rows, HU, edges, n0, s_planes=(-2, n0 + 2), unroll=2)
+    v_copy = pltpu.make_async_copy(va, v_out, out_sem.at[1])
+    v_copy.start()
+    f_copy.wait()
+    v_copy.wait()
+
+
+def tail_kernel(
+    boxes, slabs, n0, x0,
+    s3, s2, s1, below, above, f_in, v_in,
+    out,
+    sc, va3, vb3, e3p, f2, v2a, v2b, e2p, f1, v1a, v1b, e1,
+    fb, va, vb, ob, sem, out_sem,
+):
+    f_copy = pltpu.make_async_copy(f_in, fb, sem.at[0])
+    v_copy = pltpu.make_async_copy(v_in, va.at[pl.ds(1, n0 + 4)], sem.at[1])
+    f_copy.start()
+    v_copy.start()
+    edges = Edges(boxes, slabs)
+    coarse_levels(
+        edges, boxes, slabs, s3, s2, s1, below, above, e1,
+        sc, va3, vb3, e3p, f2, v2a, v2b, e2p, f1, v1a, v1b,
+    )
+    f_copy.wait()
+    v_copy.wait()
+    rows = x0 + 2 * HU
     matrix = copy_matrix(LANES)
     cut = HU // 2
     r1 = e1.shape[2]
     size1 = r1 - 2 * cut
+    first = 4 * s1.shape[1] * (r1 - HU)
+    wide = (below.shape[0] - first) // fb.shape[1]
+    for b in range(fb.shape[1]):
+        at = slice(4 + HU, 4 + HU + wide)
+        for plane, message in ((1, below), (4 + n0, above)):
+            va[plane, b, at, :] = va[plane, b, at, :] + (C * C) * message[first + wide * b : first + wide * (b + 1)]
 
     def prolong(k):
         for group in range(e1.shape[1]):
             value = select_dot(e1[k, group, cut : r1 - cut, :], matrix)
             for b in range(2):
                 part = value[:, LANES * b : LANES * (b + 1)]
-                ep[k, 2 * group + b, pl.ds(0, size1, stride=2), :] = part
-                ep[k, 2 * group + b, pl.ds(1, size1, stride=2), :] = part
+                for plane in (2 * k + 1, 2 * k + 2):
+                    for start in (8, 9):
+                        at = pl.ds(start, size1, stride=2)
+                        va[plane, 2 * group + b, at, :] = va[plane, 2 * group + b, at, :] + part
 
     each(e1.shape[0], prolong)
-    for copy in copies:
-        copy.wait()
-    tiles = Tiles()
-
-    def place(patch, slot):
-        lines = [(z, below, z) for z in range(3)] + [(3 + n0 + z, above, z) for z in range(3)]
-        tiles.put(
-            fb,
-            box_list[1, patch] - 4 + HU + 8,
-            box_list[2, patch] - 4,
-            [(plane, message[pl.ds(first + rim + z * slots + slot, 1), :]) for plane, message, z in lines],
-        )
-
-    each_owned(box_list, edges.box, place)
-
-    def extra(index, b, first, size):
-        return ep[index >> 1, b, first : first + size, :]
-
-    relax(va, 3, (-2, n0 + 2), fb, 3, rows, HU, edges, n0, extra=extra)
-    relax(vb, 3, (-1, n0 + 1), fb, 3, rows, HU, edges, n0, old=va, ooff=3)
+    relax(vb, 3, (-1, n0 + 1), fb, 1, rows, HU, edges, n0, old=va, ooff=3, unroll=2)
 
     def last(z):
         view = ob.at[pl.ds(z, 1)]
-        relax(view, 0, (0, 1), fb.at[pl.ds(z + 3, 1)], 0, rows, HU, edges, None, old=vb.at[pl.ds(z + 2, 3)], ooff=1, shift=-HU, cut=1)
+        relax(view, 0, (0, 1), fb.at[pl.ds(z + 1, 1)], 0, rows, HU, edges, None, old=vb.at[pl.ds(z + 2, 3)], ooff=1, shift=-HU, cut=1)
         for copy in block_copies(out.at[pl.ds(z, 1)], ob, (z, 1), 0, x0, out_sem, back=True):
             copy.start()
 
-    each(n0, last)
+    each(n0, last, unroll=2)
     for copy in block_copies(out, ob, (0, n0), 0, x0, out_sem, back=True):
         copy.wait()
 
@@ -643,6 +693,14 @@
 
 def scratch(*dims):
     return pltpu.VMEM(dims, F32)
+
+
+def in_hbm(array):
+    return pltpu.with_memory_space_constraint(array, pltpu.MemorySpace.HBM)
+
+
+def limit(mebibytes):
+    return pltpu.CompilerParams(vmem_limit_bytes=mebibytes << 20)
 
 
 def cost(flops, moved):
@@ -665,57 +723,66 @@
     up_rows0, up_rows1 = x0 + 2 * HU, x0 // 2 + 2 * HU
     dma = pltpu.SemaphoreType.DMA
 
-    x_low = shift_by(coarse[:, x0 - HX :], "box", 1)
-    x_high = shift_by(coarse[:, :HX], "box", -1)
-
-    z_below = shift_by(coarse[n0 - 3 :], "gz", 1)
-    z_above = shift_by(coarse[:3], "gz", -1)
-
     fine_blocks = fine_lanes // LANES
-    packed = pl.pallas_call(
+    packed, x_first, x_last, z_first, z_last = pl.pallas_call(
         pack_kernel,
         name="pack",
-        out_shape=shape_of(patches * n0, LANES),
-        in_specs=[SM, ANY, ANY],
-        out_specs=VM,
+        out_shape=(
+            shape_of(patches * n0, LANES),
+            shape_of(n0, HX, y0),
+            shape_of(n0, HX, y0),
+            shape_of(2, x0, y0),
+            shape_of(2, x0, y0),
+        ),
+        in_specs=[SM, HBM, HBM, HBM],
+        out_specs=(VM,) * 5,
         scratch_shapes=[
             scratch(fine_blocks, patches, fine_z, LANES),
             scratch(patches, fine_z, LANES),
             dma((fine_blocks + 1,)),
+            dma((4,)),
         ],
-        compiler_params=PARAMS,
+        compiler_params=limit(4),
         cost_estimate=cost(10**7, 10**6),
-    )(cf_mask.T, fine_div, reflux)
+    )(in_hbm(cf_mask.T), in_hbm(fine_div), in_hbm(reflux), in_hbm(coarse))
+    z_below = shift_by(z_last, "gz", 1)
+    z_above = shift_by(z_first, "gz", -1)
+    x_low = shift_by(x_last, "box", 1)
+    x_high = shift_by(x_first, "box", -1)
     packed = lax.all_gather(packed, "box", axis=0, tiled=True)
 
-    message = 2 * rows2 + b1 * up_rows1
     slots = boxes * max(2, patches // 4)
-    rim = 3 * (8 * b0 + slots)
-    f_own, rim_top, rim_bot, c1, c2, up, down = pl.pallas_call(
+    rim = 2 * rows2 + b1 * up_rows1
+    message = rim + 2 * (8 * b0 + slots)
+    f_own, c1, c2, up, down, third_up, third_down = pl.pallas_call(
         functools.partial(down_kernel, boxes, slabs, n0, x0),
         name="down",
         out_shape=(
-            shape_of(n0, b0, up_rows0, LANES),
-            shape_of(rim, LANES),
-            shape_of(rim, LANES),
+            pltpu.MemorySpace.HBM((n0, b0, up_rows0, LANES), F32),
             shape_of(n1 + 2, b1, up_rows1, LANES),
             shape_of(n2 + 4, 1, rows2, LANES),
             shape_of(message, LANES),
             shape_of(message, LANES),
+            shape_of(b0 * (x0 + HU), LANES),
+            shape_of(b0 * (x0 + HU), LANES),
         ),
-        in_specs=[SM, ANY, ANY, ANY, VM],
-        out_specs=(ANY,) + (VM,) * 6,
+        in_specs=[SM, HBM, HBM, HBM, VM],
+        out_specs=(HBM,) + (VM,) * 6,
         scratch_shapes=[
             scratch(n0 + 4, b0, rows0 + 16, LANES),
             scratch(n0 + 6, b0, rows0 + 16, LANES),
             scratch(n1 + 8, b1, rows1 + 16, LANES),
             scratch(n1 + 10, b1, rows1 + 16, LANES),
+            scratch(b0 // 2, rows1, 2 * LANES),
+            scratch(max(1, b1 // 2), rows2, min(2, b1) * LANES),
+            pltpu.SMEM((3, box_list.shape[0]), I32),
+            pltpu.SMEM((3, box_list.shape[0]), I32),
             dma((3,)),
             dma(()),
         ],
-        compiler_params=PARAMS,
+        compiler_params=limit(20),
         cost_estimate=cost(3 * 10**7, 10**7),
-    )(box_list.T, coarse, x_low, x_high, packed)
+    )(in_hbm(box_list.T), in_hbm(coarse), x_low, x_high, packed)
 
     from_below = shift_by(up, "gz", 1)
     from_above = shift_by(down, "gz", -1)
@@ -725,23 +792,44 @@
         out_shape=shape_of(slabs, n2 * rows2, LANES),
         in_specs=[VM] * 3,
         out_specs=VM,
-        compiler_params=PARAMS,
+        compiler_params=limit(3),
         cost_estimate=cost(10**6, 10**6),
     )(c2, from_below, from_above)
     s2 = lax.all_to_all(copies, "gz", split_axis=0, concat_axis=0, tiled=True)
     s2 = s2.reshape(slabs * n2, rows2, LANES)
-    last = 4 * b1 * (up_rows1 - HU) + rim
+    last = 4 * b1 * (up_rows1 - HU) + b0 * (x0 + HU)
     s1, up, down = pl.pallas_call(
         functools.partial(join_kernel, rows2),
         name="join",
         out_shape=(shape_of(n1, b1, up_rows1, LANES), shape_of(last, LANES), shape_of(last, LANES)),
         in_specs=[VM] * 5,
         out_specs=(VM,) * 3,
-        compiler_params=PARAMS,
+        compiler_params=limit(5),
         cost_estimate=cost(10**6, 10**6),
-    )(c1, from_below, from_above, rim_top, rim_bot)
+    )(c1, from_below, from_above, third_up, third_down)
     below = shift_by(up, "gz", 1)
     above = shift_by(down, "gz", -1)
+
+    hbm = pltpu.MemorySpace.HBM
+    f_wide, v_wide = pl.pallas_call(
+        functools.partial(early_kernel, boxes, slabs, n0, x0, rim),
+        name="early",
+        out_shape=(
+            hbm((n0 + 2, b0, up_rows0 + 16, LANES), F32),
+            hbm((n0 + 4, b0, up_rows0 + 16, LANES), F32),
+        ),
+        in_specs=[SM, HBM, HBM, HBM, VM, VM],
+        out_specs=(HBM, HBM),
+        scratch_shapes=[
+            scratch(n0 + 4, b0, up_rows0 + 16, LANES),
+            scratch(n0 + 4, b0, up_rows0 + 16, LANES),
+            pltpu.SMEM((3, box_list.shape[0]), I32),
+            dma((3,)),
+            dma((2,)),
+        ],
+        compiler_params=limit(14),
+        cost_estimate=cost(2 * 10**7, 10**7),
+    )(in_hbm(box_list.T), in_hbm(f_own), in_hbm(z_below), in_hbm(z_above), from_below, from_above)
 
     planes2, half = slabs * n2, slabs * n2 // 4
     own3 = x0 // 8
@@ -751,43 +839,30 @@
         out_shape=shape_of(half, own3, LANES),
         in_specs=[VM],
         out_specs=VM,
-        scratch_shapes=[scratch(planes2 + 2, 1, rows2 + 16, LANES)] * 2,
-        compiler_params=PARAMS,
+        scratch_shapes=[scratch(planes2 + 2, 1, rows2 + 16, LANES)] * 2 + [scratch(1, rows2 // 2, LANES)],
+        compiler_params=limit(4),
         cost_estimate=cost(10**6, 10**6),
     )(s2)
     s3 = lax.all_gather(s3, "box", axis=0)
     rows3 = boxes * own3
-    e1 = pl.pallas_call(
-        functools.partial(coarse_kernel, boxes, slabs),
-        name="coarse",
-        out_shape=shape_of(n1 + 2, b1, up_rows1, LANES),
-        in_specs=[VM] * 5,
-        out_specs=VM,
+    return pl.pallas_call(
+        functools.partial(tail_kernel, boxes, slabs, n0, x0),
+        name="tail",
+        out_shape=shape_of(n0, x0, y0),
+        in_specs=[VM] * 5 + [HBM, HBM],
+        out_specs=HBM,
         scratch_shapes=[scratch(half, 1, rows3 + 16, LANES)] * 3
         + [scratch(n2 // 2 + 4, rows2, LANES)]
         + [scratch(n2 + 10, 1, rows2 + 16, LANES)] * 3
         + [scratch(n2 + 4, 2, up_rows1, LANES)]
-        + [scratch(n1 + 8, b1, up_rows1 + 16, LANES)] * 3,
-        compiler_params=PARAMS,
-        cost_estimate=cost(10**7, 4 * 10**6),
-    )(s3, s2, s1, below, above)
-
-    return pl.pallas_call(
-        functools.partial(finish_kernel, boxes, slabs, n0, x0),
-        name="finish",
-        out_shape=shape_of(n0, x0, y0),
-        in_specs=[SM, VM, ANY, ANY, ANY, VM, VM],
-        out_specs=ANY,
-        scratch_shapes=[scratch(n0 + 6, b0, up_rows0 + 16, LANES)] * 3
-        + [
-            scratch(n1 + 2, b0, up_rows0, LANES),
-            scratch(n0, b0, x0, LANES),
-            dma((3,)),
-            dma(()),
-        ],
-        compiler_params=PARAMS,
-        cost_estimate=cost(3 * 10**7, 10**7),
-    )(box_list.T, e1, f_own, z_below, z_above, below, above)
+        + [scratch(n1 + 8, b1, up_rows1 + 16, LANES)] * 3
+        + [scratch(n1 + 2, b1, up_rows1, LANES)]
+        + [scratch(n0 + 2, b0, up_rows0 + 16, LANES)]
+        + [scratch(n0 + 6, b0, up_rows0 + 16, LANES)] * 2
+        + [scratch(n0, b0, x0, LANES), dma((2,)), dma(())],
+        compiler_params=limit(28),
+        cost_estimate=cost(4 * 10**7, 10**7),
+    )(s3, s2, s1, below, above, in_hbm(f_wide), in_hbm(v_wide))
 
 
 def solution(mesh):

time: 131 us -> 127 us (0.969)
  Pallas kernels: 52.6 us -> 41.3 us
  waiting for transfers between devices: 30.9 us -> 37.4 us
  local copies, waits for them, and re-layouts: 5.61 us -> 0.79 us
  blocking collectives: 13.4 us -> 17.6 us
    ppermute x8, waiting for transfers between devices: 0.02 us -> 37.4 us  [shift_by(): return lax.ppermute(array, axis, pairs)]
    all_to_all x1, waiting for transfers between devices: 30.9 us -> 0.01 us  [per_device(): s2 = lax.all_to_all(copies, 'gz', split_axis=0, concat_axis=0, tiled=True)]
    pallas_call x1, Pallas kernels: 17.9 us -> 11.8 us  [per_device(): pl.pallas_call(functools.partial(down_kernel, boxes, slabs, n0, x0), name...]
    all_gather x1, blocking collectives: 6.62 us -> 11.3 us  [per_device(): packed = lax.all_gather(packed, 'box', axis=0, tiled=True)]
    unnamed x18 -> x4, local copies, waits for them, and re-layouts: 4.13 us -> 0.79 us
    pallas_call x1, Pallas kernels: 2.17 us -> 0.11 us  [per_device(): pl.pallas_call(functools.partial(join_kernel, rows2), name='join', out_sh...]
    pallas_call x1, Pallas kernels: 4.98 us -> 3.38 us  [per_device(): pl.pallas_call(functools.partial(third_kernel, boxes, slabs), name='third...]
    slice x2 -> x0, local copies, waits for them, and re-layouts: 1.49 us -> none  [the longest x1 1.29 us: per_device(): x_high = shift_by(coarse[:, :HX], 'box', -1)]
  transfers between devices with their start and end apart: 9 -> 9, of which waited for: 1 -> 4; matrix products, arithmetic and copies ran while one was open for 0% -> 0% of each run, Pallas kernels for 16% -> 10%
where the time goes in v1:
time: 127 us; the launch traced here: 125 us
  Pallas kernels  41.3 us (33%)
  waiting for transfers between devices  37.4 us (29%)
  starting transfers between devices  27.4 us (22%)
  blocking collectives  17.6 us (14%)
    ppermute x8, waiting for transfers between devices, shift_by(): return lax.ppermute(array, axis, pairs)  37.4 us
    ppermute x8, starting transfers between devices, shift_by(): return lax.ppermute(array, axis, pairs)  22.1 us
    pallas_call x1, Pallas kernels, per_device(): pl.pallas_call(functools.partial(tail_kernel, boxes, slabs, n0, x0), name...  12.7 us
    pallas_call x1, Pallas kernels, per_device(): pl.pallas_call(functools.partial(down_kernel, boxes, slabs, n0, x0), name...  11.8 us
    all_gather x1, blocking collectives, per_device(): packed = lax.all_gather(packed, 'box', axis=0, tiled=True)  11.3 us
    pallas_call x1, Pallas kernels, per_device(): pl.pallas_call(functools.partial(early_kernel, boxes, slabs, n0, x0, rim)...  9.06 us
    all_gather x1, blocking collectives, per_device(): s3 = lax.all_gather(s3, 'box', axis=0)  6.27 us
    all_to_all x1, starting transfers between devices, per_device(): s2 = lax.all_to_all(copies, 'gz', split_axis=0, concat_axis=0, tiled=True)  5.29 us
  transfers between devices with their start and end apart: 9, of which 4 were waited for; matrix products, arithmetic and copies ran while one was open for 0% of the time, Pallas kernels for 10%

profile of v1, /device:TPU:19, one launch (start us, length us, event | category | flops | bytes accessed | tf_op | source)
XLA Modules:
  0.0 124.6 jit_solution(1772823053345178169)
XLA Ops:
  0.0 3.4 %pack.1 = (f32[128,128]{1,0:T(8,128)S(1)}, f32[8,32,512]{2,1,0:T(8,128)S(1)}, f32[8,32,512]{2,1,0:T(8,128)S(1)}, f32[2,128,512]{2,1,0:T(8,128)}, f32[2,128,512]{2,1,0:T(8,128)}) custom-call(s32[4,64]{1,0:T(4,128)} %bitcast.9, f32[16,16,256]{2,1,0:T(8,128)} %fine.1, f32[16,16,128]{2,1,0:T(8,128)} %flux.1, f32[8,128,512]{2,1,0:T(8,128)} %coarse.3), custom_call_target="tpu_custom_call" | custom-call | flops 10000000 | bytes 1000000 | tf_op jit(solution)/shard_map/pack/pallas_call | solution.py:727
  3.4 3.7 %collective-permute-start = (f32[8,32,512]{2,1,0:T(8,128)S(1)}, f32[8,32,512]{2,1,0:T(8,128)S(1)}, u32[]{:S(2)}, u32[]{:S(2)}) collective-permute-start(f32[8,32,512]{2,1,0:T(8,128)S(1)} %get-tuple-element.22), channel_id=1, source_target_pairs={{0,8},{8,16},{16,24},{1,9},{9,17},{17,25},{2,10},{10,18},{18,26},{... | collective-permute-start | bytes 1572872 | tf_op jit(solution)/shard_map/ppermute | solution.py:713
  7.1 1.9 %collective-permute-start.1 = (f32[8,32,512]{2,1,0:T(8,128)S(1)}, f32[8,32,512]{2,1,0:T(8,128)S(1)}, u32[]{:S(2)}, u32[]{:S(2)}) collective-permute-start(f32[8,32,512]{2,1,0:T(8,128)S(1)} %get-tuple-element.23), channel_id=1, source_target_pairs={{8,0},{16,8},{24,16},{9,1},{17,9},{25,17},{10,2},{18,10},{26,18},{... | collective-permute-start | bytes 1572872 | tf_op jit(solution)/shard_map/ppermute | solution.py:713
  9.1 11.3 %all_gather.9.packed = f32[512,128]{1,0:T(8,128)S(1)} all-gather(f32[128,128]{1,0:T(8,128)S(1)} %get-tuple-element.24), channel_id=1, replica_groups=mesh['box'=4,'gz'=8] {'box'}, dimensions={0}, use_global_device_ids=true | all-gather | bytes 327680 | tf_op jit(solution)/shard_map/all_gather | solution.py:752
  20.4 0.0 collective-permute-done.x_low
  20.4 0.0 collective-permute-done.1.x_high
  20.4 11.8 %down.1 = (f32[8,4,144,128]{3,2,1,0:T(8,128)}, f32[6,2,80,128]{3,2,1,0:T(8,128)S(1)}, f32[6,1,48,128]{3,2,1,0:T(8,128)S(1)}, f32[352,128]{1,0:T(8,128)S(1)}, f32...) custom-call(s32[3,64]{1,0:T(4,128)} %bitcast.7, f32[8,128,512]{2,1,0:T(8,128)} %coarse.3, ...), custom_call_target="tpu_custom_call" | custom-call | flops 30000000 | bytes 10000000 | tf_op jit(solution)/shard_map/down/pallas_call | solution.py:757
  32.2 3.2 %collective-permute-start.2 = (f32[352,128]{1,0:T(8,128)S(1)}, f32[352,128]{1,0:T(8,128)S(1)}, u32[]{:S(2)}, u32[]{:S(2)}) collective-permute-start(f32[352,128]{1,0:T(8,128)S(1)} %get-tuple-element.26), channel_id=1, source_target_pairs={{0,1},{1,2},{2,3},{3,4},{4,5},{5,6},{6,7},{8,9},{9,10},{10,11},{11... | collective-permute-start | bytes 540680 | tf_op jit(solution)/shard_map/ppermute | solution.py:713
  35.4 2.1 %collective-permute-start.3 = (f32[352,128]{1,0:T(8,128)S(1)}, f32[352,128]{1,0:T(8,128)S(1)}, u32[]{:S(2)}, u32[]{:S(2)}) collective-permute-start(f32[352,128]{1,0:T(8,128)S(1)} %get-tuple-element.27), channel_id=1, source_target_pairs={{1,0},{2,1},{3,2},{4,3},{5,4},{6,5},{7,6},{9,8},{10,9},{11,10},{12... | collective-permute-start | bytes 540680 | tf_op jit(solution)/shard_map/ppermute | solution.py:713
  37.5 2.3 %collective-permute-done.2.below = f32[352,128]{1,0:T(8,128)S(1)} collective-permute-done((f32[352,128]{1,0:T(8,128)S(1)}, f32[352,128]{1,0:T(8,128)S(1)}, u32[]{:S(2)}, u32[]{:S(2)}) %collective-permute-start.2) | collective-permute-done | bytes 180256 | tf_op jit(solution)/shard_map/ppermute | solution.py:713
  39.8 4.4 %collective-permute-done.3.above = f32[352,128]{1,0:T(8,128)S(1)} collective-permute-done((f32[352,128]{1,0:T(8,128)S(1)}, f32[352,128]{1,0:T(8,128)S(1)}, u32[]{:S(2)}, u32[]{:S(2)}) %collective-permute-start.3) | collective-permute-done | bytes 180256 | tf_op jit(solution)/shard_map/ppermute | solution.py:713
  44.2 0.8 total.1
  45.0 5.3 %all-to-all-start = ((f32[8,96,128]{2,1,0:T(8,128)}), f32[8,96,128]{2,1,0:T(8,128)S(1)}, u32[]{:S(2)}, u32[]{:S(2)}) async-start(f32[8,96,128]{2,1,0:T(8,128)} %total.1), calls=%async_computation | async-start | bytes 786432 | tf_op jit(solution)/shard_map/all_to_all | solution.py:798
  50.3 3.1 %collective-permute-start.6 = (f32[2,128,512]{2,1,0:T(8,128)}, f32[2,128,512]{2,1,0:T(8,128)S(1)}, u32[]{:S(2)}, u32[]{:S(2)}) collective-permute-start(f32[2,128,512]{2,1,0:T(8,128)} %get-tuple-element.35), channel_id=1, source_target_pairs={{0,1},{1,2},{2,3},{3,4},{4,5},{5,6},{6,7},{8,9},{9,10},{10,11},{11... | collective-permute-start | bytes 1572872 | tf_op jit(solution)/shard_map/ppermute | solution.py:713
  53.3 2.2 %collective-permute-start.7 = (f32[2,128,512]{2,1,0:T(8,128)}, f32[2,128,512]{2,1,0:T(8,128)S(1)}, u32[]{:S(2)}, u32[]{:S(2)}) collective-permute-start(f32[2,128,512]{2,1,0:T(8,128)} %get-tuple-element.36), channel_id=1, source_target_pairs={{1,0},{2,1},{3,2},{4,3},{5,4},{6,5},{7,6},{9,8},{10,9},{11,10},{12... | collective-permute-start | bytes 1572872 | tf_op jit(solution)/shard_map/ppermute | solution.py:713
  55.5 0.1 join.1
  55.7 4.0 %collective-permute-start.4 = (f32[1120,128]{1,0:T(8,128)S(1)}, f32[1120,128]{1,0:T(8,128)S(1)}, u32[]{:S(2)}, u32[]{:S(2)}) collective-permute-start(f32[1120,128]{1,0:T(8,128)S(1)} %get-tuple-element.32), channel_id=1, source_target_pairs={{0,1},{1,2},{2,3},{3,4},{4,5},{5,6},{6,7},{8,9},{9,10},{10,11},{11... | collective-permute-start | bytes 1720328 | tf_op jit(solution)/shard_map/ppermute | solution.py:713
  59.7 1.9 %collective-permute-start.5 = (f32[1120,128]{1,0:T(8,128)S(1)}, f32[1120,128]{1,0:T(8,128)S(1)}, u32[]{:S(2)}, u32[]{:S(2)}) collective-permute-start(f32[1120,128]{1,0:T(8,128)S(1)} %get-tuple-element.33), channel_id=1, source_target_pairs={{1,0},{2,1},{3,2},{4,3},{5,4},{6,5},{7,6},{9,8},{10,9},{11,10},{12... | collective-permute-start | bytes 1720328 | tf_op jit(solution)/shard_map/ppermute | solution.py:713
  61.6 28.6 %collective-permute-done.6.z_below = f32[2,128,512]{2,1,0:T(8,128)S(1)} collective-permute-done((f32[2,128,512]{2,1,0:T(8,128)}, f32[2,128,512]{2,1,0:T(8,128)S(1)}, u32[]{:S(2)}, u32[]{:S(2)}) %collective-permute-start.6) | collective-permute-done | bytes 524320 | tf_op jit(solution)/shard_map/ppermute | solution.py:713
  90.2 0.0 copy-start
  90.2 2.2 %collective-permute-done.7.z_above = f32[2,128,512]{2,1,0:T(8,128)S(1)} collective-permute-done((f32[2,128,512]{2,1,0:T(8,128)}, f32[2,128,512]{2,1,0:T(8,128)S(1)}, u32[]{:S(2)}, u32[]{:S(2)}) %collective-permute-start.7) | collective-permute-done | bytes 524320 | tf_op jit(solution)/shard_map/ppermute | solution.py:713
  92.4 0.0 copy-start.1
  92.4 0.0 copy-done
  92.4 0.8 copy-done.1
  93.2 9.1 %early.1 = (f32[10,4,160,128]{3,2,1,0:T(8,128)}, f32[12,4,160,128]{3,2,1,0:T(8,128)}) custom-call(s32[3,64]{1,0:T(4,128)} %bitcast.8, f32[8,4,144,128]{3,2,1,0:T(8,128)} %get-tuple-element.34.f_own, f32[2,128,512]{2,1,0:T(8,128)} %copy-done, f32[2,128,512]{2,1,0:T(8,128)} %copy-done.1, f32[352,128]{1,0:T(8,128)S(1)} %collective-permute-done.2.below, ...), custom_call_target="tpu_custom_call" | custom-call | flops 20000000 | bytes 10000000 | tf_op jit(solution)/shard_map/early/pallas_call | solution.py:814
  102.2 0.0 all-to-all-done
  102.2 3.4 %third.1 = f32[4,16,128]{2,1,0:T(8,128)S(1)} custom-call(f32[16,48,128]{2,1,0:T(8,128)S(1)} %bitcast.4), custom_call_target="tpu_custom_call" | custom-call | flops 1000000 | bytes 1000000 | tf_op jit(solution)/shard_map/third/pallas_call | solution.py:836
  105.6 6.3 %all-gather = f32[16,16,128]{2,1,0:T(8,128)S(1)} all-gather(f32[4,16,128]{2,1,0:T(8,128)S(1)} %third.1), channel_id=2, replica_groups=mesh['box'=4,'gz'=8] {'box'}, dimensions={0}, use_global_device_ids=true | all-gather | bytes 163840 | tf_op jit(solution)/shard_map/all_gather | solution.py:846
  111.9 0.0 collective-permute-done.4.below
  111.9 0.0 collective-permute-done.5.above
  111.9 12.7 %tail.1 = f32[8,128,512]{2,1,0:T(8,128)} custom-call(f32[4,4,16,128]{3,2,1,0:T(8,128)S(1)} %bitcast.6, f32[16,48,128]{2,1,0:T(8,128)S(1)} %bitcast.5, f32[4,2,80,128]{3,2,1,0:T(8,128)S(1)} %get-tuple-element.31.s1, f32[1120,128]{1,0:T(8,128)S(1)} %collective-permute-done.4.below, f32[1120,128]{1,0:T(8,128)S(1)} %collective-permute-done.5.above, ...), custom_call_target="tpu_custom_call" | custom-call | flops 40000000 | bytes 10000000 | tf_op jit(solution)/shard_map/tail/pallas_call | solution.py:848
Async XLA Ops:
  3.4 17.0 %collective-permute-start = (f32[8,32,512]{2,1,0:T(8,128)S(1)}, f32[8,32,512]{2,1,0:T(8,128)S(1)}, u32[]{:S(2)}, u32[]{:S(2)}) collective-permute-start(f32[8,32,512]{2,1,0:T(8,128)S(1)} %get-tuple-element.22), channel_id=1, source_target_pairs={{0,8},{8,16},{16,24},{1,9},{9,17},{17,25},{2,10},{10,18},{18,26},{... | collective-permute-start | bytes 1572872 | tf_op jit(solution)/shard_map/ppermute | solution.py:713
  7.1 13.3 %collective-permute-start.1 = (f32[8,32,512]{2,1,0:T(8,128)S(1)}, f32[8,32,512]{2,1,0:T(8,128)S(1)}, u32[]{:S(2)}, u32[]{:S(2)}) collective-permute-start(f32[8,32,512]{2,1,0:T(8,128)S(1)} %get-tuple-element.23), channel_id=1, source_target_pairs={{8,0},{16,8},{24,16},{9,1},{17,9},{25,17},{10,2},{18,10},{26,18},{... | collective-permute-start | bytes 1572872 | tf_op jit(solution)/shard_map/ppermute | solution.py:713
  32.2 7.6 %collective-permute-start.2 = (f32[352,128]{1,0:T(8,128)S(1)}, f32[352,128]{1,0:T(8,128)S(1)}, u32[]{:S(2)}, u32[]{:S(2)}) collective-permute-start(f32[352,128]{1,0:T(8,128)S(1)} %get-tuple-element.26), channel_id=1, source_target_pairs={{0,1},{1,2},{2,3},{3,4},{4,5},{5,6},{6,7},{8,9},{9,10},{10,11},{11... | collective-permute-start | bytes 540680 | tf_op jit(solution)/shard_map/ppermute | solution.py:713
  35.4 8.8 %collective-permute-start.3 = (f32[352,128]{1,0:T(8,128)S(1)}, f32[352,128]{1,0:T(8,128)S(1)}, u32[]{:S(2)}, u32[]{:S(2)}) collective-permute-start(f32[352,128]{1,0:T(8,128)S(1)} %get-tuple-element.27), channel_id=1, source_target_pairs={{1,0},{2,1},{3,2},{4,3},{5,4},{6,5},{7,6},{9,8},{10,9},{11,10},{12... | collective-permute-start | bytes 540680 | tf_op jit(solution)/shard_map/ppermute | solution.py:713
  45.0 57.3 %all-to-all-start = ((f32[8,96,128]{2,1,0:T(8,128)}), f32[8,96,128]{2,1,0:T(8,128)S(1)}, u32[]{:S(2)}, u32[]{:S(2)}) async-start(f32[8,96,128]{2,1,0:T(8,128)} %total.1), calls=%async_computation | async-start | bytes 786432 | tf_op jit(solution)/shard_map/all_to_all | solution.py:798
  50.3 39.9 %collective-permute-start.6 = (f32[2,128,512]{2,1,0:T(8,128)}, f32[2,128,512]{2,1,0:T(8,128)S(1)}, u32[]{:S(2)}, u32[]{:S(2)}) collective-permute-start(f32[2,128,512]{2,1,0:T(8,128)} %get-tuple-element.35), channel_id=1, source_target_pairs={{0,1},{1,2},{2,3},{3,4},{4,5},{5,6},{6,7},{8,9},{9,10},{10,11},{11... | collective-permute-start | bytes 1572872 | tf_op jit(solution)/shard_map/ppermute | solution.py:713
  53.3 39.0 %collective-permute-start.7 = (f32[2,128,512]{2,1,0:T(8,128)}, f32[2,128,512]{2,1,0:T(8,128)S(1)}, u32[]{:S(2)}, u32[]{:S(2)}) collective-permute-start(f32[2,128,512]{2,1,0:T(8,128)} %get-tuple-element.36), channel_id=1, source_target_pairs={{1,0},{2,1},{3,2},{4,3},{5,4},{6,5},{7,6},{9,8},{10,9},{11,10},{12... | collective-permute-start | bytes 1572872 | tf_op jit(solution)/shard_map/ppermute | solution.py:713
  55.7 56.2 %collective-permute-start.4 = (f32[1120,128]{1,0:T(8,128)S(1)}, f32[1120,128]{1,0:T(8,128)S(1)}, u32[]{:S(2)}, u32[]{:S(2)}) collective-permute-start(f32[1120,128]{1,0:T(8,128)S(1)} %get-tuple-element.32), channel_id=1, source_target_pairs={{0,1},{1,2},{2,3},{3,4},{4,5},{5,6},{6,7},{8,9},{9,10},{10,11},{11... | collective-permute-start | bytes 1720328 | tf_op jit(solution)/shard_map/ppermute | solution.py:713
  59.7 52.2 %collective-permute-start.5 = (f32[1120,128]{1,0:T(8,128)S(1)}, f32[1120,128]{1,0:T(8,128)S(1)}, u32[]{:S(2)}, u32[]{:S(2)}) collective-permute-start(f32[1120,128]{1,0:T(8,128)S(1)} %get-tuple-element.33), channel_id=1, source_target_pairs={{1,0},{2,1},{3,2},{4,3},{5,4},{6,5},{7,6},{9,8},{10,9},{11,10},{12... | collective-permute-start | bytes 1720328 | tf_op jit(solution)/shard_map/ppermute | solution.py:713
  90.2 2.2 %copy-start = (f32[2,128,512]{2,1,0:T(8,128)}, f32[2,128,512]{2,1,0:T(8,128)S(1)}, u32[]{:S(2)}) copy-start(f32[2,128,512]{2,1,0:T(8,128)S(1)} %collective-permute-done.6.z_below) | copy-start | bytes 1572868
  92.4 0.8 copy-start.1

commit v2 on v1

--- a/solution.py
+++ b/solution.py
@@ -239,7 +239,9 @@
     return copies
 
 
-def pack_kernel(mask, fine, flux, coarse, out, x_first, x_last, z_first, z_last, fine_s, flux_s, sem, edge_sem):
+def pack_kernel(
+    mask_in, fine, flux, coarse, out, x_first, x_last, z_first, z_last, mask, fine_s, flux_s, sem, edge_sem
+):
     patches, fine_z = fine.shape[0], fine.shape[1]
     n0 = fine_z // 2
     blocks = fine_s.shape[0]
@@ -248,6 +250,7 @@
         for b in range(blocks)
     ]
     copies.append(pltpu.make_async_copy(flux, flux_s, sem.at[blocks]))
+    copies.append(pltpu.make_async_copy(mask_in, mask, sem.at[blocks + 1]))
     n, x = coarse.shape[0], coarse.shape[1]
     cuts = [
         pltpu.make_async_copy(coarse.at[pl.ds(n - 2, 2)], z_last, edge_sem.at[0]),
@@ -331,8 +334,8 @@
 def down_kernel(
     boxes, slabs, n0, x0,
     box_list, coarse, x_low, x_high, packed,
-    f_own, c1, c2, up, down, third_up, third_down,
-    fb, vb, g1, v1, summed0, summed1, found, owned, sem, out_sem,
+    f_own, v_own, c1, c2, up, down, third_up, third_down,
+    fb, vb, g1, v1, summed0, summed1, patches, found, owned, sem, out_sem,
 ):
     edges = Edges(boxes, slabs)
     rows0, rows1, rows2 = x0 + 2 * HX, x0 // 2 + HX, x0 // 4 + HX // 2
@@ -342,8 +345,11 @@
         + block_copies(coarse, fb, (2, n0), 8 + HX, x0, sem.at[1])
         + block_copies(x_high, fb, (2, n0), 8 + HX + x0, HX, sem.at[2])
     )
+    fetch = pltpu.make_async_copy(box_list, patches, sem.at[3])
+    fetch.start()
     for copy in copies:
         copy.start()
+    fetch.wait()
 
     def near_row(owner, x):
         row = (owner - edges.box) * x0 + x - 4 + HX
@@ -352,8 +358,8 @@
     def own_row(owner, x):
         return x, owner == edges.box
 
-    near_count = listed(box_list, near_row, found)
-    own_count = listed(box_list, own_row, owned)
+    near_count = listed(patches, near_row, found)
+    own_count = listed(patches, own_row, owned)
     for copy in copies:
         copy.wait()
     tiles = Tiles()
@@ -366,10 +372,12 @@
     lax.fori_loop(0, near_count, lambda index, carry: place(index) or carry, 0)
 
     inner = pl.ds(8 + HX - HU, x0 + 2 * HU)
-    out_copy = pltpu.make_async_copy(fb.at[pl.ds(2, n0), :, inner, :], f_own, out_sem)
-    out_copy.start()
+    f_copy = pltpu.make_async_copy(fb.at[pl.ds(2, n0), :, inner, :], f_own, out_sem.at[0])
+    f_copy.start()
 
     relax(vb, 3, (-1, n0 + 1), fb, 2, rows0, HX, edges, n0, s_planes=(0, n0), unroll=2)
+    v_copy = pltpu.make_async_copy(vb.at[pl.ds(4, n0 - 2), :, inner, :], v_own, out_sem.at[1])
+    v_copy.start()
 
     h1 = HX // 2
 
@@ -427,7 +435,8 @@
             down[pl.ds(rim + z * slots + slot, 1), :] = packed[pl.ds(patch * n0 + z, 1), :]
 
     lax.fori_loop(0, own_count, lambda index, carry: keep(index) or carry, 0)
-    out_copy.wait()
+    f_copy.wait()
+    v_copy.wait()
 
 
 def total_kernel(c2, below, above, copies):
@@ -483,10 +492,13 @@
         restrict(fb, 1, vb, 1, (quarter * part, quarter * (part + 1)), rows, summed, store)
 
 
-def coarse_levels(
-    edges, boxes, slabs, s3, s2, s1, below, above, e1,
-    sc, va3, vb3, e3p, f2, v2a, v2b, e2p, f1, v1a, v1b,
+def middle_kernel(
+    boxes, slabs,
+    s3, s2,
+    e2p,
+    sc, va3, vb3, e3p, f2, v2a, v2b,
 ):
+    edges = Edges(boxes, slabs)
     slab = edges.slab
     half, rows3 = sc.shape[0], sc.shape[2] - 16
     own3 = s3.shape[2]
@@ -559,7 +571,6 @@
     relax(v2b, 5, (-3, n2 + 3), f2, 5, rows2, h2, edges, n2, old=v2a, ooff=5, chunk=32)
     relax(v2a, 5, (-2, n2 + 2), f2, 5, rows2, h2, edges, n2, old=v2b, ooff=5, chunk=32)
 
-    n1, rows1 = s1.shape[0], s1.shape[2]
     cut = h2 - HU // 2
     matrix2 = copy_matrix(LANES)
     for k in range(-2, n2 + 2):
@@ -568,6 +579,10 @@
             part = value[:, LANES * b : LANES * (b + 1)]
             e2p[k + 2, b, pl.ds(0, rows2 - 2 * cut, stride=2), :] = part
             e2p[k + 2, b, pl.ds(1, rows2 - 2 * cut, stride=2), :] = part
+
+
+def first_level(edges, s1, below, above, e2p, e1, f1, v1a, v1b):
+    n1, rows1 = s1.shape[0], s1.shape[2]
     near = rows1 - HU
     inner = slice(8 + HU // 2, 8 + HU // 2 + near)
     for b in range(f1.shape[1]):
@@ -589,23 +604,29 @@
 def early_kernel(
     boxes, slabs, n0, x0, rim,
     box_list, f_own, z_below, z_above, below, above,
-    f_out, v_out,
-    fb, va, found, sem, out_sem,
+    f_rim, v_rim,
+    fb, va, patches, found, sem, out_sem,
 ):
     edges = Edges(boxes, slabs)
     rows = x0 + 2 * HU
+    fetch = pltpu.make_async_copy(box_list, patches, sem.at[4])
     copies = (
-        [pltpu.make_async_copy(f_own, fb.at[pl.ds(2, n0), :, pl.ds(8, rows), :], sem.at[0])]
+        [
+            pltpu.make_async_copy(f_own.at[pl.ds(0, 2)], fb.at[pl.ds(2, 2), :, pl.ds(8, rows), :], sem.at[0]),
+            pltpu.make_async_copy(f_own.at[pl.ds(n0 - 2, 2)], fb.at[pl.ds(4, 2), :, pl.ds(8, rows), :], sem.at[3]),
+        ]
         + block_copies(z_below, fb, (0, 2), 8 + HU, x0, sem.at[1])
-        + block_copies(z_above, fb, (2 + n0, 2), 8 + HU, x0, sem.at[2])
+        + block_copies(z_above, fb, (6, 2), 8 + HU, x0, sem.at[2])
     )
+    fetch.start()
     for copy in copies:
         copy.start()
+    fetch.wait()
 
     def own_row(owner, x):
         return x - 4 + HU + 8, owner == edges.box
 
-    count = listed(box_list, own_row, found)
+    count = listed(patches, own_row, found)
     packed = rim + 16 * fb.shape[1]
     slots = (below.shape[0] - packed) // 2
     for copy in copies:
@@ -613,44 +634,55 @@
     for z in range(2):
         for b in range(fb.shape[1]):
             at = rim + 8 * (fb.shape[1] * z + b)
-            for plane, message in ((z, below), (2 + n0 + z, above)):
+            for plane, message in ((z, below), (6 + z, above)):
                 fb[plane, b, 5 + HU : 8 + HU, :] = message[at : at + 3]
                 fb[plane, b, 8 + HU + x0 : 11 + HU + x0, :] = message[at + 3 : at + 6]
     tiles = Tiles()
 
     def place(slot):
-        lines = [(z, below, z) for z in range(2)] + [(2 + n0 + z, above, z) for z in range(2)]
+        lines = [(z, below, z) for z in range(2)] + [(6 + z, above, z) for z in range(2)]
         lines = [(plane, message[pl.ds(packed + z * slots + slot, 1), :]) for plane, message, z in lines]
         tiles.put(fb, found[0, slot], found[1, slot], lines)
 
     lax.fori_loop(0, count, lambda index, carry: place(index) or carry, 0)
-    f_copy = pltpu.make_async_copy(fb.at[pl.ds(1, n0 + 2)], f_out, out_sem.at[0])
-    f_copy.start()
-    relax(va, 2, (-2, n0 + 2), fb, 2, rows, HU, edges, n0, s_planes=(-2, n0 + 2), unroll=2)
-    v_copy = pltpu.make_async_copy(va, v_out, out_sem.at[1])
-    v_copy.start()
-    f_copy.wait()
-    v_copy.wait()
+    outs = [
+        pltpu.make_async_copy(fb.at[pl.ds(1, 1)], f_rim.at[pl.ds(0, 1)], out_sem.at[0]),
+        pltpu.make_async_copy(fb.at[pl.ds(6, 1)], f_rim.at[pl.ds(1, 1)], out_sem.at[1]),
+        pltpu.make_async_copy(va.at[pl.ds(0, 3)], v_rim.at[pl.ds(0, 3)], out_sem.at[2]),
+        pltpu.make_async_copy(va.at[pl.ds(3, 3)], v_rim.at[pl.ds(3, 3)], out_sem.at[3]),
+    ]
+    outs[0].start()
+    outs[1].start()
+    relax(va, 2, (-2, 1), fb, 2, rows, HU, edges, n0, s_planes=(-2, n0), unroll=2)
+    outs[2].start()
+    relax(va, 4 - n0, (n0 - 1, n0 + 2), fb, 6 - n0, rows, HU, edges, n0, s_planes=(0, n0 + 2), unroll=2)
+    outs[3].start()
+    for out in outs:
+        out.wait()
 
 
 def tail_kernel(
     boxes, slabs, n0, x0,
-    s3, s2, s1, below, above, f_in, v_in,
+    e2p, s1, below, above, f_own, f_rim, v_own, v_rim,
     out,
-    sc, va3, vb3, e3p, f2, v2a, v2b, e2p, f1, v1a, v1b, e1,
+    f1, v1a, v1b, e1,
     fb, va, vb, ob, sem, out_sem,
 ):
-    f_copy = pltpu.make_async_copy(f_in, fb, sem.at[0])
-    v_copy = pltpu.make_async_copy(v_in, va.at[pl.ds(1, n0 + 4)], sem.at[1])
-    f_copy.start()
-    v_copy.start()
+    inner = pl.ds(8, x0 + 2 * HU)
+    copies = [
+        pltpu.make_async_copy(v_own, va.at[pl.ds(4, n0 - 2), :, inner, :], sem.at[0]),
+        pltpu.make_async_copy(v_rim.at[pl.ds(0, 3)], va.at[pl.ds(1, 3)], sem.at[1]),
+        pltpu.make_async_copy(v_rim.at[pl.ds(3, 3)], va.at[pl.ds(n0 + 2, 3)], sem.at[2]),
+        pltpu.make_async_copy(f_own, fb.at[pl.ds(1, n0), :, inner, :], sem.at[3]),
+        pltpu.make_async_copy(f_rim.at[pl.ds(0, 1)], fb.at[pl.ds(0, 1)], sem.at[4]),
+        pltpu.make_async_copy(f_rim.at[pl.ds(1, 1)], fb.at[pl.ds(n0 + 1, 1)], sem.at[5]),
+    ]
+    for copy in copies:
+        copy.start()
     edges = Edges(boxes, slabs)
-    coarse_levels(
-        edges, boxes, slabs, s3, s2, s1, below, above, e1,
-        sc, va3, vb3, e3p, f2, v2a, v2b, e2p, f1, v1a, v1b,
-    )
-    f_copy.wait()
-    v_copy.wait()
+    first_level(edges, s1, below, above, e2p, e1, f1, v1a, v1b)
+    for copy in copies:
+        copy.wait()
     rows = x0 + 2 * HU
     matrix = copy_matrix(LANES)
     cut = HU // 2
@@ -722,6 +754,8 @@
     rows0, rows1, rows2 = x0 + 2 * HX, x0 // 2 + HX, x0 // 4 + HX // 2
     up_rows0, up_rows1 = x0 + 2 * HU, x0 // 2 + 2 * HU
     dma = pltpu.SemaphoreType.DMA
+    hbm = pltpu.MemorySpace.HBM
+    table = pltpu.SMEM((3, box_list.shape[0]), I32)
 
     fine_blocks = fine_lanes // LANES
     packed, x_first, x_last, z_first, z_last = pl.pallas_call(
@@ -734,12 +768,13 @@
             shape_of(2, x0, y0),
             shape_of(2, x0, y0),
         ),
-        in_specs=[SM, HBM, HBM, HBM],
+        in_specs=[HBM] * 4,
         out_specs=(VM,) * 5,
         scratch_shapes=[
+            pltpu.SMEM(cf_mask.shape[::-1], I32),
             scratch(fine_blocks, patches, fine_z, LANES),
             scratch(patches, fine_z, LANES),
-            dma((fine_blocks + 1,)),
+            dma((fine_blocks + 2,)),
             dma((4,)),
         ],
         compiler_params=limit(4),
@@ -754,11 +789,12 @@
     slots = boxes * max(2, patches // 4)
     rim = 2 * rows2 + b1 * up_rows1
     message = rim + 2 * (8 * b0 + slots)
-    f_own, c1, c2, up, down, third_up, third_down = pl.pallas_call(
+    f_own, v_own, c1, c2, up, down, third_up, third_down = pl.pallas_call(
         functools.partial(down_kernel, boxes, slabs, n0, x0),
         name="down",
         out_shape=(
-            pltpu.MemorySpace.HBM((n0, b0, up_rows0, LANES), F32),
+            hbm((n0, b0, up_rows0, LANES), F32),
+            hbm((n0 - 2, b0, up_rows0, LANES), F32),
             shape_of(n1 + 2, b1, up_rows1, LANES),
             shape_of(n2 + 4, 1, rows2, LANES),
             shape_of(message, LANES),
@@ -766,8 +802,8 @@
             shape_of(b0 * (x0 + HU), LANES),
             shape_of(b0 * (x0 + HU), LANES),
         ),
-        in_specs=[SM, HBM, HBM, HBM, VM],
-        out_specs=(HBM,) + (VM,) * 6,
+        in_specs=[HBM] * 4 + [VM],
+        out_specs=(HBM,) * 2 + (VM,) * 6,
         scratch_shapes=[
             scratch(n0 + 4, b0, rows0 + 16, LANES),
             scratch(n0 + 6, b0, rows0 + 16, LANES),
@@ -775,10 +811,11 @@
             scratch(n1 + 10, b1, rows1 + 16, LANES),
             scratch(b0 // 2, rows1, 2 * LANES),
             scratch(max(1, b1 // 2), rows2, min(2, b1) * LANES),
-            pltpu.SMEM((3, box_list.shape[0]), I32),
-            pltpu.SMEM((3, box_list.shape[0]), I32),
-            dma((3,)),
-            dma(()),
+            table,
+            table,
+            table,
+            dma((4,)),
+            dma((2,)),
         ],
         compiler_params=limit(20),
         cost_estimate=cost(3 * 10**7, 10**7),
@@ -810,24 +847,22 @@
     below = shift_by(up, "gz", 1)
     above = shift_by(down, "gz", -1)
 
-    hbm = pltpu.MemorySpace.HBM
-    f_wide, v_wide = pl.pallas_call(
+    up_wide = up_rows0 + 16
+    f_rim, v_rim = pl.pallas_call(
         functools.partial(early_kernel, boxes, slabs, n0, x0, rim),
         name="early",
-        out_shape=(
-            hbm((n0 + 2, b0, up_rows0 + 16, LANES), F32),
-            hbm((n0 + 4, b0, up_rows0 + 16, LANES), F32),
-        ),
-        in_specs=[SM, HBM, HBM, HBM, VM, VM],
+        out_shape=(hbm((2, b0, up_wide, LANES), F32), hbm((6, b0, up_wide, LANES), F32)),
+        in_specs=[HBM, HBM, HBM, HBM, VM, VM],
         out_specs=(HBM, HBM),
         scratch_shapes=[
-            scratch(n0 + 4, b0, up_rows0 + 16, LANES),
-            scratch(n0 + 4, b0, up_rows0 + 16, LANES),
-            pltpu.SMEM((3, box_list.shape[0]), I32),
-            dma((3,)),
-            dma((2,)),
+            scratch(8, b0, up_wide, LANES),
+            scratch(6, b0, up_wide, LANES),
+            table,
+            table,
+            dma((5,)),
+            dma((4,)),
         ],
-        compiler_params=limit(14),
+        compiler_params=limit(10),
         cost_estimate=cost(2 * 10**7, 10**7),
     )(in_hbm(box_list.T), in_hbm(f_own), in_hbm(z_below), in_hbm(z_above), from_below, from_above)
 
@@ -845,24 +880,32 @@
     )(s2)
     s3 = lax.all_gather(s3, "box", axis=0)
     rows3 = boxes * own3
+    e2p = pl.pallas_call(
+        functools.partial(middle_kernel, boxes, slabs),
+        name="middle",
+        out_shape=shape_of(n2 + 4, 2, up_rows1, LANES),
+        in_specs=[VM] * 2,
+        out_specs=VM,
+        scratch_shapes=[scratch(half, 1, rows3 + 16, LANES)] * 3
+        + [scratch(n2 // 2 + 4, rows2, LANES)]
+        + [scratch(n2 + 10, 1, rows2 + 16, LANES)] * 3,
+        compiler_params=limit(8),
+        cost_estimate=cost(10**7, 2 * 10**6),
+    )(s3, s2)
     return pl.pallas_call(
         functools.partial(tail_kernel, boxes, slabs, n0, x0),
         name="tail",
         out_shape=shape_of(n0, x0, y0),
-        in_specs=[VM] * 5 + [HBM, HBM],
+        in_specs=[VM] * 4 + [HBM] * 4,
         out_specs=HBM,
-        scratch_shapes=[scratch(half, 1, rows3 + 16, LANES)] * 3
-        + [scratch(n2 // 2 + 4, rows2, LANES)]
-        + [scratch(n2 + 10, 1, rows2 + 16, LANES)] * 3
-        + [scratch(n2 + 4, 2, up_rows1, LANES)]
-        + [scratch(n1 + 8, b1, up_rows1 + 16, LANES)] * 3
+        scratch_shapes=[scratch(n1 + 8, b1, up_rows1 + 16, LANES)] * 3
         + [scratch(n1 + 2, b1, up_rows1, LANES)]
         + [scratch(n0 + 2, b0, up_rows0 + 16, LANES)]
         + [scratch(n0 + 6, b0, up_rows0 + 16, LANES)] * 2
-        + [scratch(n0, b0, x0, LANES), dma((2,)), dma(())],
-        compiler_params=limit(28),
+        + [scratch(n0, b0, x0, LANES), dma((6,)), dma(())],
+        compiler_params=limit(24),
         cost_estimate=cost(4 * 10**7, 10**7),
-    )(s3, s2, s1, below, above, in_hbm(f_wide), in_hbm(v_wide))
+    )(e2p, s1, below, above, in_hbm(f_own), in_hbm(f_rim), in_hbm(v_own), in_hbm(v_rim))
 
 
 def solution(mesh):

time: 127 us -> 123 us (0.969)
  Pallas kernels: 41.3 us -> 36.9 us
    pallas_call x0 -> x1, Pallas kernels: none -> 4.46 us  [per_device(): pl.pallas_call(functools.partial(middle_kernel, boxes, slabs), name='midd...]
    pallas_call x1, Pallas kernels: 12.7 us -> 8.37 us  [per_device(): pl.pallas_call(functools.partial(tail_kernel, boxes, slabs, n0, x0), name...]
    pallas_call x1, Pallas kernels: 9.06 us -> 5.87 us  [per_device(): pl.pallas_call(functools.partial(early_kernel, boxes, slabs, n0, x0, rim)...]
  transfers between devices with their start and end apart: 9 -> 9, of which waited for: 4 -> 4; matrix products, arithmetic and copies ran while one was open for 0% -> 0% of each run, Pallas kernels for 10% -> 11%
where the time goes in v2:
time: 123 us; the launch traced here: 120 us
  waiting for transfers between devices  37.4 us (30%)
  Pallas kernels  36.9 us (30%)
  starting transfers between devices  27.4 us (22%)
  blocking collectives  17.6 us (14%)
    ppermute x8, waiting for transfers between devices, shift_by(): return lax.ppermute(array, axis, pairs)  37.4 us
    ppermute x8, starting transfers between devices, shift_by(): return lax.ppermute(array, axis, pairs)  22.1 us
    all_gather x1, blocking collectives, per_device(): packed = lax.all_gather(packed, 'box', axis=0, tiled=True)  11.3 us
    pallas_call x1, Pallas kernels, per_device(): pl.pallas_call(functools.partial(down_kernel, boxes, slabs, n0, x0), name...  11.3 us
    pallas_call x1, Pallas kernels, per_device(): pl.pallas_call(functools.partial(tail_kernel, boxes, slabs, n0, x0), name...  8.37 us
    all_gather x1, blocking collectives, per_device(): s3 = lax.all_gather(s3, 'box', axis=0)  6.27 us
    pallas_call x1, Pallas kernels, per_device(): pl.pallas_call(functools.partial(early_kernel, boxes, slabs, n0, x0, rim)...  5.87 us
    all_to_all x1, starting transfers between devices, per_device(): s2 = lax.all_to_all(copies, 'gz', split_axis=0, concat_axis=0, tiled=True)  5.29 us
  transfers between devices with their start and end apart: 9, of which 4 were waited for; matrix products, arithmetic and copies ran while one was open for 0% of the time, Pallas kernels for 11%

profile of v2, /device:TPU:19, one launch (start us, length us, event | category | flops | bytes accessed | tf_op | source)
XLA Modules:
  0.0 120.3 jit_solution(10280519284224029189)
XLA Ops:
  0.0 2.7 %pack.1 = (f32[128,128]{1,0:T(8,128)S(1)}, f32[8,32,512]{2,1,0:T(8,128)S(1)}, f32[8,32,512]{2,1,0:T(8,128)S(1)}, f32[2,128,512]{2,1,0:T(8,128)}, f32[2,128,512]{2,1,0:T(8,128)}) custom-call(s32[4,64]{1,0:T(4,128)} %bitcast.9, f32[16,16,256]{2,1,0:T(8,128)} %fine.1, f32[16,16,128]{2,1,0:T(8,128)} %flux.1, f32[8,128,512]{2,1,0:T(8,128)} %coarse.3), custom_call_target="tpu_custom_call" | custom-call | flops 10000000 | bytes 1000000 | tf_op jit(solution)/shard_map/pack/pallas_call | solution.py:761
  2.7 3.7 %collective-permute-start = (f32[8,32,512]{2,1,0:T(8,128)S(1)}, f32[8,32,512]{2,1,0:T(8,128)S(1)}, u32[]{:S(2)}, u32[]{:S(2)}) collective-permute-start(f32[8,32,512]{2,1,0:T(8,128)S(1)} %get-tuple-element.23), channel_id=1, source_target_pairs={{0,8},{8,16},{16,24},{1,9},{9,17},{17,25},{2,10},{10,18},{18,26},{... | collective-permute-start | bytes 1572872 | tf_op jit(solution)/shard_map/ppermute | solution.py:745
  6.4 1.9 %collective-permute-start.1 = (f32[8,32,512]{2,1,0:T(8,128)S(1)}, f32[8,32,512]{2,1,0:T(8,128)S(1)}, u32[]{:S(2)}, u32[]{:S(2)}) collective-permute-start(f32[8,32,512]{2,1,0:T(8,128)S(1)} %get-tuple-element.24), channel_id=1, source_target_pairs={{8,0},{16,8},{24,16},{9,1},{17,9},{25,17},{10,2},{18,10},{26,18},{... | collective-permute-start | bytes 1572872 | tf_op jit(solution)/shard_map/ppermute | solution.py:745
  8.4 11.3 %all_gather.9.packed = f32[512,128]{1,0:T(8,128)S(1)} all-gather(f32[128,128]{1,0:T(8,128)S(1)} %get-tuple-element.25), channel_id=1, replica_groups=mesh['box'=4,'gz'=8] {'box'}, dimensions={0}, use_global_device_ids=true | all-gather | bytes 327680 | tf_op jit(solution)/shard_map/all_gather | solution.py:787
  19.7 0.0 collective-permute-done.x_low
  19.7 0.0 collective-permute-done.1.x_high
  19.7 11.3 %down.1 = (f32[8,4,144,128]{3,2,1,0:T(8,128)}, f32[6,4,144,128]{3,2,1,0:T(8,128)}, f32[6,2,80,128]{3,2,1,0:T(8,128)S(1)}, f32[6,1,48,128]{3,2,1,0:T(8,128)S(1)},...) custom-call(s32[3,64]{1,0:T(4,128)} %bitcast.7, ...), custom_call_target="tpu_custom_call" | custom-call | flops 30000000 | bytes 10000000 | tf_op jit(solution)/shard_map/down/pallas_call | solution.py:792
  31.0 3.2 %collective-permute-start.2 = (f32[352,128]{1,0:T(8,128)S(1)}, f32[352,128]{1,0:T(8,128)S(1)}, u32[]{:S(2)}, u32[]{:S(2)}) collective-permute-start(f32[352,128]{1,0:T(8,128)S(1)} %get-tuple-element.27), channel_id=1, source_target_pairs={{0,1},{1,2},{2,3},{3,4},{4,5},{5,6},{6,7},{8,9},{9,10},{10,11},{11... | collective-permute-start | bytes 540680 | tf_op jit(solution)/shard_map/ppermute | solution.py:745
  34.2 2.1 %collective-permute-start.3 = (f32[352,128]{1,0:T(8,128)S(1)}, f32[352,128]{1,0:T(8,128)S(1)}, u32[]{:S(2)}, u32[]{:S(2)}) collective-permute-start(f32[352,128]{1,0:T(8,128)S(1)} %get-tuple-element.28), channel_id=1, source_target_pairs={{1,0},{2,1},{3,2},{4,3},{5,4},{6,5},{7,6},{9,8},{10,9},{11,10},{12... | collective-permute-start | bytes 540680 | tf_op jit(solution)/shard_map/ppermute | solution.py:745
  36.3 2.3 %collective-permute-done.2.below = f32[352,128]{1,0:T(8,128)S(1)} collective-permute-done((f32[352,128]{1,0:T(8,128)S(1)}, f32[352,128]{1,0:T(8,128)S(1)}, u32[]{:S(2)}, u32[]{:S(2)}) %collective-permute-start.2) | collective-permute-done | bytes 180256 | tf_op jit(solution)/shard_map/ppermute | solution.py:745
  38.6 4.4 %collective-permute-done.3.above = f32[352,128]{1,0:T(8,128)S(1)} collective-permute-done((f32[352,128]{1,0:T(8,128)S(1)}, f32[352,128]{1,0:T(8,128)S(1)}, u32[]{:S(2)}, u32[]{:S(2)}) %collective-permute-start.3) | collective-permute-done | bytes 180256 | tf_op jit(solution)/shard_map/ppermute | solution.py:745
  42.9 0.8 total.1
  43.7 5.3 %all-to-all-start = ((f32[8,96,128]{2,1,0:T(8,128)}), f32[8,96,128]{2,1,0:T(8,128)S(1)}, u32[]{:S(2)}, u32[]{:S(2)}) async-start(f32[8,96,128]{2,1,0:T(8,128)} %total.1), calls=%async_computation | async-start | bytes 786432 | tf_op jit(solution)/shard_map/all_to_all | solution.py:835
  49.0 3.1 %collective-permute-start.6 = (f32[2,128,512]{2,1,0:T(8,128)}, f32[2,128,512]{2,1,0:T(8,128)S(1)}, u32[]{:S(2)}, u32[]{:S(2)}) collective-permute-start(f32[2,128,512]{2,1,0:T(8,128)} %get-tuple-element.36), channel_id=1, source_target_pairs={{0,1},{1,2},{2,3},{3,4},{4,5},{5,6},{6,7},{8,9},{9,10},{10,11},{11... | collective-permute-start | bytes 1572872 | tf_op jit(solution)/shard_map/ppermute | solution.py:745
  52.1 2.2 %collective-permute-start.7 = (f32[2,128,512]{2,1,0:T(8,128)}, f32[2,128,512]{2,1,0:T(8,128)S(1)}, u32[]{:S(2)}, u32[]{:S(2)}) collective-permute-start(f32[2,128,512]{2,1,0:T(8,128)} %get-tuple-element.37), channel_id=1, source_target_pairs={{1,0},{2,1},{3,2},{4,3},{5,4},{6,5},{7,6},{9,8},{10,9},{11,10},{12... | collective-permute-start | bytes 1572872 | tf_op jit(solution)/shard_map/ppermute | solution.py:745
  54.3 0.1 join.1
  54.4 4.0 %collective-permute-start.4 = (f32[1120,128]{1,0:T(8,128)S(1)}, f32[1120,128]{1,0:T(8,128)S(1)}, u32[]{:S(2)}, u32[]{:S(2)}) collective-permute-start(f32[1120,128]{1,0:T(8,128)S(1)} %get-tuple-element.33), channel_id=1, source_target_pairs={{0,1},{1,2},{2,3},{3,4},{4,5},{5,6},{6,7},{8,9},{9,10},{10,11},{11... | collective-permute-start | bytes 1720328 | tf_op jit(solution)/shard_map/ppermute | solution.py:745
  58.4 1.9 %collective-permute-start.5 = (f32[1120,128]{1,0:T(8,128)S(1)}, f32[1120,128]{1,0:T(8,128)S(1)}, u32[]{:S(2)}, u32[]{:S(2)}) collective-permute-start(f32[1120,128]{1,0:T(8,128)S(1)} %get-tuple-element.34), channel_id=1, source_target_pairs={{1,0},{2,1},{3,2},{4,3},{5,4},{6,5},{7,6},{9,8},{10,9},{11,10},{12... | collective-permute-start | bytes 1720328 | tf_op jit(solution)/shard_map/ppermute | solution.py:745
  60.3 28.6 %collective-permute-done.6.z_below = f32[2,128,512]{2,1,0:T(8,128)S(1)} collective-permute-done((f32[2,128,512]{2,1,0:T(8,128)}, f32[2,128,512]{2,1,0:T(8,128)S(1)}, u32[]{:S(2)}, u32[]{:S(2)}) %collective-permute-start.6) | collective-permute-done | bytes 524320 | tf_op jit(solution)/shard_map/ppermute | solution.py:745
  88.9 0.0 copy-start
  88.9 2.2 %collective-permute-done.7.z_above = f32[2,128,512]{2,1,0:T(8,128)S(1)} collective-permute-done((f32[2,128,512]{2,1,0:T(8,128)}, f32[2,128,512]{2,1,0:T(8,128)S(1)}, u32[]{:S(2)}, u32[]{:S(2)}) %collective-permute-start.7) | collective-permute-done | bytes 524320 | tf_op jit(solution)/shard_map/ppermute | solution.py:745
  91.1 0.0 copy-start.1
  91.1 0.0 copy-done
  91.1 0.8 copy-done.1
  91.9 5.9 %early.1 = (f32[2,4,160,128]{3,2,1,0:T(8,128)}, f32[6,4,160,128]{3,2,1,0:T(8,128)}) custom-call(s32[3,64]{1,0:T(4,128)} %bitcast.8, f32[8,4,144,128]{3,2,1,0:T(8,128)} %get-tuple-element.35.f_own, f32[2,128,512]{2,1,0:T(8,128)} %copy-done, f32[2,128,512]{2,1,0:T(8,128)} %copy-done.1, f32[352,128]{1,0:T(8,128)S(1)} %collective-permute-done.2.below, ...), custom_call_target="tpu_custom_call" | custom-call | flops 20000000 | bytes 10000000 | tf_op jit(solution)/shard_map/early/pallas_call | solution.py:851
  97.8 0.0 all-to-all-done
  97.8 3.4 %third.1 = f32[4,16,128]{2,1,0:T(8,128)S(1)} custom-call(f32[16,48,128]{2,1,0:T(8,128)S(1)} %bitcast.4), custom_call_target="tpu_custom_call" | custom-call | flops 1000000 | bytes 1000000 | tf_op jit(solution)/shard_map/third/pallas_call | solution.py:871
  101.2 6.3 %all-gather = f32[16,16,128]{2,1,0:T(8,128)S(1)} all-gather(f32[4,16,128]{2,1,0:T(8,128)S(1)} %third.1), channel_id=2, replica_groups=mesh['box'=4,'gz'=8] {'box'}, dimensions={0}, use_global_device_ids=true | all-gather | bytes 163840 | tf_op jit(solution)/shard_map/all_gather | solution.py:881
  107.4 4.5 %middle.1.e2p = f32[6,2,80,128]{3,2,1,0:T(8,128)S(1)} custom-call(f32[4,4,16,128]{3,2,1,0:T(8,128)S(1)} %bitcast.6, f32[16,48,128]{2,1,0:T(8,128)S(1)} %bitcast.5), custom_call_target="tpu_custom_call" | custom-call | flops 10000000 | bytes 2000000 | tf_op jit(solution)/shard_map/middle/pallas_call | solution.py:883
  111.9 0.0 collective-permute-done.4.below
  111.9 0.0 collective-permute-done.5.above
  111.9 8.4 %tail.1 = f32[8,128,512]{2,1,0:T(8,128)} custom-call(f32[6,2,80,128]{3,2,1,0:T(8,128)S(1)} %middle.1.e2p, f32[4,2,80,128]{3,2,1,0:T(8,128)S(1)} %get-tuple-element.32.s1, f32[1120,128]{1,0:T(8,128)S(1)} %collective-permute-done.4.below, f32[1120,128]{1,0:T(8,128)S(1)} %collective-permute-done.5.above, f32[8,4,144,128]{3,2,1,0:T(8,128)} %get-tuple-element.35.f_own, ...), custom_call_target="tpu_custom_call" | custom-call | flops 40000000 | bytes 10000000 | tf_op jit(solution)/shard_map/tail/pallas_call | solution.py:895
Async XLA Ops:
  2.7 17.0 %collective-permute-start = (f32[8,32,512]{2,1,0:T(8,128)S(1)}, f32[8,32,512]{2,1,0:T(8,128)S(1)}, u32[]{:S(2)}, u32[]{:S(2)}) collective-permute-start(f32[8,32,512]{2,1,0:T(8,128)S(1)} %get-tuple-element.23), channel_id=1, source_target_pairs={{0,8},{8,16},{16,24},{1,9},{9,17},{17,25},{2,10},{10,18},{18,26},{... | collective-permute-start | bytes 1572872 | tf_op jit(solution)/shard_map/ppermute | solution.py:745
  6.4 13.3 %collective-permute-start.1 = (f32[8,32,512]{2,1,0:T(8,128)S(1)}, f32[8,32,512]{2,1,0:T(8,128)S(1)}, u32[]{:S(2)}, u32[]{:S(2)}) collective-permute-start(f32[8,32,512]{2,1,0:T(8,128)S(1)} %get-tuple-element.24), channel_id=1, source_target_pairs={{8,0},{16,8},{24,16},{9,1},{17,9},{25,17},{10,2},{18,10},{26,18},{... | collective-permute-start | bytes 1572872 | tf_op jit(solution)/shard_map/ppermute | solution.py:745
  31.0 7.6 %collective-permute-start.2 = (f32[352,128]{1,0:T(8,128)S(1)}, f32[352,128]{1,0:T(8,128)S(1)}, u32[]{:S(2)}, u32[]{:S(2)}) collective-permute-start(f32[352,128]{1,0:T(8,128)S(1)} %get-tuple-element.27), channel_id=1, source_target_pairs={{0,1},{1,2},{2,3},{3,4},{4,5},{5,6},{6,7},{8,9},{9,10},{10,11},{11... | collective-permute-start | bytes 540680 | tf_op jit(solution)/shard_map/ppermute | solution.py:745
  34.2 8.8 %collective-permute-start.3 = (f32[352,128]{1,0:T(8,128)S(1)}, f32[352,128]{1,0:T(8,128)S(1)}, u32[]{:S(2)}, u32[]{:S(2)}) collective-permute-start(f32[352,128]{1,0:T(8,128)S(1)} %get-tuple-element.28), channel_id=1, source_target_pairs={{1,0},{2,1},{3,2},{4,3},{5,4},{6,5},{7,6},{9,8},{10,9},{11,10},{12... | collective-permute-start | bytes 540680 | tf_op jit(solution)/shard_map/ppermute | solution.py:745
  43.7 54.1 %all-to-all-start = ((f32[8,96,128]{2,1,0:T(8,128)}), f32[8,96,128]{2,1,0:T(8,128)S(1)}, u32[]{:S(2)}, u32[]{:S(2)}) async-start(f32[8,96,128]{2,1,0:T(8,128)} %total.1), calls=%async_computation | async-start | bytes 786432 | tf_op jit(solution)/shard_map/all_to_all | solution.py:835
  49.0 39.9 %collective-permute-start.6 = (f32[2,128,512]{2,1,0:T(8,128)}, f32[2,128,512]{2,1,0:T(8,128)S(1)}, u32[]{:S(2)}, u32[]{:S(2)}) collective-permute-start(f32[2,128,512]{2,1,0:T(8,128)} %get-tuple-element.36), channel_id=1, source_target_pairs={{0,1},{1,2},{2,3},{3,4},{4,5},{5,6},{6,7},{8,9},{9,10},{10,11},{11... | collective-permute-start | bytes 1572872 | tf_op jit(solution)/shard_map/ppermute | solution.py:745
  52.1 39.0 %collective-permute-start.7 = (f32[2,128,512]{2,1,0:T(8,128)}, f32[2,128,512]{2,1,0:T(8,128)S(1)}, u32[]{:S(2)}, u32[]{:S(2)}) collective-permute-start(f32[2,128,512]{2,1,0:T(8,128)} %get-tuple-element.37), channel_id=1, source_target_pairs={{1,0},{2,1},{3,2},{4,3},{5,4},{6,5},{7,6},{9,8},{10,9},{11,10},{12... | collective-permute-start | bytes 1572872 | tf_op jit(solution)/shard_map/ppermute | solution.py:745
  54.4 57.5 %collective-permute-start.4 = (f32[1120,128]{1,0:T(8,128)S(1)}, f32[1120,128]{1,0:T(8,128)S(1)}, u32[]{:S(2)}, u32[]{:S(2)}) collective-permute-start(f32[1120,128]{1,0:T(8,128)S(1)} %get-tuple-element.33), channel_id=1, source_target_pairs={{0,1},{1,2},{2,3},{3,4},{4,5},{5,6},{6,7},{8,9},{9,10},{10,11},{11... | collective-permute-start | bytes 1720328 | tf_op jit(solution)/shard_map/ppermute | solution.py:745
  58.4 53.5 %collective-permute-start.5 = (f32[1120,128]{1,0:T(8,128)S(1)}, f32[1120,128]{1,0:T(8,128)S(1)}, u32[]{:S(2)}, u32[]{:S(2)}) collective-permute-start(f32[1120,128]{1,0:T(8,128)S(1)} %get-tuple-element.34), channel_id=1, source_target_pairs={{1,0},{2,1},{3,2},{4,3},{5,4},{6,5},{7,6},{9,8},{10,9},{11,10},{12... | collective-permute-start | bytes 1720328 | tf_op jit(solution)/shard_map/ppermute | solution.py:745
  88.9 2.2 %copy-start = (f32[2,128,512]{2,1,0:T(8,128)}, f32[2,128,512]{2,1,0:T(8,128)S(1)}, u32[]{:S(2)}) copy-start(f32[2,128,512]{2,1,0:T(8,128)S(1)} %collective-permute-done.6.z_below) | copy-start | bytes 1572868
  91.1 0.8 copy-start.1

commit v3 on v2

--- a/solution.py
+++ b/solution.py
@@ -158,14 +158,13 @@
         each(len(inner), lambda index: body(index + first), unroll)
 
 
-def restrict(source, soff, v, voff, pairs, rows, summed, store, chunk=8, v_planes=None, s_planes=None):
+def restrict(source, soff, v, voff, pairs, rows, summed, store, chunk=8, v_planes=None, s_planes=None, unroll=1):
     count = v.shape[1]
     width = min(2, count)
     half = rows // 2
 
     def body(index, has_v=(True,) * 4, has_s=(True,) * 2):
         low_v, low_s = 2 * index + (2 * pairs[0] + voff), 2 * index + (2 * pairs[0] + soff)
-        matrix = pair_matrix(width * LANES)
         for first in range(0, half, chunk):
             size = min(chunk, half - first)
 
@@ -195,12 +194,18 @@
                 terms += [both(v, low_v + p - 1, b) for p in (0, 3) if has_v[p]]
                 sums.append(total_of(terms))
             for b in range(count):
-                summed[b // width, first : first + size, LANES * (b % width) : LANES * (b % width + 1)] = sums[b]
-        for group in range(count // width):
-            store(index, group, 0.5 * select_dot(summed[group], matrix))
+                cut = slice(LANES * (b % width), LANES * (b % width + 1))
+                summed[index, b // width, first : first + size, cut] = sums[b]
+
+    def finish():
+        matrix = pair_matrix(width * LANES)
+        for index in range(pairs[1] - pairs[0]):
+            for group in range(count // width):
+                store(index, group, 0.5 * select_dot(summed[index, group], matrix))
 
     if v_planes is None:
-        each(pairs[1] - pairs[0], body)
+        each(pairs[1] - pairs[0], body, unroll)
+        finish()
         return
     inner = []
     for coarse in range(*pairs):
@@ -212,7 +217,8 @@
             body(coarse - pairs[0], has_v, has_s)
     if inner:
         first = inner[0] - pairs[0]
-        each(len(inner), lambda index: body(index + first))
+        each(len(inner), lambda index: body(index + first), unroll)
+    finish()
 
 
 def zero(ref, planes):
@@ -334,7 +340,7 @@
 def down_kernel(
     boxes, slabs, n0, x0,
     box_list, coarse, x_low, x_high, packed,
-    f_own, v_own, c1, c2, up, down, third_up, third_down,
+    f_own, v_own, c1, c2, up, down, late_up, late_down,
     fb, vb, g1, v1, summed0, summed1, patches, found, owned, sem, out_sem,
 ):
     edges = Edges(boxes, slabs)
@@ -392,7 +398,7 @@
         for b in range(g1.shape[1]):
             c1[plane, b] = g1[plane + 3, b, 8 + h1 - HU : 8 + rows1 - h1 + HU, :]
 
-    relax(v1, 5, (-2, n1 + 2), g1, 4, rows1, h1, edges, n1, s_planes=(-1, n1 + 1))
+    relax(v1, 5, (-2, n1 + 2), g1, 4, rows1, h1, edges, n1, s_planes=(-1, n1 + 1), unroll=2)
 
     h2 = HX // 4
 
@@ -404,20 +410,19 @@
     restrict(g1, 4, v1, 5, (-2, n2 + 2), rows1, summed1, store2, v_planes=(-2, n1 + 2), s_planes=(-1, n1 + 1))
 
     r1 = c1.shape[2]
-    for target, fine_plane, coarse_first in ((up, n1 + 1, n2 + 2), (down, 0, 0)):
+    for target, late, fine_plane, coarse_first in ((up, late_up, n1 + 1, n2 + 2), (down, late_down, 0, 0)):
         target[0:rows2] = c2[coarse_first, 0]
         target[rows2 : 2 * rows2] = c2[coarse_first + 1, 0]
         for b in range(c1.shape[1]):
-            first = 2 * rows2 + b * r1
-            target[first : first + r1] = c1[fine_plane, b]
-
-    rim = 2 * rows2 + c1.shape[1] * r1
+            late[r1 * b : r1 * (b + 1)] = c1[fine_plane, b]
+    rim = 2 * rows2
     slots = (up.shape[0] - rim) // 2 - 8 * fb.shape[1]
-    wide = third_up.shape[0] // fb.shape[1]
+    begin = c1.shape[1] * r1
+    wide = (late_up.shape[0] - begin) // fb.shape[1]
     for b in range(fb.shape[1]):
         at = slice(4 + HX, 4 + HX + wide)
-        third_up[wide * b : wide * (b + 1)] = fb[n0 - 1, b, at, :]
-        third_down[wide * b : wide * (b + 1)] = fb[4, b, at, :]
+        late_up[begin + wide * b : begin + wide * (b + 1)] = fb[n0 - 1, b, at, :]
+        late_down[begin + wide * b : begin + wide * (b + 1)] = fb[4, b, at, :]
         for z in range(2):
             first = rim + 8 * (fb.shape[1] * z + b)
             for target, plane in ((up, n0 + z), (down, 2 + z)):
@@ -452,12 +457,12 @@
             copies[slab, plane * rows2 : (plane + 1) * rows2] = value
 
 
-def join_kernel(rows2, c1, below, above, third_up, third_down, s1, up, down):
+def join_kernel(c1, below, above, s1, up, down):
     n1, r1 = s1.shape[0], c1.shape[2]
     for plane in range(n1):
         s1[plane] = c1[1 + plane]
     for b in range(s1.shape[1]):
-        first = 2 * rows2 + b * r1
+        first = b * r1
         s1[0, b] = s1[0, b] + below[first : first + r1]
         s1[n1 - 1, b] = s1[n1 - 1, b] + above[first : first + r1]
     near = r1 - HU
@@ -466,9 +471,6 @@
             first = near * (p * s1.shape[1] + b)
             up[first : first + near] = s1[n1 - 4 + p, b, HU // 2 : HU // 2 + near, :]
             down[first : first + near] = s1[p, b, HU // 2 : HU // 2 + near, :]
-    first = near * 4 * s1.shape[1]
-    up[first:] = third_up[...]
-    down[first:] = third_down[...]
 
 
 def third_kernel(boxes, slabs, s2, s3, fb, vb, summed):
@@ -478,7 +480,7 @@
     zero(vb, (0, planes + 1))
     for plane in range(planes):
         fb[plane + 1, 0, 8 : 8 + rows, :] = s2[plane]
-    relax(vb, 1, (0, planes), fb, 1, rows, HX // 4, edges, None, chunk=32)
+    relax(vb, 1, (0, planes), fb, 1, rows, HX // 4, edges, None, chunk=32, unroll=4)
     quarter = planes // 4
     h3 = HX // 8
     own = rows // 2 - 2 * h3
@@ -489,7 +491,7 @@
         def store(index, group, value, part=part):
             s3[index, :, lanes * part : lanes * (part + 1)] = value[h3 : h3 + own]
 
-        restrict(fb, 1, vb, 1, (quarter * part, quarter * (part + 1)), rows, summed, store)
+        restrict(fb, 1, vb, 1, (quarter * part, quarter * (part + 1)), rows, summed, store, unroll=quarter)
 
 
 def middle_kernel(
@@ -567,9 +569,9 @@
         return e3p[index >> 1, first : first + size, :]
 
     h2 = HX // 4
-    relax(v2a, 5, (-4, n2 + 4), f2, 5, rows2, h2, edges, n2, extra=extra2, chunk=32)
-    relax(v2b, 5, (-3, n2 + 3), f2, 5, rows2, h2, edges, n2, old=v2a, ooff=5, chunk=32)
-    relax(v2a, 5, (-2, n2 + 2), f2, 5, rows2, h2, edges, n2, old=v2b, ooff=5, chunk=32)
+    relax(v2a, 5, (-4, n2 + 4), f2, 5, rows2, h2, edges, n2, extra=extra2, chunk=32, unroll=2)
+    relax(v2b, 5, (-3, n2 + 3), f2, 5, rows2, h2, edges, n2, old=v2a, ooff=5, chunk=32, unroll=2)
+    relax(v2a, 5, (-2, n2 + 2), f2, 5, rows2, h2, edges, n2, old=v2b, ooff=5, chunk=32, unroll=2)
 
     cut = h2 - HU // 2
     matrix2 = copy_matrix(LANES)
@@ -596,9 +598,9 @@
     def extra1(index, b, first, size):
         return e2p[(index + 1) >> 1, b, first : first + size, :]
 
-    relax(v1a, 4, (-3, n1 + 3), f1, 4, rows1, HU, edges, n1, extra=extra1)
-    relax(v1b, 4, (-2, n1 + 2), f1, 4, rows1, HU, edges, n1, old=v1a, ooff=4)
-    relax(e1, 1, (-1, n1 + 1), f1, 4, rows1, HU, edges, n1, old=v1b, ooff=4, shift=0)
+    relax(v1a, 4, (-3, n1 + 3), f1, 4, rows1, HU, edges, n1, extra=extra1, unroll=2)
+    relax(v1b, 4, (-2, n1 + 2), f1, 4, rows1, HU, edges, n1, old=v1a, ooff=4, unroll=2)
+    relax(e1, 1, (-1, n1 + 1), f1, 4, rows1, HU, edges, n1, old=v1b, ooff=4, shift=0, unroll=2)
 
 
 def early_kernel(
@@ -663,7 +665,7 @@
 
 def tail_kernel(
     boxes, slabs, n0, x0,
-    e2p, s1, below, above, f_own, f_rim, v_own, v_rim,
+    e2p, s1, below, above, late_below, late_above, f_own, f_rim, v_own, v_rim,
     out,
     f1, v1a, v1b, e1,
     fb, va, vb, ob, sem, out_sem,
@@ -688,12 +690,13 @@
     cut = HU // 2
     r1 = e1.shape[2]
     size1 = r1 - 2 * cut
-    first = 4 * s1.shape[1] * (r1 - HU)
-    wide = (below.shape[0] - first) // fb.shape[1]
+    begin = s1.shape[1] * r1
+    wide = (late_below.shape[0] - begin) // fb.shape[1]
     for b in range(fb.shape[1]):
         at = slice(4 + HU, 4 + HU + wide)
-        for plane, message in ((1, below), (4 + n0, above)):
-            va[plane, b, at, :] = va[plane, b, at, :] + (C * C) * message[first + wide * b : first + wide * (b + 1)]
+        for plane, message in ((1, late_below), (4 + n0, late_above)):
+            first = begin + wide * b
+            va[plane, b, at, :] = va[plane, b, at, :] + (C * C) * message[first : first + wide]
 
     def prolong(k):
         for group in range(e1.shape[1]):
@@ -705,7 +708,7 @@
                         at = pl.ds(start, size1, stride=2)
                         va[plane, 2 * group + b, at, :] = va[plane, 2 * group + b, at, :] + part
 
-    each(e1.shape[0], prolong)
+    each(e1.shape[0], prolong, unroll=2)
     relax(vb, 3, (-1, n0 + 1), fb, 1, rows, HU, edges, n0, old=va, ooff=3, unroll=2)
 
     def last(z):
@@ -787,9 +790,9 @@
     packed = lax.all_gather(packed, "box", axis=0, tiled=True)
 
     slots = boxes * max(2, patches // 4)
-    rim = 2 * rows2 + b1 * up_rows1
+    rim = 2 * rows2
     message = rim + 2 * (8 * b0 + slots)
-    f_own, v_own, c1, c2, up, down, third_up, third_down = pl.pallas_call(
+    f_own, v_own, c1, c2, up, down, late_up, late_down = pl.pallas_call(
         functools.partial(down_kernel, boxes, slabs, n0, x0),
         name="down",
         out_shape=(
@@ -799,8 +802,8 @@
             shape_of(n2 + 4, 1, rows2, LANES),
             shape_of(message, LANES),
             shape_of(message, LANES),
-            shape_of(b0 * (x0 + HU), LANES),
-            shape_of(b0 * (x0 + HU), LANES),
+            shape_of(b1 * up_rows1 + b0 * (x0 + HU), LANES),
+            shape_of(b1 * up_rows1 + b0 * (x0 + HU), LANES),
         ),
         in_specs=[HBM] * 4 + [VM],
         out_specs=(HBM,) * 2 + (VM,) * 6,
@@ -809,8 +812,8 @@
             scratch(n0 + 6, b0, rows0 + 16, LANES),
             scratch(n1 + 8, b1, rows1 + 16, LANES),
             scratch(n1 + 10, b1, rows1 + 16, LANES),
-            scratch(b0 // 2, rows1, 2 * LANES),
-            scratch(max(1, b1 // 2), rows2, min(2, b1) * LANES),
+            scratch(n1 + 2, b0 // 2, rows1, 2 * LANES),
+            scratch(n2 + 4, max(1, b1 // 2), rows2, min(2, b1) * LANES),
             table,
             table,
             table,
@@ -823,6 +826,8 @@
 
     from_below = shift_by(up, "gz", 1)
     from_above = shift_by(down, "gz", -1)
+    late_below = shift_by(late_up, "gz", 1)
+    late_above = shift_by(late_down, "gz", -1)
     copies = pl.pallas_call(
         total_kernel,
         name="total",
@@ -834,16 +839,16 @@
     )(c2, from_below, from_above)
     s2 = lax.all_to_all(copies, "gz", split_axis=0, concat_axis=0, tiled=True)
     s2 = s2.reshape(slabs * n2, rows2, LANES)
-    last = 4 * b1 * (up_rows1 - HU) + b0 * (x0 + HU)
+    last = 4 * b1 * (up_rows1 - HU)
     s1, up, down = pl.pallas_call(
-        functools.partial(join_kernel, rows2),
+        join_kernel,
         name="join",
         out_shape=(shape_of(n1, b1, up_rows1, LANES), shape_of(last, LANES), shape_of(last, LANES)),
-        in_specs=[VM] * 5,
+        in_specs=[VM] * 3,
         out_specs=(VM,) * 3,
         compiler_params=limit(5),
         cost_estimate=cost(10**6, 10**6),
-    )(c1, from_below, from_above, third_up, third_down)
+    )(c1, late_below, late_above)
     below = shift_by(up, "gz", 1)
     above = shift_by(down, "gz", -1)
 
@@ -874,7 +879,7 @@
         out_shape=shape_of(half, own3, LANES),
         in_specs=[VM],
         out_specs=VM,
-        scratch_shapes=[scratch(planes2 + 2, 1, rows2 + 16, LANES)] * 2 + [scratch(1, rows2 // 2, LANES)],
+        scratch_shapes=[scratch(planes2 + 2, 1, rows2 + 16, LANES)] * 2 + [scratch(half, 1, rows2 // 2, LANES)],
         compiler_params=limit(4),
         cost_estimate=cost(10**6, 10**6),
     )(s2)
@@ -896,7 +901,7 @@
         functools.partial(tail_kernel, boxes, slabs, n0, x0),
         name="tail",
         out_shape=shape_of(n0, x0, y0),
-        in_specs=[VM] * 4 + [HBM] * 4,
+        in_specs=[VM] * 6 + [HBM] * 4,
         out_specs=HBM,
         scratch_shapes=[scratch(n1 + 8, b1, up_rows1 + 16, LANES)] * 3
         + [scratch(n1 + 2, b1, up_rows1, LANES)]
@@ -905,7 +910,7 @@
         + [scratch(n0, b0, x0, LANES), dma((6,)), dma(())],
         compiler_params=limit(24),
         cost_estimate=cost(4 * 10**7, 10**7),
-    )(e2p, s1, below, above, in_hbm(f_own), in_hbm(f_rim), in_hbm(v_own), in_hbm(v_rim))
+    )(e2p, s1, below, above, late_below, late_above, in_hbm(f_own), in_hbm(f_rim), in_hbm(v_own), in_hbm(v_rim))
 
 
 def solution(mesh):

time: 123 us -> 125 us (1.016)
  starting transfers between devices: 27.4 us -> 32.7 us
  Pallas kernels: 36.9 us -> 32.8 us
    ppermute x8 -> x10, starting transfers between devices: 22.1 us -> 28.1 us  [shift_by(): return lax.ppermute(array, axis, pairs)]
    pallas_call x1, Pallas kernels: 3.38 us -> 0.93 us  [per_device(): pl.pallas_call(functools.partial(third_kernel, boxes, slabs), name='third...]
    ppermute x8 -> x10, waiting for transfers between devices: 37.4 us -> 37.7 us  [shift_by(): return lax.ppermute(array, axis, pairs)]
  transfers between devices with their start and end apart: 9 -> 11, of which waited for: 4 -> 6; matrix products, arithmetic and copies ran while one was open for 0% -> 0% of each run, Pallas kernels for 11% -> 9%
where the time goes in v3:
time: 125 us; the launch traced here: 122 us
  waiting for transfers between devices  37.8 us (30%)
  Pallas kernels  32.8 us (26%)
  starting transfers between devices  32.7 us (26%)
  blocking collectives  18 us (14%)
    ppermute x10, waiting for transfers between devices, shift_by(): return lax.ppermute(array, axis, pairs)  37.7 us
    ppermute x10, starting transfers between devices, shift_by(): return lax.ppermute(array, axis, pairs)  28.1 us
    all_gather x1, blocking collectives, per_device(): packed = lax.all_gather(packed, 'box', axis=0, tiled=True)  11.3 us
    pallas_call x1, Pallas kernels, per_device(): pl.pallas_call(functools.partial(down_kernel, boxes, slabs, n0, x0), name...  11.2 us
    pallas_call x1, Pallas kernels, per_device(): pl.pallas_call(functools.partial(tail_kernel, boxes, slabs, n0, x0), name...  7.83 us
    all_gather x1, blocking collectives, per_device(): s3 = lax.all_gather(s3, 'box', axis=0)  6.66 us
    pallas_call x1, Pallas kernels, per_device(): pl.pallas_call(functools.partial(early_kernel, boxes, slabs, n0, x0, rim)...  5.86 us
    all_to_all x1, starting transfers between devices, per_device(): s2 = lax.all_to_all(copies, 'gz', split_axis=0, concat_axis=0, tiled=True)  4.54 us
  transfers between devices with their start and end apart: 11, of which 6 were waited for; matrix products, arithmetic and copies ran while one was open for 0% of the time, Pallas kernels for 9%

profile of v3, /device:TPU:19, one launch (start us, length us, event | category | flops | bytes accessed | tf_op | source)
XLA Modules:
  0.0 122.2 jit_solution(6137295998992199559)
XLA Ops:
  0.0 1.7 %pack.1 = (f32[128,128]{1,0:T(8,128)S(1)}, f32[8,32,512]{2,1,0:T(8,128)S(1)}, f32[8,32,512]{2,1,0:T(8,128)S(1)}, f32[2,128,512]{2,1,0:T(8,128)S(1)}, f32[2,128,512]{2,1,0:T(8,128)S(1)}) custom-call(s32[4,64]{1,0:T(4,128)} %bitcast.9, f32[16,16,256]{2,1,0:T(8,128)} %fine.1, f32[16,16,128]{2,1,0:T(8,128)} %flux.1, f32[8,128,512]{2,1,0:T(8,128)} %coarse.3), custom_call_target="tpu_custom_call" | custom-call | flops 10000000 | bytes 1000000 | tf_op jit(solution)/shard_map/pack/pallas_call | solution.py:764
  1.7 3.7 %collective-permute-start = (f32[8,32,512]{2,1,0:T(8,128)S(1)}, f32[8,32,512]{2,1,0:T(8,128)S(1)}, u32[]{:S(2)}, u32[]{:S(2)}) collective-permute-start(f32[8,32,512]{2,1,0:T(8,128)S(1)} %get-tuple-element.23), channel_id=1, source_target_pairs={{0,8},{8,16},{16,24},{1,9},{9,17},{17,25},{2,10},{10,18},{18,26},{... | collective-permute-start | bytes 1572872 | tf_op jit(solution)/shard_map/ppermute | solution.py:748
  5.5 1.9 %collective-permute-start.1 = (f32[8,32,512]{2,1,0:T(8,128)S(1)}, f32[8,32,512]{2,1,0:T(8,128)S(1)}, u32[]{:S(2)}, u32[]{:S(2)}) collective-permute-start(f32[8,32,512]{2,1,0:T(8,128)S(1)} %get-tuple-element.24), channel_id=1, source_target_pairs={{8,0},{16,8},{24,16},{9,1},{17,9},{25,17},{10,2},{18,10},{26,18},{... | collective-permute-start | bytes 1572872 | tf_op jit(solution)/shard_map/ppermute | solution.py:748
  7.4 11.3 %all_gather.9.packed = f32[512,128]{1,0:T(8,128)S(1)} all-gather(f32[128,128]{1,0:T(8,128)S(1)} %get-tuple-element.25), channel_id=1, replica_groups=mesh['box'=4,'gz'=8] {'box'}, dimensions={0}, use_global_device_ids=true | all-gather | bytes 327680 | tf_op jit(solution)/shard_map/all_gather | solution.py:790
  18.7 0.0 collective-permute-done.x_low
  18.7 0.0 collective-permute-done.1.x_high
  18.7 11.2 %down.1 = (f32[8,4,144,128]{3,2,1,0:T(8,128)}, f32[6,4,144,128]{3,2,1,0:T(8,128)}, f32[6,2,80,128]{3,2,1,0:T(8,128)S(1)}, f32[6,1,48,128]{3,2,1,0:T(8,128)S(1)},...) custom-call(s32[3,64]{1,0:T(4,128)} %bitcast.7, ...), custom_call_target="tpu_custom_call" | custom-call | flops 30000000 | bytes 10000000 | tf_op jit(solution)/shard_map/down/pallas_call | solution.py:795
  29.9 3.2 %collective-permute-start.2 = (f32[192,128]{1,0:T(8,128)S(1)}, f32[192,128]{1,0:T(8,128)S(1)}, u32[]{:S(2)}, u32[]{:S(2)}) collective-permute-start(f32[192,128]{1,0:T(8,128)S(1)} %get-tuple-element.27), channel_id=1, source_target_pairs={{0,1},{1,2},{2,3},{3,4},{4,5},{5,6},{6,7},{8,9},{9,10},{10,11},{11... | collective-permute-start | bytes 294920 | tf_op jit(solution)/shard_map/ppermute | solution.py:748
  33.1 2.1 %collective-permute-start.3 = (f32[192,128]{1,0:T(8,128)S(1)}, f32[192,128]{1,0:T(8,128)S(1)}, u32[]{:S(2)}, u32[]{:S(2)}) collective-permute-start(f32[192,128]{1,0:T(8,128)S(1)} %get-tuple-element.28), channel_id=1, source_target_pairs={{1,0},{2,1},{3,2},{4,3},{5,4},{6,5},{7,6},{9,8},{10,9},{11,10},{12... | collective-permute-start | bytes 294920 | tf_op jit(solution)/shard_map/ppermute | solution.py:748
  35.2 0.5 collective-permute-done.2.below
  35.8 4.4 %collective-permute-done.3.above = f32[192,128]{1,0:T(8,128)S(1)} collective-permute-done((f32[192,128]{1,0:T(8,128)S(1)}, f32[192,128]{1,0:T(8,128)S(1)}, u32[]{:S(2)}, u32[]{:S(2)}) %collective-permute-start.3) | collective-permute-done | bytes 98336 | tf_op jit(solution)/shard_map/ppermute | solution.py:748
  40.1 0.8 total.1
  40.9 4.5 %all-to-all-start = ((f32[8,96,128]{2,1,0:T(8,128)}), f32[8,96,128]{2,1,0:T(8,128)S(1)}, u32[]{:S(2)}, u32[]{:S(2)}) async-start(f32[8,96,128]{2,1,0:T(8,128)} %total.1), calls=%async_computation | async-start | bytes 786432 | tf_op jit(solution)/shard_map/all_to_all | solution.py:840
  45.4 3.1 %collective-permute-start.4 = (f32[704,128]{1,0:T(8,128)}, f32[704,128]{1,0:T(8,128)S(1)}, u32[]{:S(2)}, u32[]{:S(2)}) collective-permute-start(f32[704,128]{1,0:T(8,128)} %get-tuple-element.30), channel_id=1, source_target_pairs={{0,1},{1,2},{2,3},{3,4},{4,5},{5,6},{6,7},{8,9},{9,10},{10,11},{11... | collective-permute-start | bytes 1081352 | tf_op jit(solution)/shard_map/ppermute | solution.py:748
  48.5 2.2 %collective-permute-start.5 = (f32[704,128]{1,0:T(8,128)S(1)}, f32[704,128]{1,0:T(8,128)S(1)}, u32[]{:S(2)}, u32[]{:S(2)}) collective-permute-start(f32[704,128]{1,0:T(8,128)S(1)} %get-tuple-element.31), channel_id=1, source_target_pairs={{1,0},{2,1},{3,2},{4,3},{5,4},{6,5},{7,6},{9,8},{10,9},{11,10},{12... | collective-permute-start | bytes 1081352 | tf_op jit(solution)/shard_map/ppermute | solution.py:748
  50.7 4.0 %collective-permute-start.8 = (f32[2,128,512]{2,1,0:T(8,128)S(1)}, f32[2,128,512]{2,1,0:T(8,128)S(1)}, u32[]{:S(2)}, u32[]{:S(2)}) collective-permute-start(f32[2,128,512]{2,1,0:T(8,128)S(1)} %get-tuple-element.36), channel_id=1, source_target_pairs={{0,1},{1,2},{2,3},{3,4},{4,5},{5,6},{6,7},{8,9},{9,10},{10,11},{11... | collective-permute-start | bytes 1572872 | tf_op jit(solution)/shard_map/ppermute | solution.py:748
  54.7 1.9 %collective-permute-start.9 = (f32[2,128,512]{2,1,0:T(8,128)S(1)}, f32[2,128,512]{2,1,0:T(8,128)S(1)}, u32[]{:S(2)}, u32[]{:S(2)}) collective-permute-start(f32[2,128,512]{2,1,0:T(8,128)S(1)} %get-tuple-element.37), channel_id=1, source_target_pairs={{1,0},{2,1},{3,2},{4,3},{5,4},{6,5},{7,6},{9,8},{10,9},{11,10},{12... | collective-permute-start | bytes 1572872 | tf_op jit(solution)/shard_map/ppermute | solution.py:748
  56.6 20.6 %collective-permute-done.4.below.late_below = f32[704,128]{1,0:T(8,128)S(1)} collective-permute-done((f32[704,128]{1,0:T(8,128)}, f32[704,128]{1,0:T(8,128)S(1)}, u32[]{:S(2)}, u32[]{:S(2)}) %collective-permute-start.4) | collective-permute-done | bytes 360480 | tf_op jit(solution)/shard_map/ppermute | solution.py:748
  77.3 1.7 %collective-permute-done.5.above.late_above = f32[704,128]{1,0:T(8,128)S(1)} collective-permute-done((f32[704,128]{1,0:T(8,128)S(1)}, f32[704,128]{1,0:T(8,128)S(1)}, u32[]{:S(2)}, u32[]{:S(2)}) %collective-permute-start.5) | collective-permute-done | bytes 360480 | tf_op jit(solution)/shard_map/ppermute | solution.py:748
  79.0 0.9 join.1
  79.9 4.1 %collective-permute-start.6 = (f32[576,128]{1,0:T(8,128)}, f32[576,128]{1,0:T(8,128)S(1)}, u32[]{:S(2)}, u32[]{:S(2)}) collective-permute-start(f32[576,128]{1,0:T(8,128)} %get-tuple-element.33), channel_id=1, source_target_pairs={{0,1},{1,2},{2,3},{3,4},{4,5},{5,6},{6,7},{8,9},{9,10},{10,11},{11... | collective-permute-start | bytes 884744 | tf_op jit(solution)/shard_map/ppermute | solution.py:748
  84.0 1.9 %collective-permute-start.7 = (f32[576,128]{1,0:T(8,128)}, f32[576,128]{1,0:T(8,128)S(1)}, u32[]{:S(2)}, u32[]{:S(2)}) collective-permute-start(f32[576,128]{1,0:T(8,128)} %get-tuple-element.34), channel_id=1, source_target_pairs={{1,0},{2,1},{3,2},{4,3},{5,4},{6,5},{7,6},{9,8},{10,9},{11,10},{12... | collective-permute-start | bytes 884744 | tf_op jit(solution)/shard_map/ppermute | solution.py:748
  86.0 2.6 %collective-permute-done.8.z_below = f32[2,128,512]{2,1,0:T(8,128)S(1)} collective-permute-done((f32[2,128,512]{2,1,0:T(8,128)S(1)}, f32[2,128,512]{2,1,0:T(8,128)S(1)}, u32[]{:S(2)}, u32[]{:S(2)}) %collective-permute-start.8) | collective-permute-done | bytes 524320 | tf_op jit(solution)/shard_map/ppermute | solution.py:748
  88.5 8.0 %collective-permute-done.9.z_above = f32[2,128,512]{2,1,0:T(8,128)S(1)} collective-permute-done((f32[2,128,512]{2,1,0:T(8,128)S(1)}, f32[2,128,512]{2,1,0:T(8,128)S(1)}, u32[]{:S(2)}, u32[]{:S(2)}) %collective-permute-start.9) | collective-permute-done | bytes 524320 | tf_op jit(solution)/shard_map/ppermute | solution.py:748
  96.5 0.8 copy-done.1
  97.3 5.9 %early.1 = (f32[2,4,160,128]{3,2,1,0:T(8,128)}, f32[6,4,160,128]{3,2,1,0:T(8,128)}) custom-call(s32[3,64]{1,0:T(4,128)} %bitcast.8, f32[8,4,144,128]{3,2,1,0:T(8,128)} %get-tuple-element.35.f_own, f32[2,128,512]{2,1,0:T(8,128)} %copy-done, f32[2,128,512]{2,1,0:T(8,128)} %copy-done.1, f32[192,128]{1,0:T(8,128)S(1)} %collective-permute-done.2.below, ...), custom_call_target="tpu_custom_call" | custom-call | flops 20000000 | bytes 10000000 | tf_op jit(solution)/shard_map/early/pallas_call | solution.py:856
  103.2 0.0 all-to-all-done
  103.2 0.9 third.1
  104.1 6.7 %all-gather = f32[16,16,128]{2,1,0:T(8,128)S(1)} all-gather(f32[4,16,128]{2,1,0:T(8,128)S(1)} %third.1), channel_id=2, replica_groups=mesh['box'=4,'gz'=8] {'box'}, dimensions={0}, use_global_device_ids=true | all-gather | bytes 163840 | tf_op jit(solution)/shard_map/all_gather | solution.py:886
  110.8 3.6 %middle.1.e2p = f32[6,2,80,128]{3,2,1,0:T(8,128)S(1)} custom-call(f32[4,4,16,128]{3,2,1,0:T(8,128)S(1)} %bitcast.6, f32[16,48,128]{2,1,0:T(8,128)S(1)} %bitcast.5), custom_call_target="tpu_custom_call" | custom-call | flops 10000000 | bytes 2000000 | tf_op jit(solution)/shard_map/middle/pallas_call | solution.py:888
  114.3 0.0 collective-permute-done.6.below
  114.3 7.8 %tail.1 = f32[8,128,512]{2,1,0:T(8,128)} custom-call(f32[6,2,80,128]{3,2,1,0:T(8,128)S(1)} %middle.1.e2p, f32[4,2,80,128]{3,2,1,0:T(8,128)S(1)} %get-tuple-element.32.s1, f32[576,128]{1,0:T(8,128)S(1)} %collective-permute-done.6.below, f32[576,128]{1,0:T(8,128)S(1)} %collective-permute-done.7.above, f32[704,128]{1,0:T(8,128)S(1)} %collective-permute-done.4.below.late_below, ...), custom_call_target="tpu_custom_call" | custom-call | flops 40000000 | bytes 10000000 | tf_op jit(solution)/shard_map/tail/pallas_call | solution.py:900
  (4 shorter events, 0.0 us)
Async XLA Ops:
  1.7 17.0 %collective-permute-start = (f32[8,32,512]{2,1,0:T(8,128)S(1)}, f32[8,32,512]{2,1,0:T(8,128)S(1)}, u32[]{:S(2)}, u32[]{:S(2)}) collective-permute-start(f32[8,32,512]{2,1,0:T(8,128)S(1)} %get-tuple-element.23), channel_id=1, source_target_pairs={{0,8},{8,16},{16,24},{1,9},{9,17},{17,25},{2,10},{10,18},{18,26},{... | collective-permute-start | bytes 1572872 | tf_op jit(solution)/shard_map/ppermute | solution.py:748
  5.5 13.3 %collective-permute-start.1 = (f32[8,32,512]{2,1,0:T(8,128)S(1)}, f32[8,32,512]{2,1,0:T(8,128)S(1)}, u32[]{:S(2)}, u32[]{:S(2)}) collective-permute-start(f32[8,32,512]{2,1,0:T(8,128)S(1)} %get-tuple-element.24), channel_id=1, source_target_pairs={{8,0},{16,8},{24,16},{9,1},{17,9},{25,17},{10,2},{18,10},{26,18},{... | collective-permute-start | bytes 1572872 | tf_op jit(solution)/shard_map/ppermute | solution.py:748
  29.9 5.8 %collective-permute-start.2 = (f32[192,128]{1,0:T(8,128)S(1)}, f32[192,128]{1,0:T(8,128)S(1)}, u32[]{:S(2)}, u32[]{:S(2)}) collective-permute-start(f32[192,128]{1,0:T(8,128)S(1)} %get-tuple-element.27), channel_id=1, source_target_pairs={{0,1},{1,2},{2,3},{3,4},{4,5},{5,6},{6,7},{8,9},{9,10},{10,11},{11... | collective-permute-start | bytes 294920 | tf_op jit(solution)/shard_map/ppermute | solution.py:748
  33.1 7.0 %collective-permute-start.3 = (f32[192,128]{1,0:T(8,128)S(1)}, f32[192,128]{1,0:T(8,128)S(1)}, u32[]{:S(2)}, u32[]{:S(2)}) collective-permute-start(f32[192,128]{1,0:T(8,128)S(1)} %get-tuple-element.28), channel_id=1, source_target_pairs={{1,0},{2,1},{3,2},{4,3},{5,4},{6,5},{7,6},{9,8},{10,9},{11,10},{12... | collective-permute-start | bytes 294920 | tf_op jit(solution)/shard_map/ppermute | solution.py:748
  40.9 62.3 %all-to-all-start = ((f32[8,96,128]{2,1,0:T(8,128)}), f32[8,96,128]{2,1,0:T(8,128)S(1)}, u32[]{:S(2)}, u32[]{:S(2)}) async-start(f32[8,96,128]{2,1,0:T(8,128)} %total.1), calls=%async_computation | async-start | bytes 786432 | tf_op jit(solution)/shard_map/all_to_all | solution.py:840
  45.4 31.9 %collective-permute-start.4 = (f32[704,128]{1,0:T(8,128)}, f32[704,128]{1,0:T(8,128)S(1)}, u32[]{:S(2)}, u32[]{:S(2)}) collective-permute-start(f32[704,128]{1,0:T(8,128)} %get-tuple-element.30), channel_id=1, source_target_pairs={{0,1},{1,2},{2,3},{3,4},{4,5},{5,6},{6,7},{8,9},{9,10},{10,11},{11... | collective-permute-start | bytes 1081352 | tf_op jit(solution)/shard_map/ppermute | solution.py:748
  48.5 30.4 %collective-permute-start.5 = (f32[704,128]{1,0:T(8,128)S(1)}, f32[704,128]{1,0:T(8,128)S(1)}, u32[]{:S(2)}, u32[]{:S(2)}) collective-permute-start(f32[704,128]{1,0:T(8,128)S(1)} %get-tuple-element.31), channel_id=1, source_target_pairs={{1,0},{2,1},{3,2},{4,3},{5,4},{6,5},{7,6},{9,8},{10,9},{11,10},{12... | collective-permute-start | bytes 1081352 | tf_op jit(solution)/shard_map/ppermute | solution.py:748
  50.7 37.8 %collective-permute-start.8 = (f32[2,128,512]{2,1,0:T(8,128)S(1)}, f32[2,128,512]{2,1,0:T(8,128)S(1)}, u32[]{:S(2)}, u32[]{:S(2)}) collective-permute-start(f32[2,128,512]{2,1,0:T(8,128)S(1)} %get-tuple-element.36), channel_id=1, source_target_pairs={{0,1},{1,2},{2,3},{3,4},{4,5},{5,6},{6,7},{8,9},{9,10},{10,11},{11... | collective-permute-start | bytes 1572872 | tf_op jit(solution)/shard_map/ppermute | solution.py:748
  54.7 41.8 %collective-permute-start.9 = (f32[2,128,512]{2,1,0:T(8,128)S(1)}, f32[2,128,512]{2,1,0:T(8,128)S(1)}, u32[]{:S(2)}, u32[]{:S(2)}) collective-permute-start(f32[2,128,512]{2,1,0:T(8,128)S(1)} %get-tuple-element.37), channel_id=1, source_target_pairs={{1,0},{2,1},{3,2},{4,3},{5,4},{6,5},{7,6},{9,8},{10,9},{11,10},{12... | collective-permute-start | bytes 1572872 | tf_op jit(solution)/shard_map/ppermute | solution.py:748
  79.9 34.4 %collective-permute-start.6 = (f32[576,128]{1,0:T(8,128)}, f32[576,128]{1,0:T(8,128)S(1)}, u32[]{:S(2)}, u32[]{:S(2)}) collective-permute-start(f32[576,128]{1,0:T(8,128)} %get-tuple-element.33), channel_id=1, source_target_pairs={{0,1},{1,2},{2,3},{3,4},{4,5},{5,6},{6,7},{8,9},{9,10},{10,11},{11... | collective-permute-start | bytes 884744 | tf_op jit(solution)/shard_map/ppermute | solution.py:748
  84.0 30.3 %collective-permute-start.7 = (f32[576,128]{1,0:T(8,128)}, f32[576,128]{1,0:T(8,128)S(1)}, u32[]{:S(2)}, u32[]{:S(2)}) collective-permute-start(f32[576,128]{1,0:T(8,128)} %get-tuple-element.34), channel_id=1, source_target_pairs={{1,0},{2,1},{3,2},{4,3},{5,4},{6,5},{7,6},{9,8},{10,9},{11,10},{12... | collective-permute-start | bytes 884744 | tf_op jit(solution)/shard_map/ppermute | solution.py:748
  88.5 8.0 %copy-start = (f32[2,128,512]{2,1,0:T(8,128)}, f32[2,128,512]{2,1,0:T(8,128)S(1)}, u32[]{:S(2)}) copy-start(f32[2,128,512]{2,1,0:T(8,128)S(1)} %collective-permute-done.8.z_below) | copy-start | bytes 1572868
  96.5 0.8 copy-start.1

commit v4 on v3

--- a/solution.py
+++ b/solution.py
@@ -326,22 +326,22 @@
             field[plane, block, pl.ds(row, 16), :] = jnp.where(core, 0.0, now) + jnp.where(ring, tile, 0.0)
 
 
-def listed(box_list, row_of, found):
-    def step(patch, count):
-        row, keep = row_of(box_list[0, patch], box_list[1, patch])
-        found[0, count] = row
-        found[1, count] = box_list[2, patch] - 4
-        found[2, count] = patch
-        return count + jnp.where(keep, 1, 0)
-
-    return lax.fori_loop(0, box_list.shape[1], step, jnp.zeros((), I32), unroll=8)
+def listed(table, keeps, found):
+    def step(patch, counts):
+        owner, x = table[0, patch], table[1, patch]
+        for row, count in enumerate(counts):
+            found[row, count] = patch
+        return tuple(count + jnp.where(keep(owner, x), 1, 0) for keep, count in zip(keeps, counts))
+
+    zeros = (jnp.zeros((), I32),) * len(keeps)
+    return lax.fori_loop(0, table.shape[1], step, zeros, unroll=8)
 
 
 def down_kernel(
     boxes, slabs, n0, x0,
     box_list, coarse, x_low, x_high, packed,
     f_own, v_own, c1, c2, up, down, late_up, late_down,
-    fb, vb, g1, v1, summed0, summed1, patches, found, owned, sem, out_sem,
+    fb, vb, g1, v1, summed0, summed1, patches, found, sem, out_sem,
 ):
     edges = Edges(boxes, slabs)
     rows0, rows1, rows2 = x0 + 2 * HX, x0 // 2 + HX, x0 // 4 + HX // 2
@@ -357,23 +357,22 @@
         copy.start()
     fetch.wait()
 
-    def near_row(owner, x):
-        row = (owner - edges.box) * x0 + x - 4 + HX
-        return row + 8, (row >= 0) & (row < rows0)
-
-    def own_row(owner, x):
-        return x, owner == edges.box
-
-    near_count = listed(patches, near_row, found)
-    own_count = listed(patches, own_row, owned)
+    def row_of(owner, x):
+        return (owner - edges.box) * x0 + x - 4 + HX
+
+    def is_near(owner, x):
+        row = row_of(owner, x)
+        return (row >= 0) & (row < rows0)
+
+    near_count, own_count = listed(patches, (is_near, lambda owner, x: owner == edges.box), found)
     for copy in copies:
         copy.wait()
     tiles = Tiles()
 
     def place(index):
-        patch = found[2, index]
+        patch = found[0, index]
         lines = [(2 + z, packed[pl.ds(patch * n0 + z, 1), :]) for z in range(n0)]
-        tiles.put(fb, found[0, index], found[1, index], lines)
+        tiles.put(fb, row_of(patches[0, patch], patches[1, patch]) + 8, patches[2, patch] - 4, lines)
 
     lax.fori_loop(0, near_count, lambda index, carry: place(index) or carry, 0)
 
@@ -409,20 +408,20 @@
 
     restrict(g1, 4, v1, 5, (-2, n2 + 2), rows1, summed1, store2, v_planes=(-2, n1 + 2), s_planes=(-1, n1 + 1))
 
-    r1 = c1.shape[2]
-    for target, late, fine_plane, coarse_first in ((up, late_up, n1 + 1, n2 + 2), (down, late_down, 0, 0)):
+    near = c1.shape[2] - HU
+    for target, fine_plane, coarse_first in ((up, n1 + 1, n2 + 2), (down, 0, 0)):
         target[0:rows2] = c2[coarse_first, 0]
         target[rows2 : 2 * rows2] = c2[coarse_first + 1, 0]
         for b in range(c1.shape[1]):
-            late[r1 * b : r1 * (b + 1)] = c1[fine_plane, b]
+            first = target.shape[0] - near * (c1.shape[1] - b)
+            target[first : first + near] = c1[fine_plane, b, HU // 2 : HU // 2 + near, :]
     rim = 2 * rows2
-    slots = (up.shape[0] - rim) // 2 - 8 * fb.shape[1]
-    begin = c1.shape[1] * r1
-    wide = (late_up.shape[0] - begin) // fb.shape[1]
+    slots = (up.shape[0] - rim - near * c1.shape[1]) // 2 - 8 * fb.shape[1]
+    wide = late_up.shape[0] // fb.shape[1]
     for b in range(fb.shape[1]):
         at = slice(4 + HX, 4 + HX + wide)
-        late_up[begin + wide * b : begin + wide * (b + 1)] = fb[n0 - 1, b, at, :]
-        late_down[begin + wide * b : begin + wide * (b + 1)] = fb[4, b, at, :]
+        late_up[wide * b : wide * (b + 1)] = fb[n0 - 1, b, at, :]
+        late_down[wide * b : wide * (b + 1)] = fb[4, b, at, :]
         for z in range(2):
             first = rim + 8 * (fb.shape[1] * z + b)
             for target, plane in ((up, n0 + z), (down, 2 + z)):
@@ -430,11 +429,11 @@
                 target[first + 3 : first + 6, :] = fb[plane, b, 8 + HX + x0 : 8 + HX + x0 + 3, :]
                 target[first + 6 : first + 8, :] = jnp.zeros((2, LANES), F32)
     rim = rim + 16 * fb.shape[1]
-    up[rim:, :] = jnp.zeros((2 * slots, LANES), F32)
-    down[rim:, :] = jnp.zeros((2 * slots, LANES), F32)
+    up[rim : rim + 2 * slots, :] = jnp.zeros((2 * slots, LANES), F32)
+    down[rim : rim + 2 * slots, :] = jnp.zeros((2 * slots, LANES), F32)
 
     def keep(slot):
-        patch = owned[2, slot]
+        patch = found[1, slot]
         for z in range(2):
             up[pl.ds(rim + z * slots + slot, 1), :] = packed[pl.ds(patch * n0 + n0 - 2 + z, 1), :]
             down[pl.ds(rim + z * slots + slot, 1), :] = packed[pl.ds(patch * n0 + z, 1), :]
@@ -461,11 +460,12 @@
     n1, r1 = s1.shape[0], c1.shape[2]
     for plane in range(n1):
         s1[plane] = c1[1 + plane]
+    near = r1 - HU
+    cells = slice(HU // 2, HU // 2 + near)
     for b in range(s1.shape[1]):
-        first = b * r1
-        s1[0, b] = s1[0, b] + below[first : first + r1]
-        s1[n1 - 1, b] = s1[n1 - 1, b] + above[first : first + r1]
-    near = r1 - HU
+        first = below.shape[0] - near * (s1.shape[1] - b)
+        s1[0, b, cells, :] = s1[0, b, cells, :] + below[first : first + near]
+        s1[n1 - 1, b, cells, :] = s1[n1 - 1, b, cells, :] + above[first : first + near]
     for p in range(4):
         for b in range(s1.shape[1]):
             first = near * (p * s1.shape[1] + b)
@@ -625,12 +625,9 @@
         copy.start()
     fetch.wait()
 
-    def own_row(owner, x):
-        return x - 4 + HU + 8, owner == edges.box
-
-    count = listed(patches, own_row, found)
+    (count,) = listed(patches, (lambda owner, x: owner == edges.box,), found)
     packed = rim + 16 * fb.shape[1]
-    slots = (below.shape[0] - packed) // 2
+    slots = boxes * max(2, patches.shape[1] // boxes // 4)
     for copy in copies:
         copy.wait()
     for z in range(2):
@@ -644,7 +641,8 @@
     def place(slot):
         lines = [(z, below, z) for z in range(2)] + [(6 + z, above, z) for z in range(2)]
         lines = [(plane, message[pl.ds(packed + z * slots + slot, 1), :]) for plane, message, z in lines]
-        tiles.put(fb, found[0, slot], found[1, slot], lines)
+        patch = found[0, slot]
+        tiles.put(fb, patches[1, patch] - 4 + HU + 8, patches[2, patch] - 4, lines)
 
     lax.fori_loop(0, count, lambda index, carry: place(index) or carry, 0)
     outs = [
@@ -690,12 +688,11 @@
     cut = HU // 2
     r1 = e1.shape[2]
     size1 = r1 - 2 * cut
-    begin = s1.shape[1] * r1
-    wide = (late_below.shape[0] - begin) // fb.shape[1]
+    wide = late_below.shape[0] // fb.shape[1]
     for b in range(fb.shape[1]):
         at = slice(4 + HU, 4 + HU + wide)
         for plane, message in ((1, late_below), (4 + n0, late_above)):
-            first = begin + wide * b
+            first = wide * b
             va[plane, b, at, :] = va[plane, b, at, :] + (C * C) * message[first : first + wide]
 
     def prolong(k):
@@ -791,7 +788,7 @@
 
     slots = boxes * max(2, patches // 4)
     rim = 2 * rows2
-    message = rim + 2 * (8 * b0 + slots)
+    message = rim + 2 * (8 * b0 + slots) + b1 * (up_rows1 - HU)
     f_own, v_own, c1, c2, up, down, late_up, late_down = pl.pallas_call(
         functools.partial(down_kernel, boxes, slabs, n0, x0),
         name="down",
@@ -802,8 +799,8 @@
             shape_of(n2 + 4, 1, rows2, LANES),
             shape_of(message, LANES),
             shape_of(message, LANES),
-            shape_of(b1 * up_rows1 + b0 * (x0 + HU), LANES),
-            shape_of(b1 * up_rows1 + b0 * (x0 + HU), LANES),
+            shape_of(b0 * (x0 + HU), LANES),
+            shape_of(b0 * (x0 + HU), LANES),
         ),
         in_specs=[HBM] * 4 + [VM],
         out_specs=(HBM,) * 2 + (VM,) * 6,
@@ -814,7 +811,6 @@
             scratch(n1 + 10, b1, rows1 + 16, LANES),
             scratch(n1 + 2, b0 // 2, rows1, 2 * LANES),
             scratch(n2 + 4, max(1, b1 // 2), rows2, min(2, b1) * LANES),
-            table,
             table,
             table,
             dma((4,)),
@@ -848,7 +844,7 @@
         out_specs=(VM,) * 3,
         compiler_params=limit(5),
         cost_estimate=cost(10**6, 10**6),
-    )(c1, late_below, late_above)
+    )(c1, from_below, from_above)
     below = shift_by(up, "gz", 1)
     above = shift_by(down, "gz", -1)
 

time: 125 us -> 115 us (0.920)
  the two profiles are of different devices: /device:TPU:19 before, /device:TPU:9 now
where the time goes in v4:
time: 115 us; the launch traced here: 114 us
  starting transfers between devices  34.2 us (30%)
  Pallas kernels  31.9 us (28%)
  waiting for transfers between devices  29.4 us (26%)
  blocking collectives  17.8 us (15%)
    ppermute x10, starting transfers between devices, shift_by(): return lax.ppermute(array, axis, pairs)  29.5 us
    ppermute x10, waiting for transfers between devices, shift_by(): return lax.ppermute(array, axis, pairs)  29.4 us
    all_gather x1, blocking collectives, per_device(): packed = lax.all_gather(packed, 'box', axis=0, tiled=True)  11.3 us
    pallas_call x1, Pallas kernels, per_device(): pl.pallas_call(functools.partial(down_kernel, boxes, slabs, n0, x0), name...  10.3 us
    pallas_call x1, Pallas kernels, per_device(): pl.pallas_call(functools.partial(tail_kernel, boxes, slabs, n0, x0), name...  7.82 us
    all_gather x1, blocking collectives, per_device(): s3 = lax.all_gather(s3, 'box', axis=0)  6.47 us
    pallas_call x1, Pallas kernels, per_device(): pl.pallas_call(functools.partial(early_kernel, boxes, slabs, n0, x0, rim)...  5.86 us
    all_to_all x1, starting transfers between devices, per_device(): s2 = lax.all_to_all(copies, 'gz', split_axis=0, concat_axis=0, tiled=True)  4.77 us
  transfers between devices with their start and end apart: 11, of which 2 were waited for; matrix products, arithmetic and copies ran while one was open for 0% of the time, Pallas kernels for 11%

profile of v4, /device:TPU:9, one launch (start us, length us, event | category | flops | bytes accessed | tf_op | source)
XLA Modules:
  0.0 114.4 jit_solution(13065679408822254537)
XLA Ops:
  0.0 1.7 %pack.1 = (f32[128,128]{1,0:T(8,128)S(1)}, f32[8,32,512]{2,1,0:T(8,128)S(1)}, f32[8,32,512]{2,1,0:T(8,128)S(1)}, f32[2,128,512]{2,1,0:T(8,128)S(1)}, f32[2,128,512]{2,1,0:T(8,128)S(1)}) custom-call(s32[4,64]{1,0:T(4,128)} %bitcast.9, f32[16,16,256]{2,1,0:T(8,128)} %fine.1, f32[16,16,128]{2,1,0:T(8,128)} %flux.1, f32[8,128,512]{2,1,0:T(8,128)} %coarse.3), custom_call_target="tpu_custom_call" | custom-call | flops 10000000 | bytes 1000000 | tf_op jit(solution)/shard_map/pack/pallas_call | solution.py:761
  1.7 3.7 %collective-permute-start = (f32[8,32,512]{2,1,0:T(8,128)S(1)}, f32[8,32,512]{2,1,0:T(8,128)S(1)}, u32[]{:S(2)}, u32[]{:S(2)}) collective-permute-start(f32[8,32,512]{2,1,0:T(8,128)S(1)} %get-tuple-element.23), channel_id=1, source_target_pairs={{0,8},{8,16},{16,24},{1,9},{9,17},{17,25},{2,10},{10,18},{18,26},{... | collective-permute-start | bytes 1572872 | tf_op jit(solution)/shard_map/ppermute | solution.py:745
  5.5 1.9 %collective-permute-start.1 = (f32[8,32,512]{2,1,0:T(8,128)S(1)}, f32[8,32,512]{2,1,0:T(8,128)S(1)}, u32[]{:S(2)}, u32[]{:S(2)}) collective-permute-start(f32[8,32,512]{2,1,0:T(8,128)S(1)} %get-tuple-element.24), channel_id=1, source_target_pairs={{8,0},{16,8},{24,16},{9,1},{17,9},{25,17},{10,2},{18,10},{26,18},{... | collective-permute-start | bytes 1572872 | tf_op jit(solution)/shard_map/ppermute | solution.py:745
  7.4 11.3 %all_gather.9.packed = f32[512,128]{1,0:T(8,128)S(1)} all-gather(f32[128,128]{1,0:T(8,128)S(1)} %get-tuple-element.25), channel_id=1, replica_groups=mesh['box'=4,'gz'=8] {'box'}, dimensions={0}, use_global_device_ids=true | all-gather | bytes 327680 | tf_op jit(solution)/shard_map/all_gather | solution.py:787
  18.7 0.0 collective-permute-done.x_low
  18.7 0.0 collective-permute-done.1.x_high
  18.7 10.3 %down.1 = (f32[8,4,144,128]{3,2,1,0:T(8,128)}, f32[6,4,144,128]{3,2,1,0:T(8,128)}, f32[6,2,80,128]{3,2,1,0:T(8,128)S(1)}, f32[6,1,48,128]{3,2,1,0:T(8,128)S(1)},...) custom-call(s32[3,64]{1,0:T(4,128)} %bitcast.7, ...), custom_call_target="tpu_custom_call" | custom-call | flops 30000000 | bytes 10000000 | tf_op jit(solution)/shard_map/down/pallas_call | solution.py:792
  29.1 3.1 %collective-permute-start.2 = (f32[336,128]{1,0:T(8,128)S(1)}, f32[336,128]{1,0:T(8,128)S(1)}, u32[]{:S(2)}, u32[]{:S(2)}) collective-permute-start(f32[336,128]{1,0:T(8,128)S(1)} %get-tuple-element.27), channel_id=1, source_target_pairs={{0,1},{1,2},{2,3},{3,4},{4,5},{5,6},{6,7},{8,9},{9,10},{10,11},{11... | collective-permute-start | bytes 516104 | tf_op jit(solution)/shard_map/ppermute | solution.py:745
  32.2 3.1 %collective-permute-start.3 = (f32[336,128]{1,0:T(8,128)S(1)}, f32[336,128]{1,0:T(8,128)S(1)}, u32[]{:S(2)}, u32[]{:S(2)}) collective-permute-start(f32[336,128]{1,0:T(8,128)S(1)} %get-tuple-element.28), channel_id=1, source_target_pairs={{1,0},{2,1},{3,2},{4,3},{5,4},{6,5},{7,6},{9,8},{10,9},{11,10},{12... | collective-permute-start | bytes 516104 | tf_op jit(solution)/shard_map/ppermute | solution.py:745
  35.3 2.2 %collective-permute-start.8 = (f32[2,128,512]{2,1,0:T(8,128)S(1)}, f32[2,128,512]{2,1,0:T(8,128)}, u32[]{:S(2)}, u32[]{:S(2)}) collective-permute-start(f32[2,128,512]{2,1,0:T(8,128)S(1)} %get-tuple-element.36), channel_id=1, source_target_pairs={{0,1},{1,2},{2,3},{3,4},{4,5},{5,6},{6,7},{8,9},{9,10},{10,11},{11... | collective-permute-start | bytes 1572872 | tf_op jit(solution)/shard_map/ppermute | solution.py:745
  37.5 0.0 collective-permute-done.2.below
  37.5 15.0 %collective-permute-done.3.above = f32[336,128]{1,0:T(8,128)S(1)} collective-permute-done((f32[336,128]{1,0:T(8,128)S(1)}, f32[336,128]{1,0:T(8,128)S(1)}, u32[]{:S(2)}, u32[]{:S(2)}) %collective-permute-start.3) | collective-permute-done | bytes 172064 | tf_op jit(solution)/shard_map/ppermute | solution.py:745
  52.6 0.8 total.1
  53.3 4.8 %all-to-all-start = ((f32[8,96,128]{2,1,0:T(8,128)}), f32[8,96,128]{2,1,0:T(8,128)S(1)}, u32[]{:S(2)}, u32[]{:S(2)}) async-start(f32[8,96,128]{2,1,0:T(8,128)} %total.1), calls=%async_computation | async-start | bytes 786432 | tf_op jit(solution)/shard_map/all_to_all | solution.py:836
  58.1 3.1 %collective-permute-start.9 = (f32[2,128,512]{2,1,0:T(8,128)S(1)}, f32[2,128,512]{2,1,0:T(8,128)S(1)}, u32[]{:S(2)}, u32[]{:S(2)}) collective-permute-start(f32[2,128,512]{2,1,0:T(8,128)S(1)} %get-tuple-element.37), channel_id=1, source_target_pairs={{1,0},{2,1},{3,2},{4,3},{5,4},{6,5},{7,6},{9,8},{10,9},{11,10},{12... | collective-permute-start | bytes 1572872 | tf_op jit(solution)/shard_map/ppermute | solution.py:745
  61.2 0.9 join.1
  62.1 2.2 %collective-permute-start.4 = (f32[576,128]{1,0:T(8,128)}, f32[576,128]{1,0:T(8,128)S(1)}, u32[]{:S(2)}, u32[]{:S(2)}) collective-permute-start(f32[576,128]{1,0:T(8,128)} %get-tuple-element.31), channel_id=1, source_target_pairs={{0,1},{1,2},{2,3},{3,4},{4,5},{5,6},{6,7},{8,9},{9,10},{10,11},{11... | collective-permute-start | bytes 884744 | tf_op jit(solution)/shard_map/ppermute | solution.py:745
  64.3 4.0 %collective-permute-start.5 = (f32[576,128]{1,0:T(8,128)}, f32[576,128]{1,0:T(8,128)S(1)}, u32[]{:S(2)}, u32[]{:S(2)}) collective-permute-start(f32[576,128]{1,0:T(8,128)} %get-tuple-element.32), channel_id=1, source_target_pairs={{1,0},{2,1},{3,2},{4,3},{5,4},{6,5},{7,6},{9,8},{10,9},{11,10},{12... | collective-permute-start | bytes 884744 | tf_op jit(solution)/shard_map/ppermute | solution.py:745
  68.3 1.9 %collective-permute-start.6 = (f32[544,128]{1,0:T(8,128)}, f32[544,128]{1,0:T(8,128)S(1)}, u32[]{:S(2)}, u32[]{:S(2)}) collective-permute-start(f32[544,128]{1,0:T(8,128)} %copy-done), channel_id=1, source_target_pairs={{0,1},{1,2},{2,3},{3,4},{4,5},{5,6},{6,7},{8,9},{9,10},{10,11},{11... | collective-permute-start | bytes 835592 | tf_op jit(solution)/shard_map/ppermute | solution.py:745
  70.2 0.0 collective-permute-done.8.z_below
  70.3 4.3 %collective-permute-start.7 = (f32[544,128]{1,0:T(8,128)S(1)}, f32[544,128]{1,0:T(8,128)S(1)}, u32[]{:S(2)}, u32[]{:S(2)}) collective-permute-start(f32[544,128]{1,0:T(8,128)S(1)} %get-tuple-element.34), channel_id=1, source_target_pairs={{1,0},{2,1},{3,2},{4,3},{5,4},{6,5},{7,6},{9,8},{10,9},{11,10},{12... | collective-permute-start | bytes 835592 | tf_op jit(solution)/shard_map/ppermute | solution.py:745
  74.5 14.4 %collective-permute-done.9.z_above = f32[2,128,512]{2,1,0:T(8,128)S(1)} collective-permute-done((f32[2,128,512]{2,1,0:T(8,128)S(1)}, f32[2,128,512]{2,1,0:T(8,128)S(1)}, u32[]{:S(2)}, u32[]{:S(2)}) %collective-permute-start.9) | collective-permute-done | bytes 524320 | tf_op jit(solution)/shard_map/ppermute | solution.py:745
  88.9 0.8 copy-done.1
  89.7 5.9 %early.1 = (f32[2,4,160,128]{3,2,1,0:T(8,128)}, f32[6,4,160,128]{3,2,1,0:T(8,128)}) custom-call(s32[3,64]{1,0:T(4,128)} %bitcast.8, f32[8,4,144,128]{3,2,1,0:T(8,128)} %get-tuple-element.35.f_own, f32[2,128,512]{2,1,0:T(8,128)} %collective-permute-done.8.z_below, f32[2,128,512]{2,1,0:T(8,128)} %copy-done.1, f32[336,128]{1,0:T(8,128)S(1)} %collective-permute-done.2.below, ...), custom_call_target="tpu_custom_call" | custom-call | flops 20000000 | bytes 10000000 | tf_op jit(solution)/shard_map/early/pallas_call | solution.py:852
  95.6 0.0 all-to-all-done
  95.6 0.9 third.1
  96.5 6.5 %all-gather = f32[16,16,128]{2,1,0:T(8,128)S(1)} all-gather(f32[4,16,128]{2,1,0:T(8,128)S(1)} %third.1), channel_id=2, replica_groups=mesh['box'=4,'gz'=8] {'box'}, dimensions={0}, use_global_device_ids=true | all-gather | bytes 163840 | tf_op jit(solution)/shard_map/all_gather | solution.py:882
  103.0 3.6 %middle.1.e2p = f32[6,2,80,128]{3,2,1,0:T(8,128)S(1)} custom-call(f32[4,4,16,128]{3,2,1,0:T(8,128)S(1)} %bitcast.6, f32[16,48,128]{2,1,0:T(8,128)S(1)} %bitcast.5), custom_call_target="tpu_custom_call" | custom-call | flops 10000000 | bytes 2000000 | tf_op jit(solution)/shard_map/middle/pallas_call | solution.py:884
  106.5 0.0 collective-permute-done.6.late_below
  106.5 0.0 collective-permute-done.7.late_above
  106.6 0.0 collective-permute-done.4.below
  106.6 7.8 %tail.1 = f32[8,128,512]{2,1,0:T(8,128)} custom-call(f32[6,2,80,128]{3,2,1,0:T(8,128)S(1)} %middle.1.e2p, f32[4,2,80,128]{3,2,1,0:T(8,128)S(1)} %get-tuple-element.30.s1, f32[576,128]{1,0:T(8,128)S(1)} %collective-permute-done.4.below, f32[576,128]{1,0:T(8,128)S(1)} %collective-permute-done.5.above, f32[544,128]{1,0:T(8,128)S(1)} %collective-permute-done.6.late_below, ...), custom_call_target="tpu_custom_call" | custom-call | flops 40000000 | bytes 10000000 | tf_op jit(solution)/shard_map/tail/pallas_call | solution.py:896
  (4 shorter events, 0.0 us)
Async XLA Ops:
  1.7 17.0 %collective-permute-start = (f32[8,32,512]{2,1,0:T(8,128)S(1)}, f32[8,32,512]{2,1,0:T(8,128)S(1)}, u32[]{:S(2)}, u32[]{:S(2)}) collective-permute-start(f32[8,32,512]{2,1,0:T(8,128)S(1)} %get-tuple-element.23), channel_id=1, source_target_pairs={{0,8},{8,16},{16,24},{1,9},{9,17},{17,25},{2,10},{10,18},{18,26},{... | collective-permute-start | bytes 1572872 | tf_op jit(solution)/shard_map/ppermute | solution.py:745
  5.5 13.3 %collective-permute-start.1 = (f32[8,32,512]{2,1,0:T(8,128)S(1)}, f32[8,32,512]{2,1,0:T(8,128)S(1)}, u32[]{:S(2)}, u32[]{:S(2)}) collective-permute-start(f32[8,32,512]{2,1,0:T(8,128)S(1)} %get-tuple-element.24), channel_id=1, source_target_pairs={{8,0},{16,8},{24,16},{9,1},{17,9},{25,17},{10,2},{18,10},{26,18},{... | collective-permute-start | bytes 1572872 | tf_op jit(solution)/shard_map/ppermute | solution.py:745
  29.1 32.1 %copy-start = (f32[544,128]{1,0:T(8,128)}, f32[544,128]{1,0:T(8,128)S(1)}, u32[]{:S(2)}) copy-start(f32[544,128]{1,0:T(8,128)S(1)} %get-tuple-element.33) | copy-start | bytes 835588
  29.1 8.4 %collective-permute-start.2 = (f32[336,128]{1,0:T(8,128)S(1)}, f32[336,128]{1,0:T(8,128)S(1)}, u32[]{:S(2)}, u32[]{:S(2)}) collective-permute-start(f32[336,128]{1,0:T(8,128)S(1)} %get-tuple-element.27), channel_id=1, source_target_pairs={{0,1},{1,2},{2,3},{3,4},{4,5},{5,6},{6,7},{8,9},{9,10},{10,11},{11... | collective-permute-start | bytes 516104 | tf_op jit(solution)/shard_map/ppermute | solution.py:745
  32.2 20.4 %collective-permute-start.3 = (f32[336,128]{1,0:T(8,128)S(1)}, f32[336,128]{1,0:T(8,128)S(1)}, u32[]{:S(2)}, u32[]{:S(2)}) collective-permute-start(f32[336,128]{1,0:T(8,128)S(1)} %get-tuple-element.28), channel_id=1, source_target_pairs={{1,0},{2,1},{3,2},{4,3},{5,4},{6,5},{7,6},{9,8},{10,9},{11,10},{12... | collective-permute-start | bytes 516104 | tf_op jit(solution)/shard_map/ppermute | solution.py:745
  35.3 35.0 %collective-permute-start.8 = (f32[2,128,512]{2,1,0:T(8,128)S(1)}, f32[2,128,512]{2,1,0:T(8,128)}, u32[]{:S(2)}, u32[]{:S(2)}) collective-permute-start(f32[2,128,512]{2,1,0:T(8,128)S(1)} %get-tuple-element.36), channel_id=1, source_target_pairs={{0,1},{1,2},{2,3},{3,4},{4,5},{5,6},{6,7},{8,9},{9,10},{10,11},{11... | collective-permute-start | bytes 1572872 | tf_op jit(solution)/shard_map/ppermute | solution.py:745
  53.3 42.2 %all-to-all-start = ((f32[8,96,128]{2,1,0:T(8,128)}), f32[8,96,128]{2,1,0:T(8,128)S(1)}, u32[]{:S(2)}, u32[]{:S(2)}) async-start(f32[8,96,128]{2,1,0:T(8,128)} %total.1), calls=%async_computation | async-start | bytes 786432 | tf_op jit(solution)/shard_map/all_to_all | solution.py:836
  58.1 30.8 %collective-permute-start.9 = (f32[2,128,512]{2,1,0:T(8,128)S(1)}, f32[2,128,512]{2,1,0:T(8,128)S(1)}, u32[]{:S(2)}, u32[]{:S(2)}) collective-permute-start(f32[2,128,512]{2,1,0:T(8,128)S(1)} %get-tuple-element.37), channel_id=1, source_target_pairs={{1,0},{2,1},{3,2},{4,3},{5,4},{6,5},{7,6},{9,8},{10,9},{11,10},{12... | collective-permute-start | bytes 1572872 | tf_op jit(solution)/shard_map/ppermute | solution.py:745
  62.1 44.4 %collective-permute-start.4 = (f32[576,128]{1,0:T(8,128)}, f32[576,128]{1,0:T(8,128)S(1)}, u32[]{:S(2)}, u32[]{:S(2)}) collective-permute-start(f32[576,128]{1,0:T(8,128)} %get-tuple-element.31), channel_id=1, source_target_pairs={{0,1},{1,2},{2,3},{3,4},{4,5},{5,6},{6,7},{8,9},{9,10},{10,11},{11... | collective-permute-start | bytes 884744 | tf_op jit(solution)/shard_map/ppermute | solution.py:745
  64.3 42.3 %collective-permute-start.5 = (f32[576,128]{1,0:T(8,128)}, f32[576,128]{1,0:T(8,128)S(1)}, u32[]{:S(2)}, u32[]{:S(2)}) collective-permute-start(f32[576,128]{1,0:T(8,128)} %get-tuple-element.32), channel_id=1, source_target_pairs={{1,0},{2,1},{3,2},{4,3},{5,4},{6,5},{7,6},{9,8},{10,9},{11,10},{12... | collective-permute-start | bytes 884744 | tf_op jit(solution)/shard_map/ppermute | solution.py:745
  68.3 38.2 %collective-permute-start.6 = (f32[544,128]{1,0:T(8,128)}, f32[544,128]{1,0:T(8,128)S(1)}, u32[]{:S(2)}, u32[]{:S(2)}) collective-permute-start(f32[544,128]{1,0:T(8,128)} %copy-done), channel_id=1, source_target_pairs={{0,1},{1,2},{2,3},{3,4},{4,5},{5,6},{6,7},{8,9},{9,10},{10,11},{11... | collective-permute-start | bytes 835592 | tf_op jit(solution)/shard_map/ppermute | solution.py:745
  70.3 36.3 %collective-permute-start.7 = (f32[544,128]{1,0:T(8,128)S(1)}, f32[544,128]{1,0:T(8,128)S(1)}, u32[]{:S(2)}, u32[]{:S(2)}) collective-permute-start(f32[544,128]{1,0:T(8,128)S(1)} %get-tuple-element.34), channel_id=1, source_target_pairs={{1,0},{2,1},{3,2},{4,3},{5,4},{6,5},{7,6},{9,8},{10,9},{11,10},{12... | collective-permute-start | bytes 835592 | tf_op jit(solution)/shard_map/ppermute | solution.py:745
  88.9 0.8 copy-start.1

commit v5 on v4

--- a/solution.py
+++ b/solution.py
@@ -380,7 +380,7 @@
     f_copy = pltpu.make_async_copy(fb.at[pl.ds(2, n0), :, inner, :], f_own, out_sem.at[0])
     f_copy.start()
 
-    relax(vb, 3, (-1, n0 + 1), fb, 2, rows0, HX, edges, n0, s_planes=(0, n0), unroll=2)
+    relax(vb, 3, (-1, n0 + 1), fb, 2, rows0, HX, edges, n0, s_planes=(0, n0), unroll=3)
     v_copy = pltpu.make_async_copy(vb.at[pl.ds(4, n0 - 2), :, inner, :], v_own, out_sem.at[1])
     v_copy.start()
 
@@ -705,8 +705,8 @@
                         at = pl.ds(start, size1, stride=2)
                         va[plane, 2 * group + b, at, :] = va[plane, 2 * group + b, at, :] + part
 
-    each(e1.shape[0], prolong, unroll=2)
-    relax(vb, 3, (-1, n0 + 1), fb, 1, rows, HU, edges, n0, old=va, ooff=3, unroll=2)
+    each(e1.shape[0], prolong, unroll=3)
+    relax(vb, 3, (-1, n0 + 1), fb, 1, rows, HU, edges, n0, old=va, ooff=3, unroll=5)
 
     def last(z):
         view = ob.at[pl.ds(z, 1)]
@@ -714,7 +714,7 @@
         for copy in block_copies(out.at[pl.ds(z, 1)], ob, (z, 1), 0, x0, out_sem, back=True):
             copy.start()
 
-    each(n0, last, unroll=2)
+    each(n0, last, unroll=4)
     for copy in block_copies(out, ob, (0, n0), 0, x0, out_sem, back=True):
         copy.wait()
 

time: 115 us -> 114 us (level)
  no operation moved by 1% of the time
where the time goes in v5:
time: 114 us
  starting transfers between devices  34.2 us (30%)
  Pallas kernels  31.3 us (27%)
  waiting for transfers between devices  29.4 us (26%)
  blocking collectives  17.8 us (16%)
    ppermute x10, starting transfers between devices, shift_by(): return lax.ppermute(array, axis, pairs)  29.5 us
    ppermute x10, waiting for transfers between devices, shift_by(): return lax.ppermute(array, axis, pairs)  29.4 us
    all_gather x1, blocking collectives, per_device(): packed = lax.all_gather(packed, 'box', axis=0, tiled=True)  11.3 us
    pallas_call x1, Pallas kernels, per_device(): pl.pallas_call(functools.partial(down_kernel, boxes, slabs, n0, x0), name...  10.2 us
    pallas_call x1, Pallas kernels, per_device(): pl.pallas_call(functools.partial(tail_kernel, boxes, slabs, n0, x0), name...  7.27 us
    all_gather x1, blocking collectives, per_device(): s3 = lax.all_gather(s3, 'box', axis=0)  6.47 us
    pallas_call x1, Pallas kernels, per_device(): pl.pallas_call(functools.partial(early_kernel, boxes, slabs, n0, x0, rim)...  5.86 us
    all_to_all x1, starting transfers between devices, per_device(): s2 = lax.all_to_all(copies, 'gz', split_axis=0, concat_axis=0, tiled=True)  4.76 us
  transfers between devices with their start and end apart: 11, of which 2 were waited for; matrix products, arithmetic and copies ran while one was open for 0% of the time, Pallas kernels for 11%

profile of v5, /device:TPU:9, one launch (start us, length us, event | category | flops | bytes accessed | tf_op | source)
XLA Modules:
  0.0 113.8 jit_solution(17572704076672094900)
XLA Ops:
  0.0 1.7 %pack.1 = (f32[128,128]{1,0:T(8,128)S(1)}, f32[8,32,512]{2,1,0:T(8,128)S(1)}, f32[8,32,512]{2,1,0:T(8,128)S(1)}, f32[2,128,512]{2,1,0:T(8,128)S(1)}, f32[2,128,512]{2,1,0:T(8,128)S(1)}) custom-call(s32[4,64]{1,0:T(4,128)} %bitcast.9, f32[16,16,256]{2,1,0:T(8,128)} %fine.1, f32[16,16,128]{2,1,0:T(8,128)} %flux.1, f32[8,128,512]{2,1,0:T(8,128)} %coarse.3), custom_call_target="tpu_custom_call" | custom-call | flops 10000000 | bytes 1000000 | tf_op jit(solution)/shard_map/pack/pallas_call | solution.py:761
  1.7 3.7 %collective-permute-start = (f32[8,32,512]{2,1,0:T(8,128)S(1)}, f32[8,32,512]{2,1,0:T(8,128)S(1)}, u32[]{:S(2)}, u32[]{:S(2)}) collective-permute-start(f32[8,32,512]{2,1,0:T(8,128)S(1)} %get-tuple-element.23), channel_id=1, source_target_pairs={{0,8},{8,16},{16,24},{1,9},{9,17},{17,25},{2,10},{10,18},{18,26},{... | collective-permute-start | bytes 1572872 | tf_op jit(solution)/shard_map/ppermute | solution.py:745
  5.5 1.9 %collective-permute-start.1 = (f32[8,32,512]{2,1,0:T(8,128)S(1)}, f32[8,32,512]{2,1,0:T(8,128)S(1)}, u32[]{:S(2)}, u32[]{:S(2)}) collective-permute-start(f32[8,32,512]{2,1,0:T(8,128)S(1)} %get-tuple-element.24), channel_id=1, source_target_pairs={{8,0},{16,8},{24,16},{9,1},{17,9},{25,17},{10,2},{18,10},{26,18},{... | collective-permute-start | bytes 1572872 | tf_op jit(solution)/shard_map/ppermute | solution.py:745
  7.4 11.3 %all_gather.9.packed = f32[512,128]{1,0:T(8,128)S(1)} all-gather(f32[128,128]{1,0:T(8,128)S(1)} %get-tuple-element.25), channel_id=1, replica_groups=mesh['box'=4,'gz'=8] {'box'}, dimensions={0}, use_global_device_ids=true | all-gather | bytes 327680 | tf_op jit(solution)/shard_map/all_gather | solution.py:787
  18.7 0.0 collective-permute-done.x_low
  18.7 0.0 collective-permute-done.1.x_high
  18.7 10.2 %down.1 = (f32[8,4,144,128]{3,2,1,0:T(8,128)}, f32[6,4,144,128]{3,2,1,0:T(8,128)}, f32[6,2,80,128]{3,2,1,0:T(8,128)S(1)}, f32[6,1,48,128]{3,2,1,0:T(8,128)S(1)},...) custom-call(s32[3,64]{1,0:T(4,128)} %bitcast.7, ...), custom_call_target="tpu_custom_call" | custom-call | flops 30000000 | bytes 10000000 | tf_op jit(solution)/shard_map/down/pallas_call | solution.py:792
  29.0 3.1 %collective-permute-start.2 = (f32[336,128]{1,0:T(8,128)S(1)}, f32[336,128]{1,0:T(8,128)S(1)}, u32[]{:S(2)}, u32[]{:S(2)}) collective-permute-start(f32[336,128]{1,0:T(8,128)S(1)} %get-tuple-element.27), channel_id=1, source_target_pairs={{0,1},{1,2},{2,3},{3,4},{4,5},{5,6},{6,7},{8,9},{9,10},{10,11},{11... | collective-permute-start | bytes 516104 | tf_op jit(solution)/shard_map/ppermute | solution.py:745
  32.1 3.1 %collective-permute-start.3 = (f32[336,128]{1,0:T(8,128)S(1)}, f32[336,128]{1,0:T(8,128)S(1)}, u32[]{:S(2)}, u32[]{:S(2)}) collective-permute-start(f32[336,128]{1,0:T(8,128)S(1)} %get-tuple-element.28), channel_id=1, source_target_pairs={{1,0},{2,1},{3,2},{4,3},{5,4},{6,5},{7,6},{9,8},{10,9},{11,10},{12... | collective-permute-start | bytes 516104 | tf_op jit(solution)/shard_map/ppermute | solution.py:745
  35.2 2.2 %collective-permute-start.8 = (f32[2,128,512]{2,1,0:T(8,128)S(1)}, f32[2,128,512]{2,1,0:T(8,128)}, u32[]{:S(2)}, u32[]{:S(2)}) collective-permute-start(f32[2,128,512]{2,1,0:T(8,128)S(1)} %get-tuple-element.36), channel_id=1, source_target_pairs={{0,1},{1,2},{2,3},{3,4},{4,5},{5,6},{6,7},{8,9},{9,10},{10,11},{11... | collective-permute-start | bytes 1572872 | tf_op jit(solution)/shard_map/ppermute | solution.py:745
  37.4 0.0 collective-permute-done.2.below
  37.4 15.0 %collective-permute-done.3.above = f32[336,128]{1,0:T(8,128)S(1)} collective-permute-done((f32[336,128]{1,0:T(8,128)S(1)}, f32[336,128]{1,0:T(8,128)S(1)}, u32[]{:S(2)}, u32[]{:S(2)}) %collective-permute-start.3) | collective-permute-done | bytes 172064 | tf_op jit(solution)/shard_map/ppermute | solution.py:745
  52.5 0.8 total.1
  53.2 4.8 %all-to-all-start = ((f32[8,96,128]{2,1,0:T(8,128)}), f32[8,96,128]{2,1,0:T(8,128)S(1)}, u32[]{:S(2)}, u32[]{:S(2)}) async-start(f32[8,96,128]{2,1,0:T(8,128)} %total.1), calls=%async_computation | async-start | bytes 786432 | tf_op jit(solution)/shard_map/all_to_all | solution.py:836
  58.0 3.1 %collective-permute-start.9 = (f32[2,128,512]{2,1,0:T(8,128)S(1)}, f32[2,128,512]{2,1,0:T(8,128)S(1)}, u32[]{:S(2)}, u32[]{:S(2)}) collective-permute-start(f32[2,128,512]{2,1,0:T(8,128)S(1)} %get-tuple-element.37), channel_id=1, source_target_pairs={{1,0},{2,1},{3,2},{4,3},{5,4},{6,5},{7,6},{9,8},{10,9},{11,10},{12... | collective-permute-start | bytes 1572872 | tf_op jit(solution)/shard_map/ppermute | solution.py:745
  61.1 0.9 join.1
  62.0 2.2 %collective-permute-start.4 = (f32[576,128]{1,0:T(8,128)}, f32[576,128]{1,0:T(8,128)S(1)}, u32[]{:S(2)}, u32[]{:S(2)}) collective-permute-start(f32[576,128]{1,0:T(8,128)} %get-tuple-element.31), channel_id=1, source_target_pairs={{0,1},{1,2},{2,3},{3,4},{4,5},{5,6},{6,7},{8,9},{9,10},{10,11},{11... | collective-permute-start | bytes 884744 | tf_op jit(solution)/shard_map/ppermute | solution.py:745
  64.2 4.0 %collective-permute-start.5 = (f32[576,128]{1,0:T(8,128)}, f32[576,128]{1,0:T(8,128)S(1)}, u32[]{:S(2)}, u32[]{:S(2)}) collective-permute-start(f32[576,128]{1,0:T(8,128)} %get-tuple-element.32), channel_id=1, source_target_pairs={{1,0},{2,1},{3,2},{4,3},{5,4},{6,5},{7,6},{9,8},{10,9},{11,10},{12... | collective-permute-start | bytes 884744 | tf_op jit(solution)/shard_map/ppermute | solution.py:745
  68.2 1.9 %collective-permute-start.6 = (f32[544,128]{1,0:T(8,128)}, f32[544,128]{1,0:T(8,128)S(1)}, u32[]{:S(2)}, u32[]{:S(2)}) collective-permute-start(f32[544,128]{1,0:T(8,128)} %copy-done), channel_id=1, source_target_pairs={{0,1},{1,2},{2,3},{3,4},{4,5},{5,6},{6,7},{8,9},{9,10},{10,11},{11... | collective-permute-start | bytes 835592 | tf_op jit(solution)/shard_map/ppermute | solution.py:745
  70.2 0.0 collective-permute-done.8.z_below
  70.2 4.3 %collective-permute-start.7 = (f32[544,128]{1,0:T(8,128)S(1)}, f32[544,128]{1,0:T(8,128)S(1)}, u32[]{:S(2)}, u32[]{:S(2)}) collective-permute-start(f32[544,128]{1,0:T(8,128)S(1)} %get-tuple-element.34), channel_id=1, source_target_pairs={{1,0},{2,1},{3,2},{4,3},{5,4},{6,5},{7,6},{9,8},{10,9},{11,10},{12... | collective-permute-start | bytes 835592 | tf_op jit(solution)/shard_map/ppermute | solution.py:745
  74.4 14.4 %collective-permute-done.9.z_above = f32[2,128,512]{2,1,0:T(8,128)S(1)} collective-permute-done((f32[2,128,512]{2,1,0:T(8,128)S(1)}, f32[2,128,512]{2,1,0:T(8,128)S(1)}, u32[]{:S(2)}, u32[]{:S(2)}) %collective-permute-start.9) | collective-permute-done | bytes 524320 | tf_op jit(solution)/shard_map/ppermute | solution.py:745
  88.8 0.8 copy-done.1
  89.6 5.9 %early.1 = (f32[2,4,160,128]{3,2,1,0:T(8,128)}, f32[6,4,160,128]{3,2,1,0:T(8,128)}) custom-call(s32[3,64]{1,0:T(4,128)} %bitcast.8, f32[8,4,144,128]{3,2,1,0:T(8,128)} %get-tuple-element.35.f_own, f32[2,128,512]{2,1,0:T(8,128)} %collective-permute-done.8.z_below, f32[2,128,512]{2,1,0:T(8,128)} %copy-done.1, f32[336,128]{1,0:T(8,128)S(1)} %collective-permute-done.2.below, ...), custom_call_target="tpu_custom_call" | custom-call | flops 20000000 | bytes 10000000 | tf_op jit(solution)/shard_map/early/pallas_call | solution.py:852
  95.5 0.0 all-to-all-done
  95.5 0.9 third.1
  96.4 6.5 %all-gather = f32[16,16,128]{2,1,0:T(8,128)S(1)} all-gather(f32[4,16,128]{2,1,0:T(8,128)S(1)} %third.1), channel_id=2, replica_groups=mesh['box'=4,'gz'=8] {'box'}, dimensions={0}, use_global_device_ids=true | all-gather | bytes 163840 | tf_op jit(solution)/shard_map/all_gather | solution.py:882
  102.9 3.6 %middle.1.e2p = f32[6,2,80,128]{3,2,1,0:T(8,128)S(1)} custom-call(f32[4,4,16,128]{3,2,1,0:T(8,128)S(1)} %bitcast.6, f32[16,48,128]{2,1,0:T(8,128)S(1)} %bitcast.5), custom_call_target="tpu_custom_call" | custom-call | flops 10000000 | bytes 2000000 | tf_op jit(solution)/shard_map/middle/pallas_call | solution.py:884
  106.5 0.0 collective-permute-done.6.late_below
  106.5 0.0 collective-permute-done.7.late_above
  106.5 0.0 collective-permute-done.5.above
  106.5 7.3 %tail.1 = f32[8,128,512]{2,1,0:T(8,128)} custom-call(f32[6,2,80,128]{3,2,1,0:T(8,128)S(1)} %middle.1.e2p, f32[4,2,80,128]{3,2,1,0:T(8,128)S(1)} %get-tuple-element.30.s1, f32[576,128]{1,0:T(8,128)S(1)} %collective-permute-done.4.below, f32[576,128]{1,0:T(8,128)S(1)} %collective-permute-done.5.above, f32[544,128]{1,0:T(8,128)S(1)} %collective-permute-done.6.late_below, ...), custom_call_target="tpu_custom_call" | custom-call | flops 40000000 | bytes 10000000 | tf_op jit(solution)/shard_map/tail/pallas_call | solution.py:896
  (4 shorter events, 0.0 us)
Async XLA Ops:
  1.7 17.0 %collective-permute-start = (f32[8,32,512]{2,1,0:T(8,128)S(1)}, f32[8,32,512]{2,1,0:T(8,128)S(1)}, u32[]{:S(2)}, u32[]{:S(2)}) collective-permute-start(f32[8,32,512]{2,1,0:T(8,128)S(1)} %get-tuple-element.23), channel_id=1, source_target_pairs={{0,8},{8,16},{16,24},{1,9},{9,17},{17,25},{2,10},{10,18},{18,26},{... | collective-permute-start | bytes 1572872 | tf_op jit(solution)/shard_map/ppermute | solution.py:745
  5.5 13.3 %collective-permute-start.1 = (f32[8,32,512]{2,1,0:T(8,128)S(1)}, f32[8,32,512]{2,1,0:T(8,128)S(1)}, u32[]{:S(2)}, u32[]{:S(2)}) collective-permute-start(f32[8,32,512]{2,1,0:T(8,128)S(1)} %get-tuple-element.24), channel_id=1, source_target_pairs={{8,0},{16,8},{24,16},{9,1},{17,9},{25,17},{10,2},{18,10},{26,18},{... | collective-permute-start | bytes 1572872 | tf_op jit(solution)/shard_map/ppermute | solution.py:745
  29.0 32.1 %copy-start = (f32[544,128]{1,0:T(8,128)}, f32[544,128]{1,0:T(8,128)S(1)}, u32[]{:S(2)}) copy-start(f32[544,128]{1,0:T(8,128)S(1)} %get-tuple-element.33) | copy-start | bytes 835588
  29.0 8.4 %collective-permute-start.2 = (f32[336,128]{1,0:T(8,128)S(1)}, f32[336,128]{1,0:T(8,128)S(1)}, u32[]{:S(2)}, u32[]{:S(2)}) collective-permute-start(f32[336,128]{1,0:T(8,128)S(1)} %get-tuple-element.27), channel_id=1, source_target_pairs={{0,1},{1,2},{2,3},{3,4},{4,5},{5,6},{6,7},{8,9},{9,10},{10,11},{11... | collective-permute-start | bytes 516104 | tf_op jit(solution)/shard_map/ppermute | solution.py:745
  32.1 20.4 %collective-permute-start.3 = (f32[336,128]{1,0:T(8,128)S(1)}, f32[336,128]{1,0:T(8,128)S(1)}, u32[]{:S(2)}, u32[]{:S(2)}) collective-permute-start(f32[336,128]{1,0:T(8,128)S(1)} %get-tuple-element.28), channel_id=1, source_target_pairs={{1,0},{2,1},{3,2},{4,3},{5,4},{6,5},{7,6},{9,8},{10,9},{11,10},{12... | collective-permute-start | bytes 516104 | tf_op jit(solution)/shard_map/ppermute | solution.py:745
  35.2 35.0 %collective-permute-start.8 = (f32[2,128,512]{2,1,0:T(8,128)S(1)}, f32[2,128,512]{2,1,0:T(8,128)}, u32[]{:S(2)}, u32[]{:S(2)}) collective-permute-start(f32[2,128,512]{2,1,0:T(8,128)S(1)} %get-tuple-element.36), channel_id=1, source_target_pairs={{0,1},{1,2},{2,3},{3,4},{4,5},{5,6},{6,7},{8,9},{9,10},{10,11},{11... | collective-permute-start | bytes 1572872 | tf_op jit(solution)/shard_map/ppermute | solution.py:745
  53.2 42.2 %all-to-all-start = ((f32[8,96,128]{2,1,0:T(8,128)}), f32[8,96,128]{2,1,0:T(8,128)S(1)}, u32[]{:S(2)}, u32[]{:S(2)}) async-start(f32[8,96,128]{2,1,0:T(8,128)} %total.1), calls=%async_computation | async-start | bytes 786432 | tf_op jit(solution)/shard_map/all_to_all | solution.py:836
  58.0 30.8 %collective-permute-start.9 = (f32[2,128,512]{2,1,0:T(8,128)S(1)}, f32[2,128,512]{2,1,0:T(8,128)S(1)}, u32[]{:S(2)}, u32[]{:S(2)}) collective-permute-start(f32[2,128,512]{2,1,0:T(8,128)S(1)} %get-tuple-element.37), channel_id=1, source_target_pairs={{1,0},{2,1},{3,2},{4,3},{5,4},{6,5},{7,6},{9,8},{10,9},{11,10},{12... | collective-permute-start | bytes 1572872 | tf_op jit(solution)/shard_map/ppermute | solution.py:745
  62.0 44.4 %collective-permute-start.4 = (f32[576,128]{1,0:T(8,128)}, f32[576,128]{1,0:T(8,128)S(1)}, u32[]{:S(2)}, u32[]{:S(2)}) collective-permute-start(f32[576,128]{1,0:T(8,128)} %get-tuple-element.31), channel_id=1, source_target_pairs={{0,1},{1,2},{2,3},{3,4},{4,5},{5,6},{6,7},{8,9},{9,10},{10,11},{11... | collective-permute-start | bytes 884744 | tf_op jit(solution)/shard_map/ppermute | solution.py:745
  64.2 42.3 %collective-permute-start.5 = (f32[576,128]{1,0:T(8,128)}, f32[576,128]{1,0:T(8,128)S(1)}, u32[]{:S(2)}, u32[]{:S(2)}) collective-permute-start(f32[576,128]{1,0:T(8,128)} %get-tuple-element.32), channel_id=1, source_target_pairs={{1,0},{2,1},{3,2},{4,3},{5,4},{6,5},{7,6},{9,8},{10,9},{11,10},{12... | collective-permute-start | bytes 884744 | tf_op jit(solution)/shard_map/ppermute | solution.py:745
  68.2 38.2 %collective-permute-start.6 = (f32[544,128]{1,0:T(8,128)}, f32[544,128]{1,0:T(8,128)S(1)}, u32[]{:S(2)}, u32[]{:S(2)}) collective-permute-start(f32[544,128]{1,0:T(8,128)} %copy-done), channel_id=1, source_target_pairs={{0,1},{1,2},{2,3},{3,4},{4,5},{5,6},{6,7},{8,9},{9,10},{10,11},{11... | collective-permute-start | bytes 835592 | tf_op jit(solution)/shard_map/ppermute | solution.py:745
  70.2 36.3 %collective-permute-start.7 = (f32[544,128]{1,0:T(8,128)S(1)}, f32[544,128]{1,0:T(8,128)S(1)}, u32[]{:S(2)}, u32[]{:S(2)}) collective-permute-start(f32[544,128]{1,0:T(8,128)S(1)} %get-tuple-element.34), channel_id=1, source_target_pairs={{1,0},{2,1},{3,2},{4,3},{5,4},{6,5},{7,6},{9,8},{10,9},{11,10},{12... | collective-permute-start | bytes 835592 | tf_op jit(solution)/shard_map/ppermute | solution.py:745
  88.8 0.8 copy-start.1

commit v6 on v5

--- a/solution.py
+++ b/solution.py
@@ -569,9 +569,9 @@
         return e3p[index >> 1, first : first + size, :]
 
     h2 = HX // 4
-    relax(v2a, 5, (-4, n2 + 4), f2, 5, rows2, h2, edges, n2, extra=extra2, chunk=32, unroll=2)
-    relax(v2b, 5, (-3, n2 + 3), f2, 5, rows2, h2, edges, n2, old=v2a, ooff=5, chunk=32, unroll=2)
-    relax(v2a, 5, (-2, n2 + 2), f2, 5, rows2, h2, edges, n2, old=v2b, ooff=5, chunk=32, unroll=2)
+    relax(v2a, 5, (-4, n2 + 4), f2, 5, rows2, h2, edges, n2, extra=extra2, chunk=32, unroll=5)
+    relax(v2b, 5, (-3, n2 + 3), f2, 5, rows2, h2, edges, n2, old=v2a, ooff=5, chunk=32, unroll=4)
+    relax(v2a, 5, (-2, n2 + 2), f2, 5, rows2, h2, edges, n2, old=v2b, ooff=5, chunk=32, unroll=3)
 
     cut = h2 - HU // 2
     matrix2 = copy_matrix(LANES)
@@ -598,9 +598,9 @@
     def extra1(index, b, first, size):
         return e2p[(index + 1) >> 1, b, first : first + size, :]
 
-    relax(v1a, 4, (-3, n1 + 3), f1, 4, rows1, HU, edges, n1, extra=extra1, unroll=2)
-    relax(v1b, 4, (-2, n1 + 2), f1, 4, rows1, HU, edges, n1, old=v1a, ooff=4, unroll=2)
-    relax(e1, 1, (-1, n1 + 1), f1, 4, rows1, HU, edges, n1, old=v1b, ooff=4, shift=0, unroll=2)
+    relax(v1a, 4, (-3, n1 + 3), f1, 4, rows1, HU, edges, n1, extra=extra1, unroll=5)
+    relax(v1b, 4, (-2, n1 + 2), f1, 4, rows1, HU, edges, n1, old=v1a, ooff=4, unroll=4)
+    relax(e1, 1, (-1, n1 + 1), f1, 4, rows1, HU, edges, n1, old=v1b, ooff=4, shift=0, unroll=3)
 
 
 def early_kernel(

time: 114 us -> 114 us (level)
  transfers between devices with their start and end apart: 11 -> 11, of which waited for: 2 -> 2; matrix products, arithmetic and copies ran while one was open for 0% -> 0% of each run, Pallas kernels for 11% -> 10%
where the time goes in v6:
time: 114 us; the launch traced here: 113 us
  starting transfers between devices  34.2 us (30%)
  Pallas kernels  30.8 us (27%)
  waiting for transfers between devices  29.4 us (26%)
  blocking collectives  17.8 us (16%)
    ppermute x10, starting transfers between devices, shift_by(): return lax.ppermute(array, axis, pairs)  29.5 us
    ppermute x10, waiting for transfers between devices, shift_by(): return lax.ppermute(array, axis, pairs)  29.4 us
    all_gather x1, blocking collectives, per_device(): packed = lax.all_gather(packed, 'box', axis=0, tiled=True)  11.3 us
    pallas_call x1, Pallas kernels, per_device(): pl.pallas_call(functools.partial(down_kernel, boxes, slabs, n0, x0), name...  10.2 us
    pallas_call x1, Pallas kernels, per_device(): pl.pallas_call(functools.partial(tail_kernel, boxes, slabs, n0, x0), name...  7.27 us
    all_gather x1, blocking collectives, per_device(): s3 = lax.all_gather(s3, 'box', axis=0)  6.47 us
    pallas_call x1, Pallas kernels, per_device(): pl.pallas_call(functools.partial(early_kernel, boxes, slabs, n0, x0, rim)...  5.86 us
    all_to_all x1, starting transfers between devices, per_device(): s2 = lax.all_to_all(copies, 'gz', split_axis=0, concat_axis=0, tiled=True)  4.76 us
  transfers between devices with their start and end apart: 11, of which 2 were waited for; matrix products, arithmetic and copies ran while one was open for 0% of the time, Pallas kernels for 10%

profile of v6, /device:TPU:9, one launch (start us, length us, event | category | flops | bytes accessed | tf_op | source)
XLA Modules:
  0.0 113.3 jit_solution(10346678213468176799)
XLA Ops:
  0.0 1.7 %pack.1 = (f32[128,128]{1,0:T(8,128)S(1)}, f32[8,32,512]{2,1,0:T(8,128)S(1)}, f32[8,32,512]{2,1,0:T(8,128)S(1)}, f32[2,128,512]{2,1,0:T(8,128)S(1)}, f32[2,128,512]{2,1,0:T(8,128)S(1)}) custom-call(s32[4,64]{1,0:T(4,128)} %bitcast.9, f32[16,16,256]{2,1,0:T(8,128)} %fine.1, f32[16,16,128]{2,1,0:T(8,128)} %flux.1, f32[8,128,512]{2,1,0:T(8,128)} %coarse.3), custom_call_target="tpu_custom_call" | custom-call | flops 10000000 | bytes 1000000 | tf_op jit(solution)/shard_map/pack/pallas_call | solution.py:761
  1.7 3.7 %collective-permute-start = (f32[8,32,512]{2,1,0:T(8,128)S(1)}, f32[8,32,512]{2,1,0:T(8,128)S(1)}, u32[]{:S(2)}, u32[]{:S(2)}) collective-permute-start(f32[8,32,512]{2,1,0:T(8,128)S(1)} %get-tuple-element.23), channel_id=1, source_target_pairs={{0,8},{8,16},{16,24},{1,9},{9,17},{17,25},{2,10},{10,18},{18,26},{... | collective-permute-start | bytes 1572872 | tf_op jit(solution)/shard_map/ppermute | solution.py:745
  5.5 1.9 %collective-permute-start.1 = (f32[8,32,512]{2,1,0:T(8,128)S(1)}, f32[8,32,512]{2,1,0:T(8,128)S(1)}, u32[]{:S(2)}, u32[]{:S(2)}) collective-permute-start(f32[8,32,512]{2,1,0:T(8,128)S(1)} %get-tuple-element.24), channel_id=1, source_target_pairs={{8,0},{16,8},{24,16},{9,1},{17,9},{25,17},{10,2},{18,10},{26,18},{... | collective-permute-start | bytes 1572872 | tf_op jit(solution)/shard_map/ppermute | solution.py:745
  7.4 11.3 %all_gather.9.packed = f32[512,128]{1,0:T(8,128)S(1)} all-gather(f32[128,128]{1,0:T(8,128)S(1)} %get-tuple-element.25), channel_id=1, replica_groups=mesh['box'=4,'gz'=8] {'box'}, dimensions={0}, use_global_device_ids=true | all-gather | bytes 327680 | tf_op jit(solution)/shard_map/all_gather | solution.py:787
  18.7 0.0 collective-permute-done.x_low
  18.7 0.0 collective-permute-done.1.x_high
  18.7 10.2 %down.1 = (f32[8,4,144,128]{3,2,1,0:T(8,128)}, f32[6,4,144,128]{3,2,1,0:T(8,128)}, f32[6,2,80,128]{3,2,1,0:T(8,128)S(1)}, f32[6,1,48,128]{3,2,1,0:T(8,128)S(1)},...) custom-call(s32[3,64]{1,0:T(4,128)} %bitcast.7, ...), custom_call_target="tpu_custom_call" | custom-call | flops 30000000 | bytes 10000000 | tf_op jit(solution)/shard_map/down/pallas_call | solution.py:792
  29.0 3.1 %collective-permute-start.2 = (f32[336,128]{1,0:T(8,128)S(1)}, f32[336,128]{1,0:T(8,128)S(1)}, u32[]{:S(2)}, u32[]{:S(2)}) collective-permute-start(f32[336,128]{1,0:T(8,128)S(1)} %get-tuple-element.27), channel_id=1, source_target_pairs={{0,1},{1,2},{2,3},{3,4},{4,5},{5,6},{6,7},{8,9},{9,10},{10,11},{11... | collective-permute-start | bytes 516104 | tf_op jit(solution)/shard_map/ppermute | solution.py:745
  32.1 3.1 %collective-permute-start.3 = (f32[336,128]{1,0:T(8,128)S(1)}, f32[336,128]{1,0:T(8,128)S(1)}, u32[]{:S(2)}, u32[]{:S(2)}) collective-permute-start(f32[336,128]{1,0:T(8,128)S(1)} %get-tuple-element.28), channel_id=1, source_target_pairs={{1,0},{2,1},{3,2},{4,3},{5,4},{6,5},{7,6},{9,8},{10,9},{11,10},{12... | collective-permute-start | bytes 516104 | tf_op jit(solution)/shard_map/ppermute | solution.py:745
  35.2 2.2 %collective-permute-start.8 = (f32[2,128,512]{2,1,0:T(8,128)S(1)}, f32[2,128,512]{2,1,0:T(8,128)}, u32[]{:S(2)}, u32[]{:S(2)}) collective-permute-start(f32[2,128,512]{2,1,0:T(8,128)S(1)} %get-tuple-element.36), channel_id=1, source_target_pairs={{0,1},{1,2},{2,3},{3,4},{4,5},{5,6},{6,7},{8,9},{9,10},{10,11},{11... | collective-permute-start | bytes 1572872 | tf_op jit(solution)/shard_map/ppermute | solution.py:745
  37.4 0.0 collective-permute-done.2.below
  37.4 15.0 %collective-permute-done.3.above = f32[336,128]{1,0:T(8,128)S(1)} collective-permute-done((f32[336,128]{1,0:T(8,128)S(1)}, f32[336,128]{1,0:T(8,128)S(1)}, u32[]{:S(2)}, u32[]{:S(2)}) %collective-permute-start.3) | collective-permute-done | bytes 172064 | tf_op jit(solution)/shard_map/ppermute | solution.py:745
  52.5 0.8 total.1
  53.2 4.8 %all-to-all-start = ((f32[8,96,128]{2,1,0:T(8,128)}), f32[8,96,128]{2,1,0:T(8,128)S(1)}, u32[]{:S(2)}, u32[]{:S(2)}) async-start(f32[8,96,128]{2,1,0:T(8,128)} %total.1), calls=%async_computation | async-start | bytes 786432 | tf_op jit(solution)/shard_map/all_to_all | solution.py:836
  58.0 3.1 %collective-permute-start.9 = (f32[2,128,512]{2,1,0:T(8,128)S(1)}, f32[2,128,512]{2,1,0:T(8,128)S(1)}, u32[]{:S(2)}, u32[]{:S(2)}) collective-permute-start(f32[2,128,512]{2,1,0:T(8,128)S(1)} %get-tuple-element.37), channel_id=1, source_target_pairs={{1,0},{2,1},{3,2},{4,3},{5,4},{6,5},{7,6},{9,8},{10,9},{11,10},{12... | collective-permute-start | bytes 1572872 | tf_op jit(solution)/shard_map/ppermute | solution.py:745
  61.1 0.9 join.1
  62.0 2.2 %collective-permute-start.4 = (f32[576,128]{1,0:T(8,128)}, f32[576,128]{1,0:T(8,128)S(1)}, u32[]{:S(2)}, u32[]{:S(2)}) collective-permute-start(f32[576,128]{1,0:T(8,128)} %get-tuple-element.31), channel_id=1, source_target_pairs={{0,1},{1,2},{2,3},{3,4},{4,5},{5,6},{6,7},{8,9},{9,10},{10,11},{11... | collective-permute-start | bytes 884744 | tf_op jit(solution)/shard_map/ppermute | solution.py:745
  64.2 4.0 %collective-permute-start.5 = (f32[576,128]{1,0:T(8,128)}, f32[576,128]{1,0:T(8,128)S(1)}, u32[]{:S(2)}, u32[]{:S(2)}) collective-permute-start(f32[576,128]{1,0:T(8,128)} %get-tuple-element.32), channel_id=1, source_target_pairs={{1,0},{2,1},{3,2},{4,3},{5,4},{6,5},{7,6},{9,8},{10,9},{11,10},{12... | collective-permute-start | bytes 884744 | tf_op jit(solution)/shard_map/ppermute | solution.py:745
  68.2 1.9 %collective-permute-start.6 = (f32[544,128]{1,0:T(8,128)}, f32[544,128]{1,0:T(8,128)S(1)}, u32[]{:S(2)}, u32[]{:S(2)}) collective-permute-start(f32[544,128]{1,0:T(8,128)} %copy-done), channel_id=1, source_target_pairs={{0,1},{1,2},{2,3},{3,4},{4,5},{5,6},{6,7},{8,9},{9,10},{10,11},{11... | collective-permute-start | bytes 835592 | tf_op jit(solution)/shard_map/ppermute | solution.py:745
  70.2 0.0 collective-permute-done.8.z_below
  70.2 4.3 %collective-permute-start.7 = (f32[544,128]{1,0:T(8,128)S(1)}, f32[544,128]{1,0:T(8,128)S(1)}, u32[]{:S(2)}, u32[]{:S(2)}) collective-permute-start(f32[544,128]{1,0:T(8,128)S(1)} %get-tuple-element.34), channel_id=1, source_target_pairs={{1,0},{2,1},{3,2},{4,3},{5,4},{6,5},{7,6},{9,8},{10,9},{11,10},{12... | collective-permute-start | bytes 835592 | tf_op jit(solution)/shard_map/ppermute | solution.py:745
  74.4 14.4 %collective-permute-done.9.z_above = f32[2,128,512]{2,1,0:T(8,128)S(1)} collective-permute-done((f32[2,128,512]{2,1,0:T(8,128)S(1)}, f32[2,128,512]{2,1,0:T(8,128)S(1)}, u32[]{:S(2)}, u32[]{:S(2)}) %collective-permute-start.9) | collective-permute-done | bytes 524320 | tf_op jit(solution)/shard_map/ppermute | solution.py:745
  88.8 0.8 copy-done.1
  89.6 5.9 %early.1 = (f32[2,4,160,128]{3,2,1,0:T(8,128)}, f32[6,4,160,128]{3,2,1,0:T(8,128)}) custom-call(s32[3,64]{1,0:T(4,128)} %bitcast.8, f32[8,4,144,128]{3,2,1,0:T(8,128)} %get-tuple-element.35.f_own, f32[2,128,512]{2,1,0:T(8,128)} %collective-permute-done.8.z_below, f32[2,128,512]{2,1,0:T(8,128)} %copy-done.1, f32[336,128]{1,0:T(8,128)S(1)} %collective-permute-done.2.below, ...), custom_call_target="tpu_custom_call" | custom-call | flops 20000000 | bytes 10000000 | tf_op jit(solution)/shard_map/early/pallas_call | solution.py:852
  95.5 0.0 all-to-all-done
  95.5 0.9 third.1
  96.4 6.5 %all-gather = f32[16,16,128]{2,1,0:T(8,128)S(1)} all-gather(f32[4,16,128]{2,1,0:T(8,128)S(1)} %third.1), channel_id=2, replica_groups=mesh['box'=4,'gz'=8] {'box'}, dimensions={0}, use_global_device_ids=true | all-gather | bytes 163840 | tf_op jit(solution)/shard_map/all_gather | solution.py:882
  102.9 3.1 %middle.1.e2p = f32[6,2,80,128]{3,2,1,0:T(8,128)S(1)} custom-call(f32[4,4,16,128]{3,2,1,0:T(8,128)S(1)} %bitcast.6, f32[16,48,128]{2,1,0:T(8,128)S(1)} %bitcast.5), custom_call_target="tpu_custom_call" | custom-call | flops 10000000 | bytes 2000000 | tf_op jit(solution)/shard_map/middle/pallas_call | solution.py:884
  106.0 0.0 collective-permute-done.6.late_below
  106.0 0.0 collective-permute-done.7.late_above
  106.0 0.0 collective-permute-done.4.below
  106.0 7.3 %tail.1 = f32[8,128,512]{2,1,0:T(8,128)} custom-call(f32[6,2,80,128]{3,2,1,0:T(8,128)S(1)} %middle.1.e2p, f32[4,2,80,128]{3,2,1,0:T(8,128)S(1)} %get-tuple-element.30.s1, f32[576,128]{1,0:T(8,128)S(1)} %collective-permute-done.4.below, f32[576,128]{1,0:T(8,128)S(1)} %collective-permute-done.5.above, f32[544,128]{1,0:T(8,128)S(1)} %collective-permute-done.6.late_below, ...), custom_call_target="tpu_custom_call" | custom-call | flops 40000000 | bytes 10000000 | tf_op jit(solution)/shard_map/tail/pallas_call | solution.py:896
  (4 shorter events, 0.0 us)
Async XLA Ops:
  1.7 17.0 %collective-permute-start = (f32[8,32,512]{2,1,0:T(8,128)S(1)}, f32[8,32,512]{2,1,0:T(8,128)S(1)}, u32[]{:S(2)}, u32[]{:S(2)}) collective-permute-start(f32[8,32,512]{2,1,0:T(8,128)S(1)} %get-tuple-element.23), channel_id=1, source_target_pairs={{0,8},{8,16},{16,24},{1,9},{9,17},{17,25},{2,10},{10,18},{18,26},{... | collective-permute-start | bytes 1572872 | tf_op jit(solution)/shard_map/ppermute | solution.py:745
  5.5 13.3 %collective-permute-start.1 = (f32[8,32,512]{2,1,0:T(8,128)S(1)}, f32[8,32,512]{2,1,0:T(8,128)S(1)}, u32[]{:S(2)}, u32[]{:S(2)}) collective-permute-start(f32[8,32,512]{2,1,0:T(8,128)S(1)} %get-tuple-element.24), channel_id=1, source_target_pairs={{8,0},{16,8},{24,16},{9,1},{17,9},{25,17},{10,2},{18,10},{26,18},{... | collective-permute-start | bytes 1572872 | tf_op jit(solution)/shard_map/ppermute | solution.py:745
  29.0 32.1 %copy-start = (f32[544,128]{1,0:T(8,128)}, f32[544,128]{1,0:T(8,128)S(1)}, u32[]{:S(2)}) copy-start(f32[544,128]{1,0:T(8,128)S(1)} %get-tuple-element.33) | copy-start | bytes 835588
  29.0 8.4 %collective-permute-start.2 = (f32[336,128]{1,0:T(8,128)S(1)}, f32[336,128]{1,0:T(8,128)S(1)}, u32[]{:S(2)}, u32[]{:S(2)}) collective-permute-start(f32[336,128]{1,0:T(8,128)S(1)} %get-tuple-element.27), channel_id=1, source_target_pairs={{0,1},{1,2},{2,3},{3,4},{4,5},{5,6},{6,7},{8,9},{9,10},{10,11},{11... | collective-permute-start | bytes 516104 | tf_op jit(solution)/shard_map/ppermute | solution.py:745
  32.1 20.4 %collective-permute-start.3 = (f32[336,128]{1,0:T(8,128)S(1)}, f32[336,128]{1,0:T(8,128)S(1)}, u32[]{:S(2)}, u32[]{:S(2)}) collective-permute-start(f32[336,128]{1,0:T(8,128)S(1)} %get-tuple-element.28), channel_id=1, source_target_pairs={{1,0},{2,1},{3,2},{4,3},{5,4},{6,5},{7,6},{9,8},{10,9},{11,10},{12... | collective-permute-start | bytes 516104 | tf_op jit(solution)/shard_map/ppermute | solution.py:745
  35.2 35.0 %collective-permute-start.8 = (f32[2,128,512]{2,1,0:T(8,128)S(1)}, f32[2,128,512]{2,1,0:T(8,128)}, u32[]{:S(2)}, u32[]{:S(2)}) collective-permute-start(f32[2,128,512]{2,1,0:T(8,128)S(1)} %get-tuple-element.36), channel_id=1, source_target_pairs={{0,1},{1,2},{2,3},{3,4},{4,5},{5,6},{6,7},{8,9},{9,10},{10,11},{11... | collective-permute-start | bytes 1572872 | tf_op jit(solution)/shard_map/ppermute | solution.py:745
  53.2 42.2 %all-to-all-start = ((f32[8,96,128]{2,1,0:T(8,128)}), f32[8,96,128]{2,1,0:T(8,128)S(1)}, u32[]{:S(2)}, u32[]{:S(2)}) async-start(f32[8,96,128]{2,1,0:T(8,128)} %total.1), calls=%async_computation | async-start | bytes 786432 | tf_op jit(solution)/shard_map/all_to_all | solution.py:836
  58.0 30.8 %collective-permute-start.9 = (f32[2,128,512]{2,1,0:T(8,128)S(1)}, f32[2,128,512]{2,1,0:T(8,128)S(1)}, u32[]{:S(2)}, u32[]{:S(2)}) collective-permute-start(f32[2,128,512]{2,1,0:T(8,128)S(1)} %get-tuple-element.37), channel_id=1, source_target_pairs={{1,0},{2,1},{3,2},{4,3},{5,4},{6,5},{7,6},{9,8},{10,9},{11,10},{12... | collective-permute-start | bytes 1572872 | tf_op jit(solution)/shard_map/ppermute | solution.py:745
  62.0 44.0 %collective-permute-start.4 = (f32[576,128]{1,0:T(8,128)}, f32[576,128]{1,0:T(8,128)S(1)}, u32[]{:S(2)}, u32[]{:S(2)}) collective-permute-start(f32[576,128]{1,0:T(8,128)} %get-tuple-element.31), channel_id=1, source_target_pairs={{0,1},{1,2},{2,3},{3,4},{4,5},{5,6},{6,7},{8,9},{9,10},{10,11},{11... | collective-permute-start | bytes 884744 | tf_op jit(solution)/shard_map/ppermute | solution.py:745
  64.2 41.8 %collective-permute-start.5 = (f32[576,128]{1,0:T(8,128)}, f32[576,128]{1,0:T(8,128)S(1)}, u32[]{:S(2)}, u32[]{:S(2)}) collective-permute-start(f32[576,128]{1,0:T(8,128)} %get-tuple-element.32), channel_id=1, source_target_pairs={{1,0},{2,1},{3,2},{4,3},{5,4},{6,5},{7,6},{9,8},{10,9},{11,10},{12... | collective-permute-start | bytes 884744 | tf_op jit(solution)/shard_map/ppermute | solution.py:745
  68.2 37.8 %collective-permute-start.6 = (f32[544,128]{1,0:T(8,128)}, f32[544,128]{1,0:T(8,128)S(1)}, u32[]{:S(2)}, u32[]{:S(2)}) collective-permute-start(f32[544,128]{1,0:T(8,128)} %copy-done), channel_id=1, source_target_pairs={{0,1},{1,2},{2,3},{3,4},{4,5},{5,6},{6,7},{8,9},{9,10},{10,11},{11... | collective-permute-start | bytes 835592 | tf_op jit(solution)/shard_map/ppermute | solution.py:745
  70.2 35.8 %collective-permute-start.7 = (f32[544,128]{1,0:T(8,128)S(1)}, f32[544,128]{1,0:T(8,128)S(1)}, u32[]{:S(2)}, u32[]{:S(2)}) collective-permute-start(f32[544,128]{1,0:T(8,128)S(1)} %get-tuple-element.34), channel_id=1, source_target_pairs={{1,0},{2,1},{3,2},{4,3},{5,4},{6,5},{7,6},{9,8},{10,9},{11,10},{12... | collective-permute-start | bytes 835592 | tf_op jit(solution)/shard_map/ppermute | solution.py:745
  88.8 0.8 copy-start.1
